TPU v7x, 32 devices: a whole 2x2x4 slice. The times are simulated.
32 devices in a mesh: dp: 16 (over z, y, core), tensor: 2 (over x).
Axes of the slice: x: 2, y: 2, z: 4, core: 2. Of those that a mesh axis runs over, the one named last changes fastest.
Arguments:
- block_input: bfloat16 [16384, 768], P('dp'), may hold values from -6 to 6
- first_gain: float32 [768], replicated, may hold values from 0.5 to 1.5
- first_shift: float32 [768], replicated, may hold values from -1.2 to 1.2
- qkv_weight: bfloat16 [3, 768, 768], P(None, None, 'tensor'), may hold values from -0.21875 to 0.21875
- qv_bias: float32 [2, 768], P(None, 'tensor'), may hold values from -0.6 to 0.6
- proj_weight: bfloat16 [768, 768], P('tensor'), may hold values from -12 to 12
- proj_bias: float32 [768], replicated, may hold values from -6 to 6
- second_gain: float32 [768], replicated, may hold values from 0.5 to 1.5
- second_shift: float32 [768], replicated, may hold values from -1.2 to 1.2
- fc_weight: bfloat16 [768, 3072], P(None, 'tensor'), may hold values from -0.21875 to 0.21875
- fc_bias: float32 [3072], P('tensor'), may hold values from -3 to 3
- out_weight: bfloat16 [3072, 768], P('tensor'), may hold values from -0.75 to 0.75
- out_bias: float32 [768], replicated, may hold values from -6 to 6
- cotangent: bfloat16 [16384, 768], P('dp'), may hold values from -6 to 6
- lengths: int32 [16], P('dp'), may hold values from 256 to 1024, as said below
Outputs:
- block_output: bfloat16 [16384, 768], P('dp')
- grad_input: float32 [16384, 768], P('dp')
- grad_first_gain: float32 [768], replicated
- grad_first_shift: float32 [768], replicated
- grad_qkv_weight: float32 [3, 768, 768], P(None, 'dp', 'tensor')
- grad_qv_bias: float32 [2, 768], P(None, 'tensor')
- grad_proj_weight: float32 [768, 768], P('tensor', 'dp')
- grad_proj_bias: float32 [768], replicated
- grad_second_gain: float32 [768], replicated
- grad_second_shift: float32 [768], replicated
- grad_fc_weight: float32 [768, 3072], P('dp', 'tensor')
- grad_fc_bias: float32 [3072], P('tensor')
- grad_out_weight: float32 [3072, 768], P('tensor', 'dp')
- grad_out_bias: float32 [768], replicated
Inputs may be any that keep to these rules, and one draw needn't show every extreme that they name: Sequence s has its valid tokens in its first lengths[s] slots of 1024, padding after them; some sequence is full.
All inputs are finite; a program needn't handle non-finite values.
Results may differ from a plain program's by a relative error of at most 0.015.
Values may be sent and summed in bfloat16 or wider, within the bound.
No kernel may reach another device: no remote copies, remote signals or barrier semaphores. Data moves between devices by JAX's collectives and lax.ppermute only.
A program may use at most 192 MiB of HBM per device.

v0:
```python
import functools

import jax
import jax.numpy as jnp
from jax import lax
from jax.experimental import pallas as pl
from jax.experimental.pallas import tpu as pltpu
from jax.sharding import PartitionSpec as P

EPSILON = 1e-05
BRANCH = 48 ** (-0.5)
GELU = 0.7978845608028654
CUBIC = 0.044715
FILL = -1e30
BF = jnp.bfloat16
F32 = jnp.float32
MIB = 1024 * 1024
TILE = 256
HIDDEN = 512
GAIN1, SHIFT1, BIAS_P, GAIN2, SHIFT2, BIAS_O = range(6)
BIAS_QV, BIAS_FC = 8, 9


def dot(left, right):
    return lax.dot_general(left, right, (((1,), (0,)), ((), ())), preferred_element_type=F32)


def dot_nt(left, right):
    return lax.dot_general(left, right, (((1,), (1,)), ((), ())), preferred_element_type=F32)


def norm_parts(values):
    row_mean = jnp.mean(values, -1, keepdims=True)
    centered = values - row_mean
    inverse = lax.rsqrt(jnp.mean(centered * centered, -1, keepdims=True) + EPSILON)
    return centered * inverse, inverse


def norm_back(grad_out, normed, inverse, gain):
    scaled = grad_out * gain
    inner = (
        scaled
        - jnp.mean(scaled, -1, keepdims=True)
        - normed * jnp.mean(scaled * normed, -1, keepdims=True)
    )
    return inverse * inner


def whole(shape):
    return pl.BlockSpec(shape, lambda *_: (0,) * len(shape))


def row_tile(columns):
    return pl.BlockSpec((TILE, columns), lambda i: (i, 0))


def column_tile(rows, size=TILE):
    return pl.BlockSpec((rows, size), lambda i: (0, i))


SMEM = pl.BlockSpec(memory_space=pltpu.SMEM)
HBM = pl.BlockSpec(memory_space=pl.ANY)
KEPT = pl.BlockSpec(memory_space=pltpu.VMEM)


def call(body, name, steps, ins, outs, scratch, flops, limit=12):
    args = []
    for array, spec in ins:
        if spec is KEPT:
            array = pltpu.with_memory_space_constraint(array, pltpu.VMEM)
        elif spec is not SMEM:
            array = pltpu.with_memory_space_constraint(array, pltpu.HBM)
        args.append(array)
    moved = sum(a.size * a.dtype.itemsize for a, spec in ins if spec is not KEPT)
    moved += sum(
        jax.ShapeDtypeStruct(shape, dtype).size * jnp.dtype(dtype).itemsize
        for shape, dtype, spec in outs
        if spec is not KEPT
    )
    return pl.pallas_call(
        body,
        name=name,
        grid=(steps,),
        out_shape=tuple(
            (pltpu.VMEM if spec is KEPT else pltpu.HBM)(shape, dtype) for shape, dtype, spec in outs
        ),
        in_specs=[spec for _, spec in ins],
        out_specs=tuple(spec for _, _, spec in outs),
        scratch_shapes=scratch,
        compiler_params=pltpu.CompilerParams(vmem_limit_bytes=limit * MIB),
        cost_estimate=pl.CostEstimate(flops=flops, bytes_accessed=moved, transcendentals=0),
    )(*args)


def tile_of(step):
    return pl.ds(pl.multiple_of(step * TILE, TILE), TILE)


def fetch_rows(pieces, turn, target, sems):
    copies = []
    for index, piece in enumerate(pieces):
        rows = piece.shape[-2]
        if len(pieces) > 1:
            place = jnp.bitwise_xor(jnp.int32(index), turn)
            where = pl.ds(pl.multiple_of(place * rows, 32), rows)
        else:
            where = slice(None)
        if len(piece.shape) == 2:
            copies.append(pltpu.make_async_copy(piece, target.at[where, :], sems.at[index]))
            continue
        width = piece.shape[2]
        for matrix in range(3):
            columns = slice(matrix * width, (matrix + 1) * width)
            copies.append(
                pltpu.make_async_copy(
                    piece.at[matrix], target.at[where, columns], sems.at[3 * index + matrix]
                )
            )
    return copies


def start_all(copies):
    for copy in copies:
        copy.start()


def wait_all(copies):
    for copy in copies:
        copy.wait()


def qkv_bias(biases, width):
    bias = jnp.concatenate(
        [biases[:, :width], jnp.zeros((1, width), F32), biases[:, width:]], axis=1
    )
    lane = lax.broadcasted_iota(jnp.int32, (1, 3 * width), 1)
    return bias, jnp.where(lane < width, 0.125, 1.0)


def tiles(source, target, sems, axis=0):
    copies = []
    for index in range(source.shape[axis] // TILE):
        part = slice(index * TILE, (index + 1) * TILE)
        view = (part, slice(None)) if axis == 0 else (slice(None), part)
        copies.append(pltpu.make_async_copy(source.at[view], target.at[view], sems.at[index]))
    return copies


def tile_copy(source, target, sems, index):
    rows = tile_of(index)
    return pltpu.make_async_copy(source.at[rows, :], target.at[rows, :], sems.at[index])


def clear(*refs):
    @pl.loop(0, refs[0].shape[0] // TILE)
    def _(index):
        for ref in refs:
            ref[tile_of(index), :] = jnp.zeros((TILE, ref.shape[1]), ref.dtype)


def halves(value_ref, side, block, kept_ref, sent_ref):
    @pl.loop(0, value_ref.shape[0] // (2 * block))
    def _(index):
        rows = pl.ds(pl.multiple_of(index * block, 16), block)
        first = 2 * block * index
        here = pl.ds(pl.multiple_of(first + block * side, 16), block)
        there = pl.ds(pl.multiple_of(first + block * (1 - side), 16), block)
        kept_ref[rows, :] = value_ref[here, :]
        sent_ref[rows, :] = value_ref[there, :]


def grad_top_of(cot, length, start):
    rows, model = cot.shape
    position = lax.broadcasted_iota(jnp.int32, (rows, 128), 0) + start
    valid = jnp.where(position < length, 1.0, 0.0)
    return cot.astype(F32) * jnp.concatenate([valid] * (model // 128), axis=1)


def project_kernel(
    bits_ref,
    x_hbm,
    gain1_ref,
    shift1_ref,
    bias_p_ref,
    gain2_ref,
    shift2_ref,
    bias_o_ref,
    qv_ref,
    fcb_ref,
    qkv_hbm,
    proj_hbm,
    fc_hbm,
    out_hbm,
    length_ref,
    cot_hbm,
    vec_ref,
    qkv_ref,
    gm_ref,
    gmt_ref,
    ob_ref,
    a_out,
    at_out,
    proj_out,
    fc_out,
    out_out,
    x_ref,
    w_ref,
    a_ref,
    at_ref,
    proj_ref,
    fc_ref,
    out_ref,
    cot_ref,
    low_ref,
    x_sems,
    w_sems,
    cot_sems,
    send_sems,
    a_sems,
    at_sems,
):
    x_in = tiles(x_hbm, x_ref, x_sems)
    x_in[0].start()
    w_in = fetch_rows([qkv_hbm], 0, w_ref, w_sems)
    start_all(w_in)
    start_all(x_in[1:])
    model = x_ref.shape[1]
    half, quarter, fourth = proj_hbm.shape[0] // 2, fc_hbm.shape[0] // 4, out_hbm.shape[0] // 4
    sends_in = []
    for index, (source, target, place, rows) in enumerate(
        (
            (proj_hbm, proj_ref.at[:half, :], bits_ref[0], half),
            (fc_hbm, fc_ref, bits_ref[1], quarter),
            (out_hbm, out_ref, bits_ref[4], fourth),
        )
    ):
        where = pl.ds(pl.multiple_of(place * rows, 32), rows)
        sends_in.append(pltpu.make_async_copy(source.at[where, :], target, send_sems.at[index]))
    start_all(sends_in)
    sends_out = [
        pltpu.make_async_copy(source, target, send_sems.at[3 + index])
        for index, (source, target) in enumerate(
            ((proj_ref, proj_out), (fc_ref, fc_out), (out_ref, out_out))
        )
    ]
    cot_in = tiles(cot_hbm, cot_ref, cot_sems)
    start_all(cot_in)
    vec_ref[...] = jnp.zeros(vec_ref.shape, F32)
    for index, ref in enumerate(
        (gain1_ref, shift1_ref, bias_p_ref, gain2_ref, shift2_ref, bias_o_ref)
    ):
        vec_ref[index : index + 1, :] = ref[...].reshape(1, model)
    width = qv_ref.shape[1]
    vec_ref[BIAS_QV : BIAS_QV + 1, :width] = qv_ref[0:1, :]
    vec_ref[BIAS_QV : BIAS_QV + 1, width:] = qv_ref[1:2, :]
    fcb = fcb_ref[...].reshape(1, fcb_ref.shape[0])
    for index in range(2):
        vec_ref[BIAS_FC + index : BIAS_FC + index + 1, :] = fcb[:, index * model : (index + 1) * model]
    value = vec_ref[8 * (BIAS_QV // 8) :, :]
    high = value.astype(BF)
    rest = value - high.astype(F32)
    mid = rest.astype(BF)
    low = (rest - mid.astype(F32)).astype(BF)
    lines = value.shape[0]
    for index, part in enumerate((high, mid, low)):
        proj_ref[half + index * lines : half + (index + 1) * lines, :] = part

    def normalize(index):
        rows = tile_of(index)
        normed, _ = norm_parts(x_ref[rows, :].astype(F32))
        low = normed * vec_ref[GAIN1 : GAIN1 + 1, :] + vec_ref[SHIFT1 : SHIFT1 + 1, :]
        low = low.astype(BF)
        low_ref[...] = low
        a_ref[rows, :] = low
        at_ref[:, rows] = low.T

    def gradient(index):
        rows = tile_of(index)
        top = grad_top_of(cot_ref[rows, :], length_ref[0], index * TILE)
        ob_ref[...] += BRANCH * jnp.sum(top, 0, keepdims=True)
        low = (BRANCH * top).astype(BF)
        gm_ref[rows, :] = low
        gmt_ref[:, rows] = low.T

    def multiply(index):
        qkv_ref[tile_of(index), :] = ((dot(low_ref[...], w_ref[...]) + bias) * scale).astype(BF)

    count = len(x_in)
    bias, scale = qkv_bias(vec_ref[BIAS_QV : BIAS_QV + 1, :], width)
    a_tiles = tiles(a_ref, a_out, a_sems)
    at_tiles = tiles(at_ref, at_out, at_sems, 1)
    ob_ref[...] = jnp.zeros(ob_ref.shape, F32)
    x_in[0].wait()
    normalize(0)
    wait_all(w_in + x_in[1:])

    @pl.loop(0, count - 1)
    def _(index):
        multiply(index)
        normalize(index + 1)

    start_all(a_tiles + at_tiles)
    wait_all(sends_in + cot_in)
    start_all(sends_out)
    multiply(count - 1)

    @pl.loop(0, count)
    def _(index):
        gradient(index)

    wait_all(sends_out + a_tiles + at_tiles)


def project(bits, length, x, cot, vectors, qkv, proj, fc, ow):
    slots, model = x.shape
    width = qkv.shape[2]
    units = fc.shape[1]
    tokens = slots // TILE
    sends = [
        (width // 2 + 32, model),
        (model // 4, units),
        (units // 4, model),
    ]
    shapes = [(slots, model), (model, slots)]
    dma = pltpu.SemaphoreType.DMA
    return call(
        project_kernel,
        "project_own",
        1,
        [(bits, SMEM), (x, HBM)]
        + [(vector, whole(vector.shape)) for vector in vectors]
        + [(weight, HBM) for weight in (qkv, proj, fc, ow)]
        + [(length, SMEM), (cot, HBM)],
        [
            ((16, model), F32, whole((16, model))),
            ((slots, 3 * width), BF, KEPT),
            ((slots, model), BF, KEPT),
            ((model, slots), BF, KEPT),
            ((1, model), F32, whole((1, model))),
        ]
        + [(shape, BF, HBM) for shape in shapes + sends],
        [pltpu.VMEM((slots, model), BF), pltpu.VMEM((model, 3 * width), BF)]
        + [pltpu.VMEM(shape, BF) for shape in shapes + sends]
        + [pltpu.VMEM((slots, model), BF), pltpu.VMEM((TILE, model), BF)]
        + [dma((tokens,)), dma((3,)), dma((tokens,)), dma((6,)), dma((tokens,)), dma((tokens,))],
        6 * slots * model * width,
        20,
    )


def causal_fill():
    keys = lax.broadcasted_iota(jnp.int32, (TILE, TILE), 0)
    queries = lax.broadcasted_iota(jnp.int32, (TILE, TILE), 1)
    return jnp.where(keys <= queries, 0.0, FILL)


def masked_pair(pair_keys, pair_queries, length, keys_ref, queries_ref):
    slots = pair_keys.shape[0]
    lane = lax.broadcasted_iota(jnp.int32, (slots, 128), 1)
    position = lax.broadcasted_iota(jnp.int32, (slots, 128), 0)
    fill = jnp.where(position < length, 0.0, FILL)
    pair_keys = pair_keys.astype(F32)
    pair_queries = pair_queries.astype(F32)
    for half in (0, 1):
        spare = 64 * (1 - half)
        keys_ref[half] = jnp.where(lane == spare, fill, pair_keys).astype(BF)
        queries_ref[half] = jnp.where(
            lane // 64 == half, pair_queries, jnp.where(lane == spare, 1.0, 0.0)
        ).astype(BF)


def pair_lanes(pair, offset=0):
    return pl.ds(pl.multiple_of(offset + pair * 128, 128), 128)


def forward_pairs(length, qkv_ref, ctx_ref, ctxt_ref, lse_ref, scratch, results):
    ka_ref, qa_ref, vt_ref, score_ref, expo_ref = scratch
    width, slots = ctxt_ref.shape
    causal = causal_fill()

    @pl.loop(0, width // 128)
    def _(pair):
        lanes = pair_lanes(pair)
        masked_pair(
            qkv_ref[:, pair_lanes(pair, width)], qkv_ref[:, lanes], length, ka_ref, qa_ref
        )
        vt_ref[...] = qkv_ref[:, pair_lanes(pair, 2 * width)].T
        items = [(block, half) for block in range(slots // TILE) for half in (0, 1)]
        state = {}

        def score(item):
            block, half = items[item]
            extent = (block + 1) * TILE
            columns = slice(block * TILE, extent)
            scores = dot_nt(ka_ref[half, :extent, :], qa_ref[half, columns, :])
            high = None
            for inner in range(block + 1):
                keys = slice(inner * TILE, (inner + 1) * TILE)
                part = scores[keys]
                if inner == block:
                    part = part + causal
                score_ref[item % 2, keys, :] = part
                most = jnp.max(part.reshape(TILE // 8, 8, TILE), 0)
                high = most if high is None else jnp.maximum(high, most)
            state[item] = jnp.max(high, 0, keepdims=True)

        def exponential(item):
            block, half = items[item]
            high = state[item]
            total = None
            for inner in range(block + 1):
                keys = slice(inner * TILE, (inner + 1) * TILE)
                expo = jnp.exp(score_ref[item % 2, keys, :] - high)
                part = jnp.sum(expo.reshape(TILE // 8, 8, TILE), 0)
                total = part if total is None else total + part
                expo_ref[item % 2, keys, :] = expo.astype(BF)
            state[item] = (high, jnp.sum(total, 0, keepdims=True))

        def mix(item):
            block, half = items[item]
            extent = (block + 1) * TILE
            columns = slice(block * TILE, extent)
            high, total = state[item]
            mixed = dot(vt_ref[64 * half : 64 * half + 64, :extent], expo_ref[item % 2, :extent, :])
            row = pl.multiple_of(pair * 128 + half * 64, 64)
            ctxt_ref[pl.ds(row, 64), columns] = mixed * (1.0 / total)
            lse_ref[pl.ds(pair * 2 + half, 1), columns] = high + jnp.log(total)

        count = len(items)
        score(0)
        for item in range(count + 1):
            if item + 1 < count:
                score(item + 1)
            if item >= 1:
                mix(item - 1)
            if item < count:
                exponential(item)
        ctx_ref[:, lanes] = ctxt_ref[lanes, :].T.astype(BF)
        start_all(results(pair))


def forward_own_kernel(
    length_ref, qkv_ref, lse_ref, ctx_out, ctxt_out, qkv_out, ctx_ref, ctxt_ref, *rest
):
    scratch, sems = rest[:5], rest[5]
    saved = pltpu.make_async_copy(qkv_ref, qkv_out, sems.at[2, 0])
    saved.start()

    def results(pair):
        lanes = pair_lanes(pair)
        return [
            pltpu.make_async_copy(ctx_ref.at[:, lanes], ctx_out.at[:, lanes], sems.at[0, pair]),
            pltpu.make_async_copy(ctxt_ref.at[lanes, :], ctxt_out.at[lanes, :], sems.at[1, pair]),
        ]

    forward_pairs(length_ref[0], qkv_ref, ctx_ref, ctxt_ref, lse_ref, scratch, results)
    for pair in range(ctx_ref.shape[1] // 128):
        wait_all(results(pair))
    saved.wait()


def forward_other_kernel(
    bits_ref, length_ref, other_vec_ref, vec_ref, a_hbm, x_hbm, ctx0_hbm, proj0_hbm, *rest
):
    pieces, proj_pieces, rest = rest[:4], rest[4:6], rest[6:]
    lse_ref, c_ref, ct_ref, middle_out, ctxt_out, qkv_out, *rest = rest
    both_ref, ctxt_ref, *rest = rest
    scratch, rest = rest[:5], rest[5:]
    qkv_ref, a_ref, w_ref, x_ref, proj_ref, middle_ref, sum_ref, *rest = rest
    a_sems, w_sems, qkv_sems, sems, late_sems, proj_sems, middle_sems = rest
    slots, width = ctx0_hbm.shape
    own = pl.ds(pl.multiple_of(bits_ref[3] * width, 128), width)
    other = pl.ds(pl.multiple_of((1 - bits_ref[3]) * width, 128), width)
    ctx_ref = both_ref.at[:, other]
    w_in = fetch_rows(pieces, bits_ref[1], w_ref, w_sems)
    start_all(w_in)
    a_in = tiles(a_hbm, a_ref, a_sems)
    start_all(a_in)
    late = [
        pltpu.make_async_copy(source, target, late_sems.at[index])
        for index, (source, target) in enumerate(
            ((x_hbm, x_ref), (ctx0_hbm, both_ref.at[:, own]), (proj0_hbm, proj_ref.at[own, :]))
        )
    ]
    halves_in = [piece.at[: width // 2, :] for piece in proj_pieces]
    late += fetch_rows(halves_in, bits_ref[0], proj_ref.at[other, :], proj_sems)
    start_all(late)
    bias, scale = qkv_bias(other_vec_ref[0:1, :], width)
    qkv_tiles = tiles(qkv_ref, qkv_out, qkv_sems)
    wait_all(w_in + a_in)

    @pl.loop(0, len(a_in))
    def _(index):
        rows = tile_of(index)
        product = dot(a_ref[rows, :], w_ref[...])
        qkv_ref[rows, :] = ((product + bias) * scale).astype(BF)

    start_all(qkv_tiles)

    def results(pair):
        lanes = pair_lanes(pair)
        return [
            pltpu.make_async_copy(ctxt_ref.at[lanes, :], ctxt_out.at[lanes, :], sems.at[pair])
        ]

    forward_pairs(length_ref[0], qkv_ref, ctx_ref, ctxt_ref, lse_ref, scratch, results)
    wait_all(late)
    count = slots // TILE

    def branch(index):
        return dot(both_ref[tile_of(index), :], proj_ref[...])

    def normalize(index):
        rows = tile_of(index)
        total = sum_ref[...] + vec_ref[BIAS_P : BIAS_P + 1, :]
        middle = x_ref[rows, :].astype(F32) + BRANCH * total
        middle_ref[rows, :] = middle
        normed, _ = norm_parts(middle)
        low = (normed * vec_ref[GAIN2 : GAIN2 + 1, :] + vec_ref[SHIFT2 : SHIFT2 + 1, :]).astype(BF)
        c_ref[rows, :] = low
        ct_ref[:, rows] = low.T

    sum_ref[...] = branch(0)

    @pl.loop(0, count - 1)
    def _(index):
        normalize(index)
        sum_ref[...] = branch(index + 1)
        tile_copy(middle_ref, middle_out, middle_sems, index).start()

    normalize(count - 1)
    middle_tiles = tiles(middle_ref, middle_out, middle_sems)
    middle_tiles[-1].start()
    for pair in range(width // 128):
        wait_all(results(pair))
    wait_all(qkv_tiles + middle_tiles)


def forward_scratch(slots, width):
    return [
        pltpu.VMEM((slots, width), BF),
        pltpu.VMEM((width, slots), F32),
        pltpu.VMEM((2, slots, 128), BF),
        pltpu.VMEM((2, slots, 128), BF),
        pltpu.VMEM((128, slots), BF),
        pltpu.VMEM((2, slots, TILE), F32),
        pltpu.VMEM((2, slots, TILE), BF),
    ]


def attention_forward_own(length, qkv):
    slots = qkv.shape[0]
    width = qkv.shape[1] // 3
    heads = width // 64
    return call(
        forward_own_kernel,
        "attention_forward_own",
        1,
        [(length, SMEM), (qkv, KEPT)],
        [
            ((heads, slots), F32, whole((heads, slots))),
            ((slots, width), BF, HBM),
            ((width, slots), F32, HBM),
            ((slots, 3 * width), BF, HBM),
        ],
        [*forward_scratch(slots, width), pltpu.SemaphoreType.DMA((3, width // 128))],
        6 * slots * slots * width,
    )


def attention_forward_other(bits, length, other_vec, vec, a_low, x, ctx, proj, pieces, proj_pieces):
    slots, model = x.shape
    width = ctx.shape[1]
    heads = width // 64
    tokens = slots // TILE
    dma = pltpu.SemaphoreType.DMA
    ins = [(bits, SMEM), (length, SMEM)]
    ins += [(value, whole(value.shape)) for value in (other_vec, vec)]
    ins += [(value, HBM) for value in (a_low, x, ctx, proj, *pieces, *proj_pieces)]
    return call(
        forward_other_kernel,
        "attention_forward_other",
        1,
        ins,
        [
            ((heads, slots), F32, whole((heads, slots))),
            ((slots, model), BF, KEPT),
            ((model, slots), BF, KEPT),
            ((slots, model), F32, HBM),
            ((width, slots), F32, HBM),
            ((slots, 3 * width), BF, HBM),
        ],
        [
            pltpu.VMEM((slots, 2 * width), BF),
            *forward_scratch(slots, width)[1:],
            pltpu.VMEM((slots, 3 * width), BF),
            pltpu.VMEM((slots, model), BF),
            pltpu.VMEM((model, 3 * width), BF),
            pltpu.VMEM((slots, model), BF),
            pltpu.VMEM((2 * width, model), BF),
            pltpu.VMEM((slots, model), F32),
            pltpu.VMEM((TILE, model), F32),
            dma((tokens,)),
            dma((12,)),
            dma((tokens,)),
            dma((width // 128,)),
            dma((3,)),
            dma((2,)),
            dma((tokens,)),
        ],
        6 * slots * slots * width + 10 * slots * model * width,
        28,
    )


def mlp_step(c_ref, g_ref, fc, ow, bias):
    hidden = dot(c_ref[...], fc) + bias
    square = hidden * hidden
    tanh = jnp.tanh(hidden * (GELU + GELU * CUBIC * square))
    share = 0.5 + 0.5 * tanh
    value = hidden * share
    slope = share + value * (1.0 - share) * (2.0 * GELU + 6.0 * GELU * CUBIC * square)
    return value.astype(BF), (dot_nt(g_ref[...], ow) * slope).astype(BF)


def unit_bias(vec_ref, base, bias_ref):
    model = vec_ref.shape[1]
    for row in range(bias_ref.shape[1] // model):
        columns = slice(row * model, (row + 1) * model)
        bias_ref[:, columns] = vec_ref[base + row : base + row + 1, :]


def mlp_own_kernel(
    steps,
    block,
    bits_ref,
    c_ref,
    g_ref,
    ct_ref,
    gt_ref,
    vec_ref,
    fc_ref,
    ow_ref,
    gc_out,
    act_ref,
    fc_kept_ref,
    out_kept_ref,
    fc_sent_ref,
    out_sent_ref,
    db_ref,
    gc_ref,
    gc_low_ref,
    bias_ref,
    gh_ref,
    dw_ref,
    sem,
):
    step = pl.program_id(0)

    @pl.when(step == 0)
    def _():
        unit_bias(vec_ref, BIAS_FC, bias_ref)
        clear(gc_ref)

    lanes = pl.ds(pl.multiple_of(step * HIDDEN, HIDDEN), HIDDEN)
    act, gh = mlp_step(c_ref, g_ref, fc_ref[...], ow_ref[...], bias_ref[:, lanes])
    act_ref[...] = act
    gh_ref[...] = gh
    db_ref[...] = jnp.sum(gh.astype(F32), 0, keepdims=True)
    gc_ref[...] += dot_nt(gh, fc_ref[...])
    results = [pltpu.make_async_copy(gc_low_ref, gc_out, sem)]

    @pl.when(step == steps - 1)
    def _():
        gc_low_ref[...] = gc_ref[...].astype(BF)
        start_all(results)

    dw_ref[0] = dot(ct_ref[...], gh_ref[...]).astype(BF)
    halves(dw_ref.at[0], bits_ref[2], block, fc_kept_ref, fc_sent_ref.at[:, lanes])
    dw_ref[1] = dot(gt_ref[...], act_ref[...]).astype(BF)
    halves(dw_ref.at[1], bits_ref[2], block, out_kept_ref, out_sent_ref.at[:, lanes])

    @pl.when(step == steps - 1)
    def _():
        wait_all(results)


def feed_forward_own(bits, block, c_low, grad_mlp, c_turned, grad_turned, vec, fc, ow):
    slots, model = c_low.shape
    units = fc.shape[1]
    steps = units // HIDDEN
    half = column_tile(model // 2, HIDDEN)
    return call(
        functools.partial(mlp_own_kernel, steps, block),
        "feed_forward_own",
        steps,
        [(bits, SMEM)]
        + [(value, KEPT) for value in (c_low, grad_mlp, c_turned, grad_turned)]
        + [
            (vec, whole(vec.shape)),
            (fc, column_tile(model, HIDDEN)),
            (ow, pl.BlockSpec((HIDDEN, model), lambda i: (i, 0))),
        ],
        [((slots, model), BF, HBM), ((slots, units), BF, column_tile(slots, HIDDEN))]
        + [((model // 2, units), BF, half)] * 2
        + [((model // 2, units), BF, KEPT)] * 2
        + [((1, units), F32, column_tile(1, HIDDEN))],
        [
            pltpu.VMEM((slots, model), F32),
            pltpu.VMEM((slots, model), BF),
            pltpu.VMEM((1, units), F32),
            pltpu.VMEM((slots, HIDDEN), BF),
            pltpu.VMEM((2, model, HIDDEN), BF),
            pltpu.SemaphoreType.DMA,
        ],
        10 * slots * model * units,
        32,
    )


def mlp_other_kernel(
    steps,
    bits_ref,
    length_ref,
    c_ref,
    g_ref,
    other_vec_ref,
    vec_ref,
    gc0_hbm,
    middle_hbm,
    cot_hbm,
    proj0_hbm,
    fc_kept_hbm,
    out_kept_hbm,
    *rest,
):
    fc_pieces, out_pieces, proj_pieces, rest = rest[:4], rest[4:8], rest[8:10], rest[10:]
    do0_ref, fc_kept_ref, out_kept_ref, sums_ref, act_ref, gmid_out, ga_out, do1_out, *rest = rest
    gc_ref, bias_ref, fc_ref, ow_ref, *rest = rest
    late_refs, (gmid_ref, ga_ref, low_ref, do1_ref, proj1_ref, *rest) = rest[:4], rest[4:]
    sems, late_sems, proj_sems, out_sems = rest
    step = pl.program_id(0)
    slots, model = c_ref.shape
    copies = fetch_rows(fc_pieces, bits_ref[1], fc_ref, sems.at[0])
    copies += fetch_rows(out_pieces, bits_ref[4], ow_ref, sems.at[1])
    late = [
        pltpu.make_async_copy(source, target, late_sems.at[index])
        for index, (source, target) in enumerate(
            zip(
                (gc0_hbm, middle_hbm, cot_hbm, proj0_hbm, fc_kept_hbm, out_kept_hbm),
                (*late_refs, fc_kept_ref, out_kept_ref),
            )
        )
    ]
    half = proj1_ref.shape[0] // 2
    halves_in = [piece.at[:half, :] for piece in proj_pieces]
    late += fetch_rows(halves_in, bits_ref[0], proj1_ref, proj_sems)

    @pl.when(step == 0)
    def _():
        start_all(copies)
        unit_bias(other_vec_ref, 1, bias_ref)
        clear(gc_ref)
        wait_all(copies)
        start_all(late)

    lanes = pl.ds(pl.multiple_of(step * HIDDEN, HIDDEN), HIDDEN)
    act, gh = mlp_step(c_ref, g_ref, fc_ref[:, lanes], ow_ref[lanes, :], bias_ref[:, lanes])
    act_ref[...] = act
    gc_ref[...] += dot_nt(gh, fc_ref[:, lanes])

    @pl.when(step == steps - 1)
    def _():
        wait_all(late)
        gc0_ref, middle_ref, cot_ref, proj0_ref = late_refs
        pairs = ((gmid_ref, gmid_out), (ga_ref, ga_out), (do1_ref, do1_out))
        outs = [(*pair, out_sems.at[index]) for index, pair in enumerate(pairs)]
        count = slots // TILE
        sums_ref[...] = jnp.zeros(sums_ref.shape, F32)

        def elementwise(index):
            rows = tile_of(index)
            grad_c = gc_ref[rows, :].astype(BF).astype(F32) + gc0_ref[rows, :].astype(F32)
            normed, inverse = norm_parts(middle_ref[rows, :])
            top = grad_top_of(cot_ref[rows, :], length_ref[0], index * TILE)
            grad_middle = top + norm_back(grad_c, normed, inverse, vec_ref[GAIN2 : GAIN2 + 1, :])
            sums_ref[0:1, :] += jnp.sum(grad_c * normed, 0, keepdims=True)
            sums_ref[1:2, :] += jnp.sum(grad_c, 0, keepdims=True)
            sums_ref[2:3, :] += BRANCH * jnp.sum(grad_middle, 0, keepdims=True)
            gmid_ref[rows, :] = grad_middle
            low = (BRANCH * grad_middle).astype(BF)
            ga_ref[rows, :] = low
            low_ref[...] = low

        def project_back(index):
            rows = tile_of(index)
            do0_ref[rows, :] = dot_nt(low_ref[...], proj0_ref[...]).astype(BF)
            do1_ref[rows, :] = dot_nt(low_ref[...], proj1_ref[...]).astype(BF)

        elementwise(0)

        @pl.loop(0, count - 1)
        def _(index):
            project_back(index)
            elementwise(index + 1)
            for group in outs:
                tile_copy(*group, index).start()

        project_back(count - 1)
        for group in outs:
            tile_copy(*group, count - 1).start()
        for group in outs:
            wait_all(tiles(*group))


def feed_forward_other(
    bits, length, c_low, grad_mlp, other_vec, vec, grad_c, middle, cot, proj, kept, fc, ow, proj_pieces
):
    slots, model = c_low.shape
    width = proj.shape[0]
    units = fc[0].shape[1]
    steps = units // HIDDEN
    tokens = slots // TILE
    dma = pltpu.SemaphoreType.DMA
    return call(
        functools.partial(mlp_other_kernel, steps),
        "feed_forward_other",
        steps,
        [(bits, SMEM), (length, SMEM), (c_low, KEPT), (grad_mlp, KEPT)]
        + [(value, whole(value.shape)) for value in (other_vec, vec)]
        + [(value, HBM) for value in (grad_c, middle, cot, proj, *kept, *fc, *ow, *proj_pieces)],
        [
            ((slots, width), BF, KEPT),
            *[(value.shape, BF, KEPT) for value in kept],
            ((3, model), F32, whole((3, model))),
            ((slots, units), BF, column_tile(slots, HIDDEN)),
            ((slots, model), F32, HBM),
            ((slots, model), BF, HBM),
            ((slots, width), BF, HBM),
        ],
        [
            pltpu.VMEM((slots, model), F32),
            pltpu.VMEM((1, units), F32),
            pltpu.VMEM((model, units), BF),
            pltpu.VMEM((units, model), BF),
            pltpu.VMEM((slots, model), BF),
            pltpu.VMEM((slots, model), F32),
            pltpu.VMEM((slots, model), BF),
            pltpu.VMEM((width, model), BF),
            pltpu.VMEM((slots, model), F32),
            pltpu.VMEM((slots, model), BF),
            pltpu.VMEM((TILE, model), BF),
            pltpu.VMEM((slots, width), BF),
            pltpu.VMEM((width, model), BF),
            dma((2, 4)),
            dma((6,)),
            dma((2,)),
            dma((3, tokens)),
        ],
        6 * slots * model * units + 4 * slots * model * width,
        42,
    )


def output_kernel(bits_ref, vec_ref, act0_hbm, act1_hbm, middle_hbm, ow_hbm, *rest):
    pieces, (y_out, act_ref, ow_ref, middle_ref, y_ref, act_sems, sems, m_sem, y_sems) = (
        rest[:4],
        rest[4:],
    )
    slots, units = act0_hbm.shape
    own = pl.ds(pl.multiple_of(bits_ref[3] * units, 128), units)
    other = pl.ds(pl.multiple_of((1 - bits_ref[3]) * units, 128), units)
    copies = fetch_rows([ow_hbm], 0, ow_ref.at[own, :], sems.at[0])
    copies += fetch_rows(pieces, bits_ref[4], ow_ref.at[other, :], sems.at[1])
    acts = []
    for index in range(slots // TILE):
        rows = slice(index * TILE, (index + 1) * TILE)
        for group, (source, lanes) in enumerate(((act0_hbm, own), (act1_hbm, other))):
            acts.append(
                pltpu.make_async_copy(
                    source.at[rows, :], act_ref.at[rows, lanes], act_sems.at[group, index]
                )
            )
    middle_in = tiles(middle_hbm, middle_ref, m_sem)
    start_all(acts[:2] + copies)
    for index, copy in enumerate(middle_in):
        copy.start()
        start_all(acts[2 * index + 2 : 2 * index + 4])
    wait_all(copies)

    @pl.loop(0, slots // TILE)
    def _(index):
        rows = tile_of(index)
        for group, (source, lanes) in enumerate(((act0_hbm, own), (act1_hbm, other))):
            pltpu.make_async_copy(
                source.at[rows, :], act_ref.at[rows, lanes], act_sems.at[group, index]
            ).wait()
        tile_copy(middle_hbm, middle_ref, m_sem, index).wait()
        mlp = dot(act_ref[rows, :], ow_ref[...]) + vec_ref[BIAS_O : BIAS_O + 1, :]
        y_ref[rows, :] = (middle_ref[rows, :] + BRANCH * mlp).astype(BF)
        tile_copy(y_ref, y_out, y_sems, index).start()

    wait_all(tiles(y_ref, y_out, y_sems))


def block_result(bits, vec, act0, act1, middle, ow, pieces):
    slots, model = middle.shape
    units = act0.shape[1]
    tokens = slots // TILE
    dma = pltpu.SemaphoreType.DMA
    return call(
        output_kernel,
        "output",
        1,
        [(bits, SMEM), (vec, whole(vec.shape))]
        + [(value, HBM) for value in (act0, act1, middle, ow, *pieces)],
        [((slots, model), BF, HBM)],
        [
            pltpu.VMEM((slots, 2 * units), BF),
            pltpu.VMEM((2 * units, model), BF),
            pltpu.VMEM((slots, model), F32),
            pltpu.VMEM((slots, model), BF),
            dma((2, tokens)),
            dma((2, 4)),
            dma((tokens,)),
            dma((tokens,)),
        ],
        4 * slots * model * units,
        24,
    )[0]


def backward_pairs(length, qkv_ref, do_ref, ctxt_ref, lse_ref, d_ref, scratch, sources):
    (
        ka_ref,
        qa_ref,
        do_mask_ref,
        kt_ref,
        qt_ref,
        dot_ref,
        delta_ref,
        dqt_ref,
        dkt_ref,
        dvt_ref,
        score_ref,
        grad_ref,
        prob_ref,
        slope_ref,
    ) = scratch
    slots, width = do_ref.shape
    causal = causal_fill()
    blocks = slots // TILE

    @pl.loop(0, width // 128)
    def _(pair):
        lanes = pair_lanes(pair)
        wait_all(sources(pair))
        keys_low = qkv_ref[:, pair_lanes(pair, width)]
        queries = qkv_ref[:, lanes]
        masked_pair(keys_low, queries, length, ka_ref, qa_ref)
        grads = do_ref[:, lanes]
        lane = lax.broadcasted_iota(jnp.int32, (slots, 128), 1)
        for half in (0, 1):
            do_mask_ref[half] = jnp.where(lane // 64 == half, grads.astype(F32), 0.0).astype(BF)
        kt_ref[...] = keys_low.T
        qt_ref[...] = queries.T
        turned = grads.T
        dot_ref[...] = turned
        product = turned.astype(F32) * ctxt_ref[lanes, :]
        for half in (0, 1):
            delta_ref[half : half + 1, :] = jnp.sum(
                product[64 * half : 64 * half + 64], 0, keepdims=True
            )
        items = [(block, half) for block in reversed(range(blocks)) for half in (0, 1)]

        def score(item):
            block, half = items[item]
            extent = (block + 1) * TILE
            columns = slice(block * TILE, extent)
            score_ref[item % 2, :extent, :] = dot_nt(
                ka_ref[half, :extent, :], qa_ref[half, columns, :]
            )
            grad_ref[item % 2, :extent, :] = dot_nt(
                qkv_ref[:extent, pair_lanes(pair, 2 * width)], do_mask_ref[half, columns, :]
            )

        def softmax(item):
            block, half = items[item]
            columns = slice(block * TILE, (block + 1) * TILE)
            lse = lse_ref[pl.ds(pair * 2 + half, 1), columns]
            delta = delta_ref[half : half + 1, columns]
            for inner in range(block + 1):
                keys = slice(inner * TILE, (inner + 1) * TILE)
                scores = score_ref[item % 2, keys, :]
                if inner == block:
                    scores = scores + causal
                prob = jnp.exp(scores - lse)
                slope_ref[item % 2, keys, :] = (
                    prob * (grad_ref[item % 2, keys, :] - delta)
                ).astype(BF)
                prob_ref[item % 2, keys, :] = prob.astype(BF)

        def gradients(item):
            block, half = items[item]
            extent = (block + 1) * TILE
            columns = slice(block * TILE, extent)
            rows = slice(64 * half, 64 * half + 64)
            dv_part = dot_nt(dot_ref[rows, columns], prob_ref[item % 2, :extent, :])
            dk_part = dot_nt(qt_ref[rows, columns], slope_ref[item % 2, :extent, :])
            if block == blocks - 1:
                dvt_ref[rows, :extent] = dv_part
                dkt_ref[rows, :extent] = dk_part
            else:
                dvt_ref[rows, :extent] += dv_part
                dkt_ref[rows, :extent] += dk_part
            dqt_ref[rows, columns] = dot(kt_ref[rows, :extent], slope_ref[item % 2, :extent, :])

        count_items = len(items)
        score(0)
        for item in range(count_items + 1):
            if item + 1 < count_items:
                score(item + 1)
            if item >= 1:
                gradients(item - 1)
            if item < count_items:
                softmax(item)
        d_ref[:, lanes] = (dqt_ref[...] * 0.125).astype(BF).T
        d_ref[:, pair_lanes(pair, width)] = dkt_ref[...].astype(BF).T
        d_ref[:, pair_lanes(pair, 2 * width)] = dvt_ref[...].astype(BF).T


def pair_sources(pair, width, qkv, ctxt, do, sems):
    lanes = pair_lanes(pair)
    moves = []
    for matrix in range(3):
        columns = pair_lanes(pair, matrix * width)
        moves.append((qkv[0].at[:, columns], qkv[1].at[:, columns]))
    moves.append((ctxt[0].at[lanes, :], ctxt[1].at[lanes, :]))
    if do is not None:
        moves.append((do[0].at[:, lanes], do[1].at[:, lanes]))
    return [
        pltpu.make_async_copy(source, target, sems.at[index, pair])
        for index, (source, target) in enumerate(moves)
    ]


def backward_other_kernel(
    length_ref, lse_ref, qkv_hbm, ctxt_hbm, do_hbm, d_ref, qkv_ref, ctxt_ref, do_ref, *rest
):
    scratch, sems = rest[:14], rest[14]
    width = do_ref.shape[1]
    sources = lambda pair: pair_sources(
        pair, width, (qkv_hbm, qkv_ref), (ctxt_hbm, ctxt_ref), (do_hbm, do_ref), sems
    )
    for pair in range(width // 128):
        start_all(sources(pair))
    backward_pairs(length_ref[0], qkv_ref, do_ref, ctxt_ref, lse_ref, d_ref, scratch, sources)


def lane_sums(value):
    total = value[:, :128]
    for start in range(128, value.shape[1], 128):
        total = total + value[:, start : start + 128]
    return jnp.sum(total.T, 0, keepdims=True)


def backward_own_kernel(
    block,
    bits_ref,
    length_ref,
    lse_ref,
    vec_ref,
    ob_ref,
    sums_ref,
    db_ref,
    do_ref,
    qkv_hbm,
    ctxt_hbm,
    at_hbm,
    gat_hbm,
    w_hbm,
    lead_ref,
    vectors_ref,
    d_out,
    first_kept_out,
    first_sent_out,
    second_kept_out,
    second_sent_out,
    qkv_ref,
    ctxt_ref,
    *rest,
):
    scratch, rest = rest[:14], rest[14:]
    d_ref, at_ref, gat_ref, w_ref, dw_ref, half_ref, total_ref, sems, w_sems, late_sems, out_sems = rest
    width = do_ref.shape[1]
    model = at_ref.shape[0]
    sources = lambda pair: pair_sources(
        pair, width, (qkv_hbm, qkv_ref), (ctxt_hbm, ctxt_ref), None, sems
    )
    for pair in range(width // 128):
        start_all(sources(pair))
    late = fetch_rows([w_hbm], 0, w_ref, w_sems)
    late += [
        pltpu.make_async_copy(at_hbm, at_ref, late_sems.at[0]),
        pltpu.make_async_copy(gat_hbm, gat_ref, late_sems.at[1]),
    ]
    start_all(late)
    backward_pairs(length_ref[0], qkv_ref, do_ref, ctxt_ref, lse_ref, d_ref, scratch, sources)
    results = [pltpu.make_async_copy(d_ref, d_out, out_sems.at[4])]
    results[0].start()
    lead_ref[...] = jnp.zeros(lead_ref.shape, F32)
    wait_all(late)
    side = bits_ref[2]
    outs = (first_kept_out, first_sent_out, second_kept_out, second_sent_out)

    def give(index):
        halves(dw_ref.at[index], side, block, half_ref.at[2 * index], half_ref.at[2 * index + 1])
        for part in (2 * index, 2 * index + 1):
            results.append(pltpu.make_async_copy(half_ref.at[part], outs[part], out_sems.at[part]))
            results[-1].start()

    low = ctxt_ref[...].astype(BF)
    dw_ref[1, :, width:] = dot(low, gat_ref[...]).T.astype(BF)
    total_ref[...] = jnp.zeros(total_ref.shape, F32)

    @pl.loop(0, d_ref.shape[0] // TILE)
    def _(index):
        total_ref[...] += jnp.sum(d_ref[tile_of(index), :].astype(F32), 0, keepdims=True)

    sums = total_ref[...]

    @pl.loop(0, model // TILE)
    def _(index):
        rows = tile_of(index)
        part = dot(at_ref[rows, :], d_ref[...])
        dw_ref[0, rows, :] = part[:, :model].astype(BF)
        dw_ref[1, rows, :width] = part[:, model:].astype(BF)
        weight = w_ref[rows, :].astype(F32)
        lead_ref[0:1, rows] = lane_sums(part * weight)
        lead_ref[1:2, rows] = lane_sums(weight * sums)

    give(0)
    give(1)
    scaled, shift = lead_ref[0:1, :], lead_ref[1:2, :]
    gain1, shift1 = vec_ref[GAIN1 : GAIN1 + 1, :], vec_ref[SHIFT1 : SHIFT1 + 1, :]
    vectors_ref[...] = jnp.zeros(vectors_ref.shape, F32)
    lead_ref[0:1, :] = (scaled - shift1 * shift) / gain1
    vectors_ref[2:3, :] = ob_ref[...]
    vectors_ref[3:6, :] = sums_ref[...]
    for index in range(2):
        vectors_ref[6 + index : 7 + index, :] = db_ref[:, index * model : (index + 1) * model]
    vectors_ref[8:9, :width] = sums[:, :width]
    vectors_ref[8:9, width:] = sums[:, 2 * width :]
    wait_all(results)


def backward_scratch(slots):
    return [
        pltpu.VMEM((2, slots, 128), BF),
        pltpu.VMEM((2, slots, 128), BF),
        pltpu.VMEM((2, slots, 128), BF),
        pltpu.VMEM((128, slots), BF),
        pltpu.VMEM((128, slots), BF),
        pltpu.VMEM((128, slots), BF),
        pltpu.VMEM((2, slots), F32),
        pltpu.VMEM((128, slots), F32),
        pltpu.VMEM((128, slots), F32),
        pltpu.VMEM((128, slots), F32),
        pltpu.VMEM((2, slots, TILE), F32),
        pltpu.VMEM((2, slots, TILE), F32),
        pltpu.VMEM((2, slots, TILE), BF),
        pltpu.VMEM((2, slots, TILE), BF),
    ]


def attention_backward_other(length, lse, qkv, ctxt, do):
    slots, width = do.shape
    ins = [(length, SMEM), (lse, whole(lse.shape)), (qkv, HBM), (ctxt, HBM), (do, HBM)]
    return call(
        backward_other_kernel,
        "attention_backward_other",
        1,
        ins,
        [((slots, 3 * width), BF, KEPT)],
        [
            pltpu.VMEM((slots, 3 * width), BF),
            pltpu.VMEM((width, slots), F32),
            pltpu.VMEM((slots, width), BF),
            *backward_scratch(slots),
            pltpu.SemaphoreType.DMA((5, width // 128)),
        ],
        9 * slots * slots * width,
        18,
    )[0]


def attention_backward_own(bits, length, block, lse, vec, sums, do, qkv, ctxt, at, gat, weight):
    slots, width = do.shape
    model = at.shape[0]
    dma = pltpu.SemaphoreType.DMA
    ins = [(bits, SMEM), (length, SMEM)]
    ins += [(value, whole(value.shape)) for value in (lse, vec, *sums)]
    ins += [(do, KEPT)] + [(value, HBM) for value in (qkv, ctxt, at, gat, weight)]
    outs = [((rows, model), F32, KEPT) for rows in (8, 16)] + [((slots, 3 * width), BF, HBM)]
    outs += [((model // 2, model), BF, HBM)] * 4
    return call(
        functools.partial(backward_own_kernel, block),
        "attention_backward_own",
        1,
        ins,
        outs,
        [
            pltpu.VMEM((slots, 3 * width), BF),
            pltpu.VMEM((width, slots), F32),
            *backward_scratch(slots),
            pltpu.VMEM((slots, 3 * width), BF),
            pltpu.VMEM((model, slots), BF),
            pltpu.VMEM((slots, model), BF),
            pltpu.VMEM((model, 3 * width), BF),
            pltpu.VMEM((2, model, model), BF),
            pltpu.VMEM((4, model // 2, model), BF),
            pltpu.VMEM((1, 3 * width), F32),
            dma((4, width // 128)),
            dma((3,)),
            dma((2,)),
            dma((5,)),
        ],
        9 * slots * slots * width + 8 * slots * model * width,
        32,
    )


def final_kernel(bits_ref, vec_ref, d1_ref, d0_hbm, x_hbm, gmid_hbm, w_hbm, *rest):
    pieces, (gin_out, d_ref, x_ref, gmid_ref, w_ref, gin_ref, product_ref, *rest) = (
        rest[:4],
        rest[4:],
    )
    w_sems, d_sems, x_sems, gmid_sems, gin_sems = rest
    total = d1_ref.shape[1]
    own = pl.ds(pl.multiple_of(bits_ref[3] * total, 128), total)
    other = pl.ds(pl.multiple_of((1 - bits_ref[3]) * total, 128), total)
    copies = fetch_rows([w_hbm], 0, w_ref.at[:, own], w_sems.at[0])
    copies += fetch_rows(pieces, bits_ref[1], w_ref.at[:, other], w_sems.at[1])
    d_in = tiles(d0_hbm, d_ref.at[:, own], d_sems)
    x_in = tiles(x_hbm, x_ref, x_sems)
    gmid_in = tiles(gmid_hbm, gmid_ref, gmid_sems)
    gin_tiles = tiles(gin_ref, gin_out, gin_sems)
    d_in[0].start()
    start_all(copies)
    start_all(d_in[1:] + x_in + gmid_in)
    count = len(d_in)

    @pl.loop(0, count)
    def _(index):
        d_ref[tile_of(index), other] = d1_ref[tile_of(index), :]

    def product(index):
        return dot_nt(d_ref[tile_of(index), :], w_ref[...])

    def norm(index):
        rows = tile_of(index)
        normed, inverse = norm_parts(x_ref[rows, :].astype(F32))
        back = norm_back(product_ref[...], normed, inverse, vec_ref[GAIN1 : GAIN1 + 1, :])
        gin_ref[rows, :] = gmid_ref[rows, :] + back

    wait_all(copies + d_in)
    product_ref[...] = product(0)
    wait_all(x_in + gmid_in)

    @pl.loop(0, count - 1)
    def _(index):
        norm(index)
        product_ref[...] = product(index + 1)
        tile_copy(gin_ref, gin_out, gin_sems, index).start()

    norm(count - 1)
    gin_tiles[-1].start()
    wait_all(gin_tiles)


def gradient_of_input(bits, vec, d1, d0, x, gmid, weight, pieces):
    slots, model = x.shape
    total = d1.shape[1]
    tokens = slots // TILE
    dma = pltpu.SemaphoreType.DMA
    return call(
        final_kernel,
        "final",
        1,
        [(bits, SMEM), (vec, whole(vec.shape)), (d1, KEPT)]
        + [(value, HBM) for value in (d0, x, gmid, weight, *pieces)],
        [((slots, model), F32, HBM)],
        [
            pltpu.VMEM((slots, 2 * total), BF),
            pltpu.VMEM((slots, model), BF),
            pltpu.VMEM((slots, model), F32),
            pltpu.VMEM((model, 2 * total), BF),
            pltpu.VMEM((slots, model), F32),
            pltpu.VMEM((TILE, model), F32),
            dma((2, 12)),
            dma((tokens,)),
            dma((tokens,)),
            dma((tokens,)),
            dma((tokens,)),
        ],
        4 * slots * model * total,
        28,
    )[0]


def across(value):
    return lax.ppermute(value, "tensor", [(0, 1), (1, 0)])


def swap(value, bit):
    count = lax.axis_size("dp")
    return lax.ppermute(value, "dp", [(i, i ^ bit) for i in range(count)])


def tie(*values):
    return lax.optimization_barrier(values)


def pick(value, index, axis):
    return lax.dynamic_index_in_dim(value, index, axis, keepdims=False)


def split_rows(value, count):
    shape = value.shape
    return value.reshape(*shape[:-2], count, shape[-2] // count, shape[-1])


class Reduction:
    def __init__(self, kept, first_bit, order):
        self.order = order
        self.bits = [bit for bit in reversed(range(len(order) + 1)) if bit != first_bit]
        rows = kept.shape[0] >> len(self.bits)
        self.kept = kept.reshape(*[2] * len(self.bits), rows, kept.shape[1])

    def advance(self, got):
        got = got.reshape(self.kept.shape)
        self.bit = self.order.pop(0)
        axis = self.bits.index(self.bit)
        self.bits.remove(self.bit)
        side = (lax.axis_index("dp") >> self.bit) & 1

        def part(index):
            total = pick(self.kept, index, axis).astype(F32) + pick(got, index, axis).astype(F32)
            return total.astype(BF)

        sent = part(1 - side)
        self.kept = part(side)
        return sent.reshape(-1, sent.shape[-1])

    def finish(self, got):
        return self.kept.astype(F32) + got.reshape(self.kept.shape).astype(F32)


def local(
    block_input,
    first_gain,
    first_shift,
    qkv_weight,
    qv_bias,
    proj_weight,
    proj_bias,
    second_gain,
    second_shift,
    fc_weight,
    fc_bias,
    out_weight,
    out_bias,
    cotangent,
    lengths,
):
    slots, model = block_input.shape
    width = qkv_weight.shape[2]
    units = fc_weight.shape[1]
    shards = lax.axis_size("dp")
    levels = shards.bit_length() - 1
    share = model // shards
    first_bit = next(bit for bit in range(levels) if (share << bit) % 16 == 0)
    block = share << first_bit
    later = [bit for bit in range(levels) if bit != first_bit]
    order_a = list(later)
    order_b = [later[1], later[0]] + later[2:]
    place = lax.axis_index("dp")
    quarter = jnp.bitwise_and(place, 3)
    one_bit = jnp.bitwise_and(place, 1)
    bits = jnp.stack(
        [
            one_bit,
            quarter,
            (place >> first_bit) & 1,
            lax.axis_index("tensor"),
            ((place >> 2) & 1) * 2 + one_bit,
        ]
    ).astype(jnp.int32)
    length = lengths.astype(jnp.int32)

    qkv_mine = across(pick(split_rows(qkv_weight, 4), quarter, 1))
    vectors = (first_gain, first_shift, proj_bias, second_gain, second_shift, out_bias)
    (
        vec,
        qkv0,
        grad_mlp,
        grad_mlp_turned,
        grad_out_bias,
        a_low,
        a_turned,
        proj_send,
        fc_send,
        out_send,
    ) = project(
        bits,
        length,
        block_input,
        cotangent,
        (*vectors, qv_bias, fc_bias),
        qkv_weight,
        proj_weight,
        fc_weight,
        out_weight,
    )

    qkv_mine, qkv0, proj_send, fc_send = tie(qkv_mine, qkv0, proj_send, fc_send)
    qkv_side = swap(qkv_mine, 2)
    qkv_core = swap(qkv_mine, 1)
    proj_got = across(proj_send)
    fc_mine = across(fc_send)
    lse0, ctx0, ctxt0, qkv0 = attention_forward_own(length, qkv0)

    qkv_side, qkv_core, proj_got, ctx0, out_send = tie(
        qkv_side, qkv_core, proj_got, ctx0, out_send
    )
    half_rows = width // 2
    parts = proj_got[half_rows : half_rows + 24].astype(F32).reshape(3, 8, model)
    other_vec = (parts[0] + parts[1]) + parts[2]
    proj_other = [proj_got, swap(proj_got, 1)]
    qkv_other = [qkv_mine, qkv_core, qkv_side, swap(qkv_side, 1)]
    out_mine = across(out_send)
    lse1, c_low, c_turned, middle, ctxt1, qkv1 = attention_forward_other(
        bits,
        length,
        other_vec,
        vec,
        a_low,
        block_input,
        ctx0,
        proj_weight,
        qkv_other,
        proj_other,
    )

    c_low, fc_mine, out_mine = tie(c_low, fc_mine, out_mine)
    fc_side = swap(fc_mine, 2)
    fc_core = swap(fc_mine, 1)
    out_side = swap(out_mine, 4)
    out_core = swap(out_mine, 1)
    gc0, act0, fc_kept, out_kept, fc_sent, out_sent, grad_fc_bias = feed_forward_own(
        bits, block, c_low, grad_mlp, c_turned, grad_mlp_turned, vec, fc_weight, out_weight
    )

    fc_sent, out_sent, fc_side, fc_core, out_side, out_core = tie(
        fc_sent, out_sent, fc_side, fc_core, out_side, out_core
    )
    fc_other = [fc_mine, fc_core, fc_side, swap(fc_side, 1)]
    out_other = [out_mine, out_core, out_side, swap(out_side, 1)]
    fc_got = swap(fc_sent, 1 << first_bit)
    out_got = swap(out_sent, 1 << first_bit)
    do0, fc_kept, out_kept, sums2, act1, grad_middle, grad_attn, do1 = feed_forward_other(
        bits,
        length,
        c_low,
        grad_mlp,
        other_vec,
        vec,
        gc0,
        middle,
        cotangent,
        proj_weight,
        (fc_kept, out_kept),
        fc_other,
        out_other,
        proj_other,
    )

    fc_sum = Reduction(fc_kept, first_bit, list(order_a))
    out_sum = Reduction(out_kept, first_bit, list(order_b))
    do0, fc_got, out_got = tie(do0, fc_got, out_got)
    fc_sent = fc_sum.advance(fc_got)
    out_sent = out_sum.advance(out_got)
    do0, fc_sent, out_sent = tie(do0, fc_sent, out_sent)
    fc_got = swap(fc_sent, 1 << fc_sum.bit)
    out_got = swap(out_sent, 1 << out_sum.bit)
    lead, vectors, d0, first_kept, first_sent, second_kept, second_sent = attention_backward_own(
        bits,
        length,
        block,
        lse0,
        vec,
        (grad_out_bias, sums2, grad_fc_bias),
        do0,
        qkv0,
        ctxt0,
        a_turned,
        grad_attn,
        qkv_weight,
    )

    first_sent, second_sent, lead, fc_got, out_got = tie(
        first_sent, second_sent, lead, fc_got, out_got
    )
    first_sum = Reduction(first_kept, first_bit, list(order_a))
    second_sum = Reduction(second_kept, first_bit, list(order_b))
    first_got = swap(first_sent, 1 << first_bit)
    second_got = swap(second_sent, 1 << first_bit)
    lead_got = across(lead)
    fc_sent = fc_sum.advance(fc_got)
    out_sent = out_sum.advance(out_got)
    fc_got = swap(fc_sent, 1 << fc_sum.bit)
    out_got = swap(out_sent, 1 << out_sum.bit)
    vectors = jnp.concatenate([(lead + lead_got)[:2], vectors[2:]], 0)

    def rounded(vectors):
        return lax.reduce_precision(vectors, 8, 7)

    def join(vectors, got):
        return rounded(vectors) + got.astype(F32)

    lines = vectors.shape[0]
    vectors = join(vectors, swap(vectors.astype(BF), 1 << first_bit))
    first_sent = jnp.concatenate([first_sum.advance(first_got), vectors.astype(BF)], 0)
    second_sent = second_sum.advance(second_got)
    first_sent, second_sent, qkv1 = tie(first_sent, second_sent, qkv1)
    first_got = swap(first_sent, 1 << first_sum.bit)
    second_got = swap(second_sent, 1 << second_sum.bit)
    d1 = attention_backward_other(length, lse1, qkv1, ctxt1, do1)

    d1, fc_got, out_got, first_got, second_got = tie(d1, fc_got, out_got, first_got, second_got)
    vectors = join(vectors, first_got[-lines:])
    first_sent = jnp.concatenate(
        [first_sum.advance(first_got[:-lines]), vectors.astype(BF)], 0
    )
    second_sent = second_sum.advance(second_got)
    rest_sent = jnp.concatenate([fc_sum.advance(fc_got), out_sum.advance(out_got)], 0)
    d1, first_sent, second_sent, rest_sent = tie(d1, first_sent, second_sent, rest_sent)
    first_got = swap(first_sent, 1 << first_sum.bit)
    second_got = swap(second_sent, 1 << second_sum.bit)
    rest_got = swap(rest_sent, 1 << fc_sum.bit)
    grad_input = gradient_of_input(
        bits, vec, d1, d0, block_input, grad_middle, qkv_weight, qkv_other
    )

    grad_input, first_got, second_got, act1 = tie(grad_input, first_got, second_got, act1)
    late = act1
    for level in range(3, levels):
        vectors = join(vectors, first_got[-lines:])
        sent = [first_sum.advance(first_got[:-lines]), second_sum.advance(second_got)]
        rows = sent[0].shape[0]
        sent = jnp.concatenate([*sent, vectors.astype(BF)], 0)
        sent, late = tie(sent, late)
        got = swap(sent, 1 << first_sum.bit)
        first_got = jnp.concatenate([got[:rows], got[2 * rows :]], 0)
        second_got = got[rows : 2 * rows]
        if fc_sum.order:
            rows = rest_got.shape[0] // 2
            rest_sent = [fc_sum.advance(rest_got[:rows]), out_sum.advance(rest_got[rows:])]
            rest_got = swap(jnp.concatenate(rest_sent, 0), 1 << fc_sum.bit)
    block_output = block_result(bits, vec, act0, late, middle, out_weight, out_other)
    vectors = join(vectors, first_got[-lines:])
    first = first_sum.finish(first_got[:-lines])
    second = second_sum.finish(second_got)
    rows = rest_got.shape[0] // 2
    grad_fc_weight = fc_sum.finish(rest_got[:rows])
    grad_out_weight = out_sum.finish(rest_got[rows:]).T
    grad_qkv_weight = jnp.stack([first[:, :width], first[:, width:], second[:, :width]])
    grad_proj_weight = second[:, width:].T
    return (
        block_output,
        grad_input,
        vectors[0],
        vectors[1],
        grad_qkv_weight,
        vectors[8].reshape(2, width),
        grad_proj_weight,
        vectors[5],
        vectors[3],
        vectors[4],
        grad_fc_weight,
        vectors[6:8].reshape(units),
        grad_out_weight,
        vectors[2],
    )


def solution(mesh):
    placed = (
        P("dp", None),
        P(),
        P(),
        P(None, None, "tensor"),
        P(None, "tensor"),
        P("tensor", None),
        P(),
        P(),
        P(),
        P(None, "tensor"),
        P("tensor"),
        P("tensor", None),
        P(),
        P("dp", None),
        P("dp"),
    )
    return jax.shard_map(
        local,
        mesh=mesh,
        in_specs=placed,
        out_specs=(
            P("dp", None),
            P("dp", None),
            P(),
            P(),
            P(None, "dp", "tensor"),
            P(None, "tensor"),
            P("tensor", "dp"),
            P(),
            P(),
            P(),
            P("dp", "tensor"),
            P("tensor"),
            P("tensor", "dp"),
            P(),
        ),
        check_vma=False,
    )
```

profile of v0, /device:TPU:0, one launch (start us, length us, event | category | flops | bytes accessed | tf_op | source)
XLA Modules:
  0.0 180.6 jit_solution(4294634267534749771)
XLA Ops:
  0.6 1.1 dynamic-slice_bitcast_fusion
  1.7 3.0 %collective-permute-start = (bf16[3,192,384]{2,1,0:T(8,128)(2,1)S(1)}, bf16[3,192,384]{2,1,0:T(8,128)(2,1)S(1)}, u32[]{:S(2)}, u32[]{:S(2)}) collective-permute-start(bf16[3,192,384]{2,1,0:T(8,128)(2,1)S(1)} %dynamic-slice_bitcast_fusion), channel_id=1, source_target_pairs={{0,1},{1,0},{2,3},{3,2},{4,5},{5,4},{6,7},{7,6},{8,9},{9,8},{10,11... | collective-permute-start | bytes 1327112 | tf_op jit(solution)/shard_map/ppermute | solution.py:1312
  5.5 8.3 %project_own.1 = (f32[16,768]{1,0:T(8,128)}, bf16[1024,1152]{1,0:T(8,128)(2,1)S(1)}, bf16[1024,768]{1,0:T(8,128)(2,1)S(1)}, bf16[768,1024]{1,0:T(8,128)(2,1)S(1)...) custom-call(s32[5]{0:T(128)S(1)} %stack.35.bits_ref, ...), custom_call_target="tpu_custom_call" | custom-call | flops 1811939328 | bytes 14972952 | tf_op jit(solution)/shard_map/project_own/pallas_call | solution.py:80
  13.8 1.1 collective-permute-done.rest_0_
  14.9 1.8 collective-permute-start.1
  16.7 1.5 collective-permute-start.3
  18.7 9.4 %attention_forward_own.1 = (f32[6,1024]{1,0:T(8,128)}, bf16[1024,384]{1,0:T(8,128)(2,1)}, f32[384,1024]{1,0:T(8,128)}, bf16[1024,1152]{1,0:T(8,128)(2,1)}) custom-call(s32[1]{0:T(128)S(6)} %copy.59.length_ref, bf16[1024,1152]{1,0:T(8,128)(2,1)S(1)} %get-tuple-element.109.qkv_ref), custom_call_target="tpu_custom_call" | custom-call | flops 2415919104 | bytes 4743172 | tf_op jit(solution)/shard_map/attention_forward_own/pallas_call | solution.py:80
  28.8 1.5 collective-permute-start.7
  31.8 18.2 %attention_forward_other.1 = (f32[6,1024]{1,0:T(8,128)}, bf16[1024,768]{1,0:T(8,128)(2,1)S(1)}, bf16[768,1024]{1,0:T(8,128)(2,1)S(1)}, f32[1024,768]{1,0:T(8,128...) custom-call(s32[5]{0:T(128)S(1)} %stack.35.bits_ref, s32[1]{0:T(128)S(6)} %copy.59.length_ref, ...), custom_call_target="tpu_custom_call" | custom-call | flops 5435817984 | bytes 14155800 | tf_op jit(solution)/shard_map/attention_forward_other/pallas_call | solution.py:80
  50.0 2.6 %collective-permute-done.7.rest_4_.rest_0_ = bf16[384,768]{1,0:T(8,128)(2,1)S(1)} collective-permute-done((bf16[384,768]{1,0:T(8,128)(2,1)S(1)}, bf16[384,768]{1,0:T(8,128)(2,1)S(1)}, u32[]{:S(2)}, u32[]{:S(2)}) %collective-permute-start.7) | collective-permute-done | bytes 589856 | tf_op jit(solution)/shard_map/ppermute | solution.py:1312
  52.6 1.6 collective-permute-start.10
  54.9 19.0 %feed_forward_own.1 = (bf16[1024,768]{1,0:T(8,128)(2,1)}, bf16[1024,1536]{1,0:T(8,128)(2,1)}, bf16[384,1536]{1,0:T(8,128)(2,1)}, bf16[384,1536]{1,0:T(8,128)(2,1...) custom-call(s32[5]{0:T(128)S(1)} %stack.35.bits_ref, ...), custom_call_target="tpu_custom_call" | custom-call | flops 12079595520 | bytes 11851796 | tf_op jit(solution)/shard_map/feed_forward_own/pallas_call | solution.py:80
  75.4 1.1 collective-permute-done.12.rest_3_
  76.5 1.5 collective-permute-done.13.rest_7_.rest_3_
  78.0 1.4 copy-done.1
  79.4 18.9 %feed_forward_other.1 = (bf16[1024,384]{1,0:T(8,128)(2,1)S(1)}, bf16[384,1536]{1,0:T(8,128)(2,1)S(1)}, bf16[384,1536]{1,0:T(8,128)(2,1)S(1)}, f32[3,768]{1,0:T(4...) custom-call(s32[5]{0:T(128)S(1)} %stack.35.bits_ref, ...), custom_call_target="tpu_custom_call" | custom-call | flops 8455716864 | bytes 23381016 | tf_op jit(solution)/shard_map/feed_forward_other/pallas_call | solution.py:80
  98.3 1.2 constant_dynamic-slice_fusion.2
  99.5 1.2 add_convert_fusion.2
  100.7 1.2 add_convert_fusion.3
  101.9 1.6 collective-permute-start.16
  104.1 19.7 %attention_backward_own.1 = (f32[8,768]{1,0:T(8,128)S(1)}, f32[16,768]{1,0:T(8,128)S(1)}, bf16[1024,1152]{1,0:T(8,128)(2,1)}, bf16[384,768]{1,0:T(8,128)(2,1)}, ...) custom-call(s32[5]{0:T(128)S(1)} %stack.35.bits_ref, s32[1]{0:T(128)S(6)} %copy.59.length_ref, ...), custom_call_target="tpu_custom_call" | custom-call | flops 6039797760 | bytes 13658136 | tf_op jit(solution)/shard_map/attention_backward_own/pallas_call | solution.py:80
  123.8 1.2 constant_dynamic-slice_fusion.4
  125.2 1.6 collective-permute-start.19
  128.0 1.1 collective-permute-done.19
  129.3 1.6 collective-permute-start.22
  131.4 1.0 collective-permute-start.24
  132.4 1.6 collective-permute-start.25
  134.0 13.7 %attention_backward_other.1.d1_ref = bf16[1024,1152]{1,0:T(8,128)(2,1)S(1)} custom-call(s32[1]{0:T(128)S(6)} %copy.59.length_ref, f32[6,1024]{1,0:T(8,128)} %get-tuple-element.161.lse_ref, bf16[1024,1152]{1,0:T(8,128)(2,1)} %get-tuple-element.167.qkv_hbm, f32[384,1024]{1,0:T(8,128)} %get-tuple-element.168.ctxt_hbm, bf16[1024,384]{1,0:T(8,128)(2,1)} %get-tuple-element.169.do_hbm), custom_call_target="tpu_custom_call" | custom-call | flops 3623878656 | bytes 4743172 | tf_op jit(solution)/shard_map/attention_backward_other/pallas_call | solution.py:80
  148.1 2.6 %collective-permute-start.29 = (bf16[96,1536]{1,0:T(8,128)(2,1)S(1)}, bf16[96,1536]{1,0:T(8,128)(2,1)S(1)}, u32[]{:S(2)}, u32[]{:S(2)}) collective-permute-start(bf16[96,1536]{1,0:T(8,128)(2,1)S(1)} %pad_maximum_fusion.1), channel_id=1, source_target_pairs={{0,16},{2,18},{4,20},{6,22},{8,24},{10,26},{12,28},{14,30},{16,0},... | collective-permute-start | bytes 884744 | tf_op jit(solution)/shard_map/ppermute | solution.py:1317
  151.2 1.2 collective-permute-start.27
  152.3 11.3 %final.1 = f32[1024,768]{1,0:T(8,128)} custom-call(s32[5]{0:T(128)S(1)} %stack.35.bits_ref, f32[16,768]{1,0:T(8,128)} %get-tuple-element.103.vec_ref, bf16[1024,1152]{1,0:T(8,128)(2,1)S(1)} %attention_backward_other.1.d1_ref, bf16[1024,1152]{1,0:T(8,128)(2,1)} %get-tuple-element.180.d0_hbm, bf16[1024,768]{1,0:T(8,128)(2,1)} %x_hbm.5, ...), custom_call_target="tpu_custom_call" | custom-call | flops 3623878656 | bytes 13811732 | tf_op jit(solution)/shard_map/final/pallas_call | solution.py:80
  164.2 12.1 %output.1 = bf16[1024,768]{1,0:T(8,128)(2,1)} custom-call(s32[5]{0:T(128)S(1)} %stack.35.bits_ref, f32[16,768]{1,0:T(8,128)} %get-tuple-element.103.vec_ref, bf16[1024,1536]{1,0:T(8,128)(2,1)} %get-tuple-element.124.act0_hbm, bf16[1024,1536]{1,0:T(8,128)(2,1)} %get-tuple-element.188.act1_hbm, f32[1024,768]{1,0:T(8,128)} %get-tuple-element.128.middle_hbm, ...), custom_call_target="tpu_custom_call" | custom-call | flops 4831838208 | bytes 15777812 | tf_op jit(solution)/shard_map/output/pallas_call | solution.py:80
  (117 shorter events, 13.0 us)
Async XLA Ops:
  1.7 13.2 %collective-permute-start = (bf16[3,192,384]{2,1,0:T(8,128)(2,1)S(1)}, bf16[3,192,384]{2,1,0:T(8,128)(2,1)S(1)}, u32[]{:S(2)}, u32[]{:S(2)}) collective-permute-start(bf16[3,192,384]{2,1,0:T(8,128)(2,1)S(1)} %dynamic-slice_bitcast_fusion), channel_id=1, source_target_pairs={{0,1},{1,0},{2,3},{3,2},{4,5},{5,4},{6,7},{7,6},{8,9},{9,8},{10,11... | collective-permute-start | bytes 1327112 | tf_op jit(solution)/shard_map/ppermute | solution.py:1312
  14.9 13.3 %collective-permute-start.1 = (bf16[3,192,384]{2,1,0:T(8,128)(2,1)S(1)}, bf16[3,192,384]{2,1,0:T(8,128)(2,1)S(1)}, u32[]{:S(2)}, u32[]{:S(2)}) collective-permute-start(bf16[3,192,384]{2,1,0:T(8,128)(2,1)S(1)} %collective-permute-done.rest_0_), channel_id=1, source_target_pairs={{0,4},{2,6},{4,0},{6,2},{8,12},{10,14},{12,8},{14,10},{16,20},{18,... | collective-permute-start | bytes 1327112 | tf_op jit(solution)/shard_map/ppermute | solution.py:1317
  16.7 11.5 %collective-permute-start.2 = (bf16[3,192,384]{2,1,0:T(8,128)(2,1)S(1)}, bf16[3,192,384]{2,1,0:T(8,128)(2,1)S(1)}, u32[]{:S(2)}, u32[]{:S(2)}) collective-permute-start(bf16[3,192,384]{2,1,0:T(8,128)(2,1)S(1)} %collective-permute-done.rest_0_), channel_id=1, source_target_pairs={{0,2},{2,0},{4,6},{6,4},{8,10},{10,8},{12,14},{14,12},{16,18},{18,... | collective-permute-start | bytes 1327112 | tf_op jit(solution)/shard_map/ppermute | solution.py:1317
  16.7 11.5 %collective-permute-start.3 = (bf16[224,768]{1,0:T(8,128)(2,1)}, bf16[224,768]{1,0:T(8,128)(2,1)S(1)}, u32[]{:S(2)}, u32[]{:S(2)}) collective-permute-start(bf16[224,768]{1,0:T(8,128)(2,1)} %get-tuple-element.108), channel_id=1, source_target_pairs={{0,1},{1,0},{2,3},{3,2},{4,5},{5,4},{6,7},{7,6},{8,9},{9,8},{10,11... | collective-permute-start | bytes 1032200 | tf_op jit(solution)/shard_map/ppermute | solution.py:1312
  18.2 31.8 %collective-permute-start.6 = (bf16[192,1536]{1,0:T(8,128)(2,1)}, bf16[192,1536]{1,0:T(8,128)(2,1)S(1)}, u32[]{:S(2)}, u32[]{:S(2)}) collective-permute-start(bf16[192,1536]{1,0:T(8,128)(2,1)} %get-tuple-element.118), channel_id=1, source_target_pairs={{0,1},{1,0},{2,3},{3,2},{4,5},{5,4},{6,7},{7,6},{8,9},{9,8},{10,11... | collective-permute-start | bytes 1769480 | tf_op jit(solution)/shard_map/ppermute | solution.py:1312
  28.2 2.7 %collective-permute-start.4 = (bf16[3,192,384]{2,1,0:T(8,128)(2,1)S(1)}, bf16[3,192,384]{2,1,0:T(8,128)(2,1)S(1)}, u32[]{:S(2)}, u32[]{:S(2)}) collective-permute-start(bf16[3,192,384]{2,1,0:T(8,128)(2,1)S(1)} %collective-permute-done.1.rest_2_), channel_id=1, source_target_pairs={{0,2},{2,0},{4,6},{6,4},{8,10},{10,8},{12,14},{14,12},{16,18},{18,... | collective-permute-start | bytes 1327112 | tf_op jit(solution)/shard_map/ppermute | solution.py:1317
  28.3 2.6 %collective-permute-start.5 = (bf16[224,768]{1,0:T(8,128)(2,1)S(1)}, bf16[224,768]{1,0:T(8,128)(2,1)S(1)}, u32[]{:S(2)}, u32[]{:S(2)}) collective-permute-start(bf16[224,768]{1,0:T(8,128)(2,1)S(1)} %collective-permute-done.3.rest_4_.rest_8_), channel_id=1, source_target_pairs={{0,2},{2,0},{4,6},{6,4},{8,10},{10,8},{12,14},{14,12},{16,18},{18,... | collective-permute-start | bytes 1032200 | tf_op jit(solution)/shard_map/ppermute | solution.py:1317
  28.8 23.9 %collective-permute-start.7 = (bf16[384,768]{1,0:T(8,128)(2,1)S(1)}, bf16[384,768]{1,0:T(8,128)(2,1)S(1)}, u32[]{:S(2)}, u32[]{:S(2)}) collective-permute-start(bf16[384,768]{1,0:T(8,128)(2,1)S(1)} %copy-done.16), channel_id=1, source_target_pairs={{0,1},{1,0},{2,3},{3,2},{4,5},{5,4},{6,7},{7,6},{8,9},{9,8},{10,11... | collective-permute-start | bytes 1769480 | tf_op jit(solution)/shard_map/ppermute | solution.py:1312
  50.0 24.0 %copy-start = (bf16[1024,768]{1,0:T(8,128)(2,1)}, bf16[1024,768]{1,0:T(8,128)(2,1)S(1)}, u32[]{:S(2)}) copy-start(bf16[1024,768]{1,0:T(8,128)(2,1)S(1)} %get-tuple-element.120.c_ref) | copy-start | bytes 4718596
  50.0 24.0 %copy-start.12 = (bf16[192,1536]{1,0:T(8,128)(2,1)}, bf16[192,1536]{1,0:T(8,128)(2,1)S(1)}, u32[]{:S(2)}) copy-start(bf16[192,1536]{1,0:T(8,128)(2,1)S(1)} %collective-permute-done.6.rest_0_) | copy-start | bytes 1769476
  52.6 21.4 %collective-permute-start.10 = (bf16[384,768]{1,0:T(8,128)(2,1)S(1)}, bf16[384,768]{1,0:T(8,128)(2,1)S(1)}, u32[]{:S(2)}, u32[]{:S(2)}) collective-permute-start(bf16[384,768]{1,0:T(8,128)(2,1)S(1)} %collective-permute-done.7.rest_4_.rest_0_), channel_id=1, source_target_pairs={{0,8},{2,10},{4,12},{6,14},{8,0},{10,2},{12,4},{14,6},{16,24},{18,... | collective-permute-start | bytes 1769480 | tf_op jit(solution)/shard_map/ppermute | solution.py:1317
  54.2 19.8 %collective-permute-start.11 = (bf16[384,768]{1,0:T(8,128)(2,1)S(1)}, bf16[384,768]{1,0:T(8,128)(2,1)S(1)}, u32[]{:S(2)}, u32[]{:S(2)}) collective-permute-start(bf16[384,768]{1,0:T(8,128)(2,1)S(1)} %collective-permute-done.7.rest_4_.rest_0_), channel_id=1, source_target_pairs={{0,2},{2,0},{4,6},{6,4},{8,10},{10,8},{12,14},{14,12},{16,18},{18,... | collective-permute-start | bytes 1769480 | tf_op jit(solution)/shard_map/ppermute | solution.py:1317
  54.2 19.8 %collective-permute-start.8 = (bf16[192,1536]{1,0:T(8,128)(2,1)S(1)}, bf16[192,1536]{1,0:T(8,128)(2,1)}, u32[]{:S(2)}, u32[]{:S(2)}) collective-permute-start(bf16[192,1536]{1,0:T(8,128)(2,1)S(1)} %collective-permute-done.6.rest_0_), channel_id=1, source_target_pairs={{0,4},{2,6},{4,0},{6,2},{8,12},{10,14},{12,8},{14,10},{16,20},{18,... | collective-permute-start | bytes 1769480 | tf_op jit(solution)/shard_map/ppermute | solution.py:1317
  54.7 19.3 %collective-permute-start.9 = (bf16[192,1536]{1,0:T(8,128)(2,1)S(1)}, bf16[192,1536]{1,0:T(8,128)(2,1)S(1)}, u32[]{:S(2)}, u32[]{:S(2)}) collective-permute-start(bf16[192,1536]{1,0:T(8,128)(2,1)S(1)} %collective-permute-done.6.rest_0_), channel_id=1, source_target_pairs={{0,2},{2,0},{4,6},{6,4},{8,10},{10,8},{12,14},{14,12},{16,18},{18,... | collective-permute-start | bytes 1769480 | tf_op jit(solution)/shard_map/ppermute | solution.py:1317
  74.1 2.4 %collective-permute-start.12 = (bf16[192,1536]{1,0:T(8,128)(2,1)}, bf16[192,1536]{1,0:T(8,128)(2,1)}, u32[]{:S(2)}, u32[]{:S(2)}) collective-permute-start(bf16[192,1536]{1,0:T(8,128)(2,1)} %collective-permute-done.8.rest_2_), channel_id=1, source_target_pairs={{0,2},{2,0},{4,6},{6,4},{8,10},{10,8},{12,14},{14,12},{16,18},{18,... | collective-permute-start | bytes 1769480 | tf_op jit(solution)/shard_map/ppermute | solution.py:1317
  74.4 3.6 %collective-permute-start.13 = (bf16[384,768]{1,0:T(8,128)(2,1)S(1)}, bf16[384,768]{1,0:T(8,128)(2,1)}, u32[]{:S(2)}, u32[]{:S(2)}) collective-permute-start(bf16[384,768]{1,0:T(8,128)(2,1)S(1)} %collective-permute-done.10.rest_6_.rest_2_), channel_id=1, source_target_pairs={{0,2},{2,0},{4,6},{6,4},{8,10},{10,8},{12,14},{14,12},{16,18},{18,... | collective-permute-start | bytes 1769480 | tf_op jit(solution)/shard_map/ppermute | solution.py:1317
  74.9 23.4 %collective-permute-start.14 = (bf16[384,1536]{1,0:T(8,128)(2,1)}, bf16[384,1536]{1,0:T(8,128)(2,1)}, u32[]{:S(2)}, u32[]{:S(2)}) collective-permute-start(bf16[384,1536]{1,0:T(8,128)(2,1)} %get-tuple-element.142), channel_id=1, source_target_pairs={{0,2},{2,0},{4,6},{6,4},{8,10},{10,8},{12,14},{14,12},{16,18},{18,... | collective-permute-start | bytes 3538952 | tf_op jit(solution)/shard_map/ppermute | solution.py:1317
  75.2 23.2 %collective-permute-start.15 = (bf16[384,1536]{1,0:T(8,128)(2,1)S(1)}, bf16[384,1536]{1,0:T(8,128)(2,1)}, u32[]{:S(2)}, u32[]{:S(2)}) collective-permute-start(bf16[384,1536]{1,0:T(8,128)(2,1)S(1)} %get-tuple-element.143), channel_id=1, source_target_pairs={{0,2},{2,0},{4,6},{6,4},{8,10},{10,8},{12,14},{14,12},{16,18},{18,... | collective-permute-start | bytes 3538952 | tf_op jit(solution)/shard_map/ppermute | solution.py:1317
  101.9 23.2 %collective-permute-start.16 = (bf16[192,1536]{1,0:T(8,128)(2,1)S(1)}, bf16[192,1536]{1,0:T(8,128)(2,1)S(1)}, u32[]{:S(2)}, u32[]{:S(2)}) collective-permute-start(bf16[192,1536]{1,0:T(8,128)(2,1)S(1)} %bitcast.152), channel_id=1, source_target_pairs={{0,4},{2,6},{4,0},{6,2},{8,12},{10,14},{12,8},{14,10},{16,20},{18,... | collective-permute-start | bytes 1769480 | tf_op jit(solution)/shard_map/ppermute | solution.py:1317
  103.5 21.7 %collective-permute-start.17 = (bf16[192,1536]{1,0:T(8,128)(2,1)S(1)}, bf16[192,1536]{1,0:T(8,128)(2,1)S(1)}, u32[]{:S(2)}, u32[]{:S(2)}) collective-permute-start(bf16[192,1536]{1,0:T(8,128)(2,1)S(1)} %bitcast.151), channel_id=1, source_target_pairs={{0,8},{2,10},{4,12},{6,14},{8,0},{10,2},{12,4},{14,6},{16,24},{18,... | collective-permute-start | bytes 1769480 | tf_op jit(solution)/shard_map/ppermute | solution.py:1317
  125.2 3.9 %collective-permute-start.19 = (f32[8,768]{1,0:T(8,128)S(1)}, f32[8,768]{1,0:T(8,128)S(1)}, u32[]{:S(2)}, u32[]{:S(2)}) collective-permute-start(f32[8,768]{1,0:T(8,128)S(1)} %get-tuple-element.162), channel_id=1, source_target_pairs={{0,1},{1,0},{2,3},{3,2},{4,5},{5,4},{6,7},{7,6},{8,9},{9,8},{10,11... | collective-permute-start | bytes 73736 | tf_op jit(solution)/shard_map/ppermute | solution.py:1312
  126.9 20.7 %collective-permute-start.23 = (bf16[96,1536]{1,0:T(8,128)(2,1)S(1)}, bf16[96,1536]{1,0:T(8,128)(2,1)S(1)}, u32[]{:S(2)}, u32[]{:S(2)}) collective-permute-start(bf16[96,1536]{1,0:T(8,128)(2,1)S(1)} %bitcast.159), channel_id=1, source_target_pairs={{0,4},{2,6},{4,0},{6,2},{8,12},{10,14},{12,8},{14,10},{16,20},{18,... | collective-permute-start | bytes 884744 | tf_op jit(solution)/shard_map/ppermute | solution.py:1317
  127.5 3.5 %collective-permute-start.21 = (bf16[384,768]{1,0:T(8,128)(2,1)S(1)}, bf16[384,768]{1,0:T(8,128)(2,1)S(1)}, u32[]{:S(2)}, u32[]{:S(2)}) collective-permute-start(bf16[384,768]{1,0:T(8,128)(2,1)S(1)} %copy-done.15), channel_id=1, source_target_pairs={{0,2},{2,0},{4,6},{6,4},{8,10},{10,8},{12,14},{14,12},{16,18},{18,... | collective-permute-start | bytes 1769480 | tf_op jit(solution)/shard_map/ppermute | solution.py:1317
  127.5 3.7 %collective-permute-start.18 = (bf16[384,768]{1,0:T(8,128)(2,1)S(1)}, bf16[384,768]{1,0:T(8,128)(2,1)S(1)}, u32[]{:S(2)}, u32[]{:S(2)}) collective-permute-start(bf16[384,768]{1,0:T(8,128)(2,1)S(1)} %copy-done.14), channel_id=1, source_target_pairs={{0,2},{2,0},{4,6},{6,4},{8,10},{10,8},{12,14},{14,12},{16,18},{18,... | collective-permute-start | bytes 1769480 | tf_op jit(solution)/shard_map/ppermute | solution.py:1317
  129.1 1.9 %collective-permute-start.20 = (bf16[16,768]{1,0:T(8,128)(2,1)S(1)}, bf16[16,768]{1,0:T(8,128)(2,1)S(1)}, u32[]{:S(2)}, u32[]{:S(2)}) collective-permute-start(bf16[16,768]{1,0:T(8,128)(2,1)S(1)} %fusion.25), channel_id=1, source_target_pairs={{0,2},{2,0},{4,6},{6,4},{8,10},{10,8},{12,14},{14,12},{16,18},{18,... | collective-permute-start | bytes 73736 | tf_op jit(solution)/shard_map/ppermute | solution.py:1317
  129.3 18.3 %collective-permute-start.22 = (bf16[96,1536]{1,0:T(8,128)(2,1)S(1)}, bf16[96,1536]{1,0:T(8,128)(2,1)S(1)}, u32[]{:S(2)}, u32[]{:S(2)}) collective-permute-start(bf16[96,1536]{1,0:T(8,128)(2,1)S(1)} %bitcast.160), channel_id=1, source_target_pairs={{0,8},{2,10},{4,12},{6,14},{8,0},{10,2},{12,4},{14,6},{16,24},{18,... | collective-permute-start | bytes 884744 | tf_op jit(solution)/shard_map/ppermute | solution.py:1317
  131.4 16.2 %collective-permute-start.24 = (bf16[208,768]{1,0:T(8,128)(2,1)S(1)}, bf16[208,768]{1,0:T(8,128)(2,1)S(1)}, u32[]{:S(2)}, u32[]{:S(2)}) collective-permute-start(bf16[208,768]{1,0:T(8,128)(2,1)S(1)} %pad_maximum_fusion), channel_id=1, source_target_pairs={{0,4},{2,6},{4,0},{6,2},{8,12},{10,14},{12,8},{14,10},{16,20},{18,... | collective-permute-start | bytes 958472 | tf_op jit(solution)/shard_map/ppermute | solution.py:1317
  132.4 15.3 %collective-permute-start.25 = (bf16[192,768]{1,0:T(8,128)(2,1)S(1)}, bf16[192,768]{1,0:T(8,128)(2,1)S(1)}, u32[]{:S(2)}, u32[]{:S(2)}) collective-permute-start(bf16[192,768]{1,0:T(8,128)(2,1)S(1)} %bitcast.154), channel_id=1, source_target_pairs={{0,8},{2,10},{4,12},{6,14},{8,0},{10,2},{12,4},{14,6},{16,24},{18,... | collective-permute-start | bytes 884744 | tf_op jit(solution)/shard_map/ppermute | solution.py:1317
  148.1 28.3 %collective-permute-start.29 = (bf16[96,1536]{1,0:T(8,128)(2,1)S(1)}, bf16[96,1536]{1,0:T(8,128)(2,1)S(1)}, u32[]{:S(2)}, u32[]{:S(2)}) collective-permute-start(bf16[96,1536]{1,0:T(8,128)(2,1)S(1)} %pad_maximum_fusion.1), channel_id=1, source_target_pairs={{0,16},{2,18},{4,20},{6,22},{8,24},{10,26},{12,28},{14,30},{16,0},... | collective-permute-start | bytes 884744 | tf_op jit(solution)/shard_map/ppermute | solution.py:1317
  150.7 12.9 %collective-permute-start.26 = (bf16[112,768]{1,0:T(8,128)(2,1)S(1)}, bf16[112,768]{1,0:T(8,128)(2,1)S(1)}, u32[]{:S(2)}, u32[]{:S(2)}) collective-permute-start(bf16[112,768]{1,0:T(8,128)(2,1)S(1)} %pad_maximum_fusion.3), channel_id=1, source_target_pairs={{0,8},{2,10},{4,12},{6,14},{8,0},{10,2},{12,4},{14,6},{16,24},{18,... | collective-permute-start | bytes 516104 | tf_op jit(solution)/shard_map/ppermute | solution.py:1317
  151.2 12.4 %collective-permute-start.27 = (bf16[96,768]{1,0:T(8,128)(2,1)S(1)}, bf16[96,768]{1,0:T(8,128)(2,1)S(1)}, u32[]{:S(2)}, u32[]{:S(2)}) collective-permute-start(bf16[96,768]{1,0:T(8,128)(2,1)S(1)} %bitcast.164), channel_id=1, source_target_pairs={{0,4},{2,6},{4,0},{6,2},{8,12},{10,14},{12,8},{14,10},{16,20},{18,... | collective-permute-start | bytes 442376 | tf_op jit(solution)/shard_map/ppermute | solution.py:1317
  163.8 13.5 %collective-permute-start.28 = (bf16[112,768]{1,0:T(8,128)(2,1)S(1)}, bf16[112,768]{1,0:T(8,128)(2,1)S(1)}, u32[]{:S(2)}, u32[]{:S(2)}) collective-permute-start(bf16[112,768]{1,0:T(8,128)(2,1)S(1)} %pad_maximum_fusion.4), channel_id=1, source_target_pairs={{0,16},{2,18},{4,20},{6,22},{8,24},{10,26},{12,28},{14,30},{16,0},... | collective-permute-start | bytes 516104 | tf_op jit(solution)/shard_map/ppermute | solution.py:1317
  (16 other events, 76.4 us)
where the time goes:
time: 181 us
  Pallas kernels  131 us (72%)
  starting transfers between devices  25.8 us (14%)
  local copies, waits for them, and re-layouts  8.6 us (5%)
  waiting for transfers between devices  7.41 us (4%)
  other arithmetic  6.17 us (3%)
  between operations  1.93 us (1%)
    pallas_call x9, Pallas kernels, call(): pl.pallas_call(body, name=name, grid=(steps,), out_shape=tuple(((pltpu.VM...  131 us
    ppermute x25, starting transfers between devices, swap(): return lax.ppermute(value, 'dp', [(i, i ^ bit) for i in range(count)])  17.7 us
    ppermute x5, starting transfers between devices, across(): return lax.ppermute(value, 'tensor', [(0, 1), (1, 0)])  8.09 us
    ppermute x5, waiting for transfers between devices, across(): return lax.ppermute(value, 'tensor', [(0, 1), (1, 0)])  4.81 us
    convert_element_type x16, other arithmetic, part(): return total.astype(BF)  3.66 us
  transfers between devices with their start and end apart: 30, of which 5 were waited for; matrix products, arithmetic and copies ran while one was open for 2% of the time, Pallas kernels for 72%

commit v1 on v0

--- a/solution.py
+++ b/solution.py
@@ -344,7 +344,7 @@
         + [pltpu.VMEM((slots, model), BF), pltpu.VMEM((TILE, model), BF)]
         + [dma((tokens,)), dma((3,)), dma((tokens,)), dma((6,)), dma((tokens,)), dma((tokens,))],
         6 * slots * model * width,
-        20,
+        12,
     )
 
 
@@ -369,6 +369,10 @@
         ).astype(BF)
 
 
+def block_order(blocks):
+    return [(block, 0) for block in range(blocks)] + [(block, 1) for block in reversed(range(blocks))]
+
+
 def pair_lanes(pair, offset=0):
     return pl.ds(pl.multiple_of(offset + pair * 128, 128), 128)
 
@@ -385,7 +389,7 @@
             qkv_ref[:, pair_lanes(pair, width)], qkv_ref[:, lanes], length, ka_ref, qa_ref
         )
         vt_ref[...] = qkv_ref[:, pair_lanes(pair, 2 * width)].T
-        items = [(block, half) for block in range(slots // TILE) for half in (0, 1)]
+        items = block_order(slots // TILE)
         state = {}
 
         def score(item):
@@ -565,6 +569,7 @@
         ],
         [*forward_scratch(slots, width), pltpu.SemaphoreType.DMA((3, width // 128))],
         6 * slots * slots * width,
+        6,
     )
 
 
@@ -609,7 +614,7 @@
             dma((tokens,)),
         ],
         6 * slots * slots * width + 10 * slots * model * width,
-        28,
+        20,
     )
 
 
@@ -714,7 +719,7 @@
             pltpu.SemaphoreType.DMA,
         ],
         10 * slots * model * units,
-        32,
+        19,
     )
 
 
@@ -858,75 +863,26 @@
             dma((3, tokens)),
         ],
         6 * slots * model * units + 4 * slots * model * width,
-        42,
-    )
-
-
-def output_kernel(bits_ref, vec_ref, act0_hbm, act1_hbm, middle_hbm, ow_hbm, *rest):
-    pieces, (y_out, act_ref, ow_ref, middle_ref, y_ref, act_sems, sems, m_sem, y_sems) = (
-        rest[:4],
-        rest[4:],
-    )
-    slots, units = act0_hbm.shape
-    own = pl.ds(pl.multiple_of(bits_ref[3] * units, 128), units)
-    other = pl.ds(pl.multiple_of((1 - bits_ref[3]) * units, 128), units)
-    copies = fetch_rows([ow_hbm], 0, ow_ref.at[own, :], sems.at[0])
-    copies += fetch_rows(pieces, bits_ref[4], ow_ref.at[other, :], sems.at[1])
-    acts = []
-    for index in range(slots // TILE):
-        rows = slice(index * TILE, (index + 1) * TILE)
-        for group, (source, lanes) in enumerate(((act0_hbm, own), (act1_hbm, other))):
-            acts.append(
-                pltpu.make_async_copy(
-                    source.at[rows, :], act_ref.at[rows, lanes], act_sems.at[group, index]
-                )
-            )
-    middle_in = tiles(middle_hbm, middle_ref, m_sem)
-    start_all(acts[:2] + copies)
-    for index, copy in enumerate(middle_in):
-        copy.start()
-        start_all(acts[2 * index + 2 : 2 * index + 4])
-    wait_all(copies)
-
-    @pl.loop(0, slots // TILE)
-    def _(index):
-        rows = tile_of(index)
-        for group, (source, lanes) in enumerate(((act0_hbm, own), (act1_hbm, other))):
-            pltpu.make_async_copy(
-                source.at[rows, :], act_ref.at[rows, lanes], act_sems.at[group, index]
-            ).wait()
-        tile_copy(middle_hbm, middle_ref, m_sem, index).wait()
-        mlp = dot(act_ref[rows, :], ow_ref[...]) + vec_ref[BIAS_O : BIAS_O + 1, :]
-        y_ref[rows, :] = (middle_ref[rows, :] + BRANCH * mlp).astype(BF)
-        tile_copy(y_ref, y_out, y_sems, index).start()
-
-    wait_all(tiles(y_ref, y_out, y_sems))
-
-
-def block_result(bits, vec, act0, act1, middle, ow, pieces):
+        31,
+    )
+
+
+def output_kernel(vec_ref, act_ref, ow_ref, middle_ref, y_ref):
+    mlp = dot(act_ref[tile_of(pl.program_id(0)), :], ow_ref[...]) + vec_ref[BIAS_O : BIAS_O + 1, :]
+    y_ref[...] = (middle_ref[...] + BRANCH * mlp).astype(BF)
+
+
+def block_result(vec, act, ow, middle):
     slots, model = middle.shape
-    units = act0.shape[1]
-    tokens = slots // TILE
-    dma = pltpu.SemaphoreType.DMA
     return call(
         output_kernel,
         "output",
-        1,
-        [(bits, SMEM), (vec, whole(vec.shape))]
-        + [(value, HBM) for value in (act0, act1, middle, ow, *pieces)],
-        [((slots, model), BF, HBM)],
-        [
-            pltpu.VMEM((slots, 2 * units), BF),
-            pltpu.VMEM((2 * units, model), BF),
-            pltpu.VMEM((slots, model), F32),
-            pltpu.VMEM((slots, model), BF),
-            dma((2, tokens)),
-            dma((2, 4)),
-            dma((tokens,)),
-            dma((tokens,)),
-        ],
-        4 * slots * model * units,
-        24,
+        slots // TILE,
+        [(vec, whole(vec.shape)), (act, KEPT), (ow, KEPT), (middle, row_tile(model))],
+        [((slots, model), BF, row_tile(model))],
+        [],
+        2 * slots * model * act.shape[1],
+        5,
     )[0]
 
 
@@ -971,7 +927,7 @@
             delta_ref[half : half + 1, :] = jnp.sum(
                 product[64 * half : 64 * half + 64], 0, keepdims=True
             )
-        items = [(block, half) for block in reversed(range(blocks)) for half in (0, 1)]
+        items = block_order(blocks)
 
         def score(item):
             block, half = items[item]
@@ -1007,12 +963,13 @@
             rows = slice(64 * half, 64 * half + 64)
             dv_part = dot_nt(dot_ref[rows, columns], prob_ref[item % 2, :extent, :])
             dk_part = dot_nt(qt_ref[rows, columns], slope_ref[item % 2, :extent, :])
-            if block == blocks - 1:
-                dvt_ref[rows, :extent] = dv_part
-                dkt_ref[rows, :extent] = dk_part
-            else:
-                dvt_ref[rows, :extent] += dv_part
-                dkt_ref[rows, :extent] += dk_part
+            fresh = block * TILE if half == 0 else (0 if block == blocks - 1 else extent)
+            if fresh < extent:
+                dvt_ref[rows, fresh:extent] = dv_part[:, fresh:]
+                dkt_ref[rows, fresh:extent] = dk_part[:, fresh:]
+            if fresh:
+                dvt_ref[rows, :fresh] += dv_part[:, :fresh]
+                dkt_ref[rows, :fresh] += dk_part[:, :fresh]
             dqt_ref[rows, columns] = dot(kt_ref[rows, :extent], slope_ref[item % 2, :extent, :])
 
         count_items = len(items)
@@ -1045,16 +1002,31 @@
 
 
 def backward_other_kernel(
-    length_ref, lse_ref, qkv_hbm, ctxt_hbm, do_hbm, d_ref, qkv_ref, ctxt_ref, do_ref, *rest
+    bits_ref, length_ref, lse_ref, qkv_hbm, ctxt_hbm, do_hbm, d0_hbm, w_hbm, ow_hbm, *rest
 ):
-    scratch, sems = rest[:14], rest[14]
+    pieces, out_pieces, rest = rest[:4], rest[4:8], rest[8:]
+    both_ref, weight_ref, ow_ref, qkv_ref, ctxt_ref, do_ref, *rest = rest
+    scratch, (sems, late_sem, w_sems, ow_sems) = rest[:14], rest[14:]
     width = do_ref.shape[1]
     sources = lambda pair: pair_sources(
         pair, width, (qkv_hbm, qkv_ref), (ctxt_hbm, ctxt_ref), (do_hbm, do_ref), sems
     )
     for pair in range(width // 128):
         start_all(sources(pair))
+    own = pl.ds(pl.multiple_of(bits_ref[3] * 3 * width, 128), 3 * width)
+    other = pl.ds(pl.multiple_of((1 - bits_ref[3]) * 3 * width, 128), 3 * width)
+    late = [pltpu.make_async_copy(d0_hbm, both_ref.at[:, own], late_sem)]
+    late += fetch_rows([w_hbm], 0, weight_ref.at[:, own], w_sems.at[0])
+    late += fetch_rows(pieces, bits_ref[1], weight_ref.at[:, other], w_sems.at[1])
+    units = ow_hbm.shape[0]
+    rows = pl.ds(pl.multiple_of(bits_ref[3] * units, 128), units)
+    late += fetch_rows([ow_hbm], 0, ow_ref.at[rows, :], ow_sems.at[0])
+    rows = pl.ds(pl.multiple_of((1 - bits_ref[3]) * units, 128), units)
+    late += fetch_rows(out_pieces, bits_ref[4], ow_ref.at[rows, :], ow_sems.at[1])
+    start_all(late)
+    d_ref = both_ref.at[:, other]
     backward_pairs(length_ref[0], qkv_ref, do_ref, ctxt_ref, lse_ref, d_ref, scratch, sources)
+    wait_all(late)
 
 
 def lane_sums(value):
@@ -1081,17 +1053,15 @@
     w_hbm,
     lead_ref,
     vectors_ref,
+    kept_ref,
+    sent_ref,
     d_out,
-    first_kept_out,
-    first_sent_out,
-    second_kept_out,
-    second_sent_out,
     qkv_ref,
     ctxt_ref,
     *rest,
 ):
     scratch, rest = rest[:14], rest[14:]
-    d_ref, at_ref, gat_ref, w_ref, dw_ref, half_ref, total_ref, sems, w_sems, late_sems, out_sems = rest
+    d_ref, at_ref, gat_ref, w_ref, dw_ref, total_ref, sems, w_sems, late_sems, out_sem = rest
     width = do_ref.shape[1]
     model = at_ref.shape[0]
     sources = lambda pair: pair_sources(
@@ -1106,21 +1076,12 @@
     ]
     start_all(late)
     backward_pairs(length_ref[0], qkv_ref, do_ref, ctxt_ref, lse_ref, d_ref, scratch, sources)
-    results = [pltpu.make_async_copy(d_ref, d_out, out_sems.at[4])]
-    results[0].start()
+    saved = pltpu.make_async_copy(d_ref, d_out, out_sem)
+    saved.start()
     lead_ref[...] = jnp.zeros(lead_ref.shape, F32)
     wait_all(late)
-    side = bits_ref[2]
-    outs = (first_kept_out, first_sent_out, second_kept_out, second_sent_out)
-
-    def give(index):
-        halves(dw_ref.at[index], side, block, half_ref.at[2 * index], half_ref.at[2 * index + 1])
-        for part in (2 * index, 2 * index + 1):
-            results.append(pltpu.make_async_copy(half_ref.at[part], outs[part], out_sems.at[part]))
-            results[-1].start()
-
     low = ctxt_ref[...].astype(BF)
-    dw_ref[1, :, width:] = dot(low, gat_ref[...]).T.astype(BF)
+    dw_ref[:, 3 * width :] = dot(low, gat_ref[...]).T.astype(BF)
     total_ref[...] = jnp.zeros(total_ref.shape, F32)
 
     @pl.loop(0, d_ref.shape[0] // TILE)
@@ -1133,14 +1094,12 @@
     def _(index):
         rows = tile_of(index)
         part = dot(at_ref[rows, :], d_ref[...])
-        dw_ref[0, rows, :] = part[:, :model].astype(BF)
-        dw_ref[1, rows, :width] = part[:, model:].astype(BF)
+        dw_ref[rows, : 3 * width] = part.astype(BF)
         weight = w_ref[rows, :].astype(F32)
         lead_ref[0:1, rows] = lane_sums(part * weight)
         lead_ref[1:2, rows] = lane_sums(weight * sums)
 
-    give(0)
-    give(1)
+    halves(dw_ref, bits_ref[2], block, kept_ref, sent_ref)
     scaled, shift = lead_ref[0:1, :], lead_ref[1:2, :]
     gain1, shift1 = vec_ref[GAIN1 : GAIN1 + 1, :], vec_ref[SHIFT1 : SHIFT1 + 1, :]
     vectors_ref[...] = jnp.zeros(vectors_ref.shape, F32)
@@ -1151,7 +1110,7 @@
         vectors_ref[6 + index : 7 + index, :] = db_ref[:, index * model : (index + 1) * model]
     vectors_ref[8:9, :width] = sums[:, :width]
     vectors_ref[8:9, width:] = sums[:, 2 * width :]
-    wait_all(results)
+    saved.wait()
 
 
 def backward_scratch(slots):
@@ -1173,25 +1132,35 @@
     ]
 
 
-def attention_backward_other(length, lse, qkv, ctxt, do):
+def attention_backward_other(bits, length, lse, qkv, ctxt, do, d0, weight, ow, pieces, out_pieces):
     slots, width = do.shape
-    ins = [(length, SMEM), (lse, whole(lse.shape)), (qkv, HBM), (ctxt, HBM), (do, HBM)]
+    model = weight.shape[1]
+    dma = pltpu.SemaphoreType.DMA
+    ins = [(bits, SMEM), (length, SMEM), (lse, whole(lse.shape))]
+    ins += [(value, HBM) for value in (qkv, ctxt, do, d0, weight, ow, *pieces, *out_pieces)]
     return call(
         backward_other_kernel,
         "attention_backward_other",
         1,
         ins,
-        [((slots, 3 * width), BF, KEPT)],
+        [
+            ((slots, 6 * width), BF, KEPT),
+            ((model, 6 * width), BF, KEPT),
+            ((2 * ow.shape[0], model), BF, KEPT),
+        ],
         [
             pltpu.VMEM((slots, 3 * width), BF),
             pltpu.VMEM((width, slots), F32),
             pltpu.VMEM((slots, width), BF),
             *backward_scratch(slots),
-            pltpu.SemaphoreType.DMA((5, width // 128)),
+            dma((5, width // 128)),
+            dma,
+            dma((2, 12)),
+            dma((2, 4)),
         ],
         9 * slots * slots * width,
-        18,
-    )[0]
+        12,
+    )
 
 
 def attention_backward_own(bits, length, block, lse, vec, sums, do, qkv, ctxt, at, gat, weight):
@@ -1201,8 +1170,8 @@
     ins = [(bits, SMEM), (length, SMEM)]
     ins += [(value, whole(value.shape)) for value in (lse, vec, *sums)]
     ins += [(do, KEPT)] + [(value, HBM) for value in (qkv, ctxt, at, gat, weight)]
-    outs = [((rows, model), F32, KEPT) for rows in (8, 16)] + [((slots, 3 * width), BF, HBM)]
-    outs += [((model // 2, model), BF, HBM)] * 4
+    outs = [((rows, model), F32, KEPT) for rows in (8, 16)] + [((model // 2, 4 * width), BF, KEPT)] * 2
+    outs += [((slots, 3 * width), BF, HBM)]
     return call(
         functools.partial(backward_own_kernel, block),
         "attention_backward_own",
@@ -1217,42 +1186,36 @@
             pltpu.VMEM((model, slots), BF),
             pltpu.VMEM((slots, model), BF),
             pltpu.VMEM((model, 3 * width), BF),
-            pltpu.VMEM((2, model, model), BF),
-            pltpu.VMEM((4, model // 2, model), BF),
+            pltpu.VMEM((model, 4 * width), BF),
             pltpu.VMEM((1, 3 * width), F32),
             dma((4, width // 128)),
             dma((3,)),
             dma((2,)),
-            dma((5,)),
+            dma,
         ],
         9 * slots * slots * width + 8 * slots * model * width,
-        32,
-    )
-
-
-def final_kernel(bits_ref, vec_ref, d1_ref, d0_hbm, x_hbm, gmid_hbm, w_hbm, *rest):
-    pieces, (gin_out, d_ref, x_ref, gmid_ref, w_ref, gin_ref, product_ref, *rest) = (
-        rest[:4],
-        rest[4:],
-    )
-    w_sems, d_sems, x_sems, gmid_sems, gin_sems = rest
-    total = d1_ref.shape[1]
-    own = pl.ds(pl.multiple_of(bits_ref[3] * total, 128), total)
-    other = pl.ds(pl.multiple_of((1 - bits_ref[3]) * total, 128), total)
-    copies = fetch_rows([w_hbm], 0, w_ref.at[:, own], w_sems.at[0])
-    copies += fetch_rows(pieces, bits_ref[1], w_ref.at[:, other], w_sems.at[1])
-    d_in = tiles(d0_hbm, d_ref.at[:, own], d_sems)
+        21,
+    )
+
+
+def final_kernel(
+    bits_ref, vec_ref, d_ref, w_ref, x_hbm, gmid_hbm, act0_hbm, act1_hbm, *rest
+):
+    gin_out, act_ref, x_ref, gmid_ref, gin_ref, product_ref, *rest = rest
+    x_sems, gmid_sems, gin_sems, act_sems = rest
     x_in = tiles(x_hbm, x_ref, x_sems)
     gmid_in = tiles(gmid_hbm, gmid_ref, gmid_sems)
     gin_tiles = tiles(gin_ref, gin_out, gin_sems)
-    d_in[0].start()
-    start_all(copies)
-    start_all(d_in[1:] + x_in + gmid_in)
-    count = len(d_in)
-
-    @pl.loop(0, count)
-    def _(index):
-        d_ref[tile_of(index), other] = d1_ref[tile_of(index), :]
+    start_all(x_in + gmid_in)
+    units = act0_hbm.shape[1]
+    own = pl.ds(pl.multiple_of(bits_ref[3] * units, 128), units)
+    other = pl.ds(pl.multiple_of((1 - bits_ref[3]) * units, 128), units)
+    late = [
+        pltpu.make_async_copy(act0_hbm, act_ref.at[:, own], act_sems.at[0]),
+        pltpu.make_async_copy(act1_hbm, act_ref.at[:, other], act_sems.at[1]),
+    ]
+    start_all(late)
+    count = len(x_in)
 
     def product(index):
         return dot_nt(d_ref[tile_of(index), :], w_ref[...])
@@ -1263,7 +1226,6 @@
         back = norm_back(product_ref[...], normed, inverse, vec_ref[GAIN1 : GAIN1 + 1, :])
         gin_ref[rows, :] = gmid_ref[rows, :] + back
 
-    wait_all(copies + d_in)
     product_ref[...] = product(0)
     wait_all(x_in + gmid_in)
 
@@ -1275,37 +1237,37 @@
 
     norm(count - 1)
     gin_tiles[-1].start()
-    wait_all(gin_tiles)
-
-
-def gradient_of_input(bits, vec, d1, d0, x, gmid, weight, pieces):
+    wait_all(late + gin_tiles)
+
+
+def gradient_of_input(bits, vec, both, weight, x, gmid, act0, act1):
     slots, model = x.shape
-    total = d1.shape[1]
+    units = act0.shape[1]
     tokens = slots // TILE
     dma = pltpu.SemaphoreType.DMA
     return call(
         final_kernel,
         "final",
         1,
-        [(bits, SMEM), (vec, whole(vec.shape)), (d1, KEPT)]
-        + [(value, HBM) for value in (d0, x, gmid, weight, *pieces)],
-        [((slots, model), F32, HBM)],
+        [(bits, SMEM), (vec, whole(vec.shape)), (both, KEPT), (weight, KEPT)]
+        + [(value, HBM) for value in (x, gmid, act0, act1)],
         [
-            pltpu.VMEM((slots, 2 * total), BF),
+            ((slots, model), F32, HBM),
+            ((slots, 2 * units), BF, KEPT),
+        ],
+        [
             pltpu.VMEM((slots, model), BF),
             pltpu.VMEM((slots, model), F32),
-            pltpu.VMEM((model, 2 * total), BF),
             pltpu.VMEM((slots, model), F32),
             pltpu.VMEM((TILE, model), F32),
-            dma((2, 12)),
             dma((tokens,)),
             dma((tokens,)),
             dma((tokens,)),
-            dma((tokens,)),
+            dma((2,)),
         ],
-        4 * slots * model * total,
-        28,
-    )[0]
+        2 * slots * model * both.shape[1],
+        13,
+    )
 
 
 def across(value):
@@ -1493,7 +1455,7 @@
     do0, fc_sent, out_sent = tie(do0, fc_sent, out_sent)
     fc_got = swap(fc_sent, 1 << fc_sum.bit)
     out_got = swap(out_sent, 1 << out_sum.bit)
-    lead, vectors, d0, first_kept, first_sent, second_kept, second_sent = attention_backward_own(
+    lead, vectors, kept, sent, d0 = attention_backward_own(
         bits,
         length,
         block,
@@ -1508,19 +1470,13 @@
         qkv_weight,
     )
 
-    first_sent, second_sent, lead, fc_got, out_got = tie(
-        first_sent, second_sent, lead, fc_got, out_got
-    )
-    first_sum = Reduction(first_kept, first_bit, list(order_a))
-    second_sum = Reduction(second_kept, first_bit, list(order_b))
-    first_got = swap(first_sent, 1 << first_bit)
-    second_got = swap(second_sent, 1 << first_bit)
+    sent, lead, fc_got, out_got = tie(sent, lead, fc_got, out_got)
+    attn_got = swap(sent, 1 << first_bit)
     lead_got = across(lead)
     fc_sent = fc_sum.advance(fc_got)
     out_sent = out_sum.advance(out_got)
     fc_got = swap(fc_sent, 1 << fc_sum.bit)
     out_got = swap(out_sent, 1 << out_sum.bit)
-    vectors = jnp.concatenate([(lead + lead_got)[:2], vectors[2:]], 0)
 
     def rounded(vectors):
         return lax.reduce_precision(vectors, 8, 7)
@@ -1528,38 +1484,44 @@
     def join(vectors, got):
         return rounded(vectors) + got.astype(F32)
 
+    vectors = jnp.concatenate([(lead + lead_got)[:2], vectors[2:]], 0)
     lines = vectors.shape[0]
     vectors = join(vectors, swap(vectors.astype(BF), 1 << first_bit))
-    first_sent = jnp.concatenate([first_sum.advance(first_got), vectors.astype(BF)], 0)
-    second_sent = second_sum.advance(second_got)
+    first_sum = Reduction(kept[:, :model], first_bit, list(order_a))
+    second_sum = Reduction(kept[:, model:], first_bit, list(order_b))
+    first_sent = jnp.concatenate(
+        [first_sum.advance(attn_got[:, :model]), vectors.astype(BF)], 0
+    )
+    second_sent = second_sum.advance(attn_got[:, model:])
     first_sent, second_sent, qkv1 = tie(first_sent, second_sent, qkv1)
     first_got = swap(first_sent, 1 << first_sum.bit)
     second_got = swap(second_sent, 1 << second_sum.bit)
-    d1 = attention_backward_other(length, lse1, qkv1, ctxt1, do1)
-
-    d1, fc_got, out_got, first_got, second_got = tie(d1, fc_got, out_got, first_got, second_got)
+    both, weights, ow = attention_backward_other(
+        bits, length, lse1, qkv1, ctxt1, do1, d0, qkv_weight, out_weight, qkv_other, out_other
+    )
+
+    both, fc_got, out_got, first_got, second_got = tie(both, fc_got, out_got, first_got, second_got)
     vectors = join(vectors, first_got[-lines:])
     first_sent = jnp.concatenate(
         [first_sum.advance(first_got[:-lines]), vectors.astype(BF)], 0
     )
     second_sent = second_sum.advance(second_got)
     rest_sent = jnp.concatenate([fc_sum.advance(fc_got), out_sum.advance(out_got)], 0)
-    d1, first_sent, second_sent, rest_sent = tie(d1, first_sent, second_sent, rest_sent)
+    both, first_sent, second_sent, rest_sent = tie(both, first_sent, second_sent, rest_sent)
     first_got = swap(first_sent, 1 << first_sum.bit)
     second_got = swap(second_sent, 1 << second_sum.bit)
     rest_got = swap(rest_sent, 1 << fc_sum.bit)
-    grad_input = gradient_of_input(
-        bits, vec, d1, d0, block_input, grad_middle, qkv_weight, qkv_other
-    )
-
-    grad_input, first_got, second_got, act1 = tie(grad_input, first_got, second_got, act1)
-    late = act1
+    grad_input, act = gradient_of_input(
+        bits, vec, both, weights, block_input, grad_middle, act0, act1
+    )
+
+    grad_input, first_got, second_got, act = tie(grad_input, first_got, second_got, act)
     for level in range(3, levels):
         vectors = join(vectors, first_got[-lines:])
         sent = [first_sum.advance(first_got[:-lines]), second_sum.advance(second_got)]
         rows = sent[0].shape[0]
         sent = jnp.concatenate([*sent, vectors.astype(BF)], 0)
-        sent, late = tie(sent, late)
+        sent, act = tie(sent, act)
         got = swap(sent, 1 << first_sum.bit)
         first_got = jnp.concatenate([got[:rows], got[2 * rows :]], 0)
         second_got = got[rows : 2 * rows]
@@ -1567,7 +1529,7 @@
             rows = rest_got.shape[0] // 2
             rest_sent = [fc_sum.advance(rest_got[:rows]), out_sum.advance(rest_got[rows:])]
             rest_got = swap(jnp.concatenate(rest_sent, 0), 1 << fc_sum.bit)
-    block_output = block_result(bits, vec, act0, late, middle, out_weight, out_other)
+    block_output = block_result(vec, act, ow, middle)
     vectors = join(vectors, first_got[-lines:])
     first = first_sum.finish(first_got[:-lines])
     second = second_sum.finish(second_got)

time: 181 us -> 176 us (0.972)
  Pallas kernels: 131 us -> 122 us
  waiting for transfers between devices: 7.41 us -> 10.7 us
    pallas_call x9, Pallas kernels: 131 us -> 122 us  [call(): pl.pallas_call(body, name=name, grid=(steps,), out_shape=tuple(((pltpu.VM...]
    ppermute x5, waiting for transfers between devices: 4.81 us -> 7.19 us  [across(): return lax.ppermute(value, 'tensor', [(0, 1), (1, 0)])]
    ppermute x25 -> x24, starting transfers between devices: 17.7 us -> 17.3 us  [swap(): return lax.ppermute(value, 'dp', [(i, i ^ bit) for i in range(count)])]
  transfers between devices with their start and end apart: 30 -> 29, of which waited for: 5 -> 7; matrix products, arithmetic and copies ran while one was open for 2% -> 2% of each run, Pallas kernels for 72% -> 69%
where the time goes in v1:
time: 176 us
  Pallas kernels  122 us (69%)
  starting transfers between devices  25.4 us (14%)
  waiting for transfers between devices  10.7 us (6%)
  local copies, waits for them, and re-layouts  9.6 us (5%)
  other arithmetic  6.13 us (3%)
  between operations  1.86 us (1%)
    pallas_call x9, Pallas kernels, call(): pl.pallas_call(body, name=name, grid=(steps,), out_shape=tuple(((pltpu.VM...  122 us
    ppermute x24, starting transfers between devices, swap(): return lax.ppermute(value, 'dp', [(i, i ^ bit) for i in range(count)])  17.3 us
    ppermute x5, starting transfers between devices, across(): return lax.ppermute(value, 'tensor', [(0, 1), (1, 0)])  8.07 us
    ppermute x5, waiting for transfers between devices, across(): return lax.ppermute(value, 'tensor', [(0, 1), (1, 0)])  7.19 us
    convert_element_type x16, other arithmetic, part(): return total.astype(BF)  3.64 us
    ppermute x24, waiting for transfers between devices, swap(): return lax.ppermute(value, 'dp', [(i, i ^ bit) for i in range(count)])  3.55 us
  transfers between devices with their start and end apart: 29, of which 7 were waited for; matrix products, arithmetic and copies ran while one was open for 2% of the time, Pallas kernels for 69%

profile of v1, /device:TPU:0, one launch (start us, length us, event | category | flops | bytes accessed | tf_op | source)
XLA Modules:
  0.0 175.5 jit_solution(9523647496287176135)
XLA Ops:
  0.6 1.1 dynamic-slice_bitcast_fusion
  1.7 3.0 %collective-permute-start = (bf16[3,192,384]{2,1,0:T(8,128)(2,1)S(1)}, bf16[3,192,384]{2,1,0:T(8,128)(2,1)S(1)}, u32[]{:S(2)}, u32[]{:S(2)}) collective-permute-start(bf16[3,192,384]{2,1,0:T(8,128)(2,1)S(1)} %dynamic-slice_bitcast_fusion), channel_id=1, source_target_pairs={{0,1},{1,0},{2,3},{3,2},{4,5},{5,4},{6,7},{7,6},{8,9},{9,8},{10,11... | collective-permute-start | bytes 1327112 | tf_op jit(solution)/shard_map/ppermute | solution.py:1274
  5.5 8.3 %project_own.1 = (f32[16,768]{1,0:T(8,128)}, bf16[1024,1152]{1,0:T(8,128)(2,1)S(1)}, bf16[1024,768]{1,0:T(8,128)(2,1)S(1)}, bf16[768,1024]{1,0:T(8,128)(2,1)S(1)...) custom-call(s32[5]{0:T(128)S(1)} %stack.35.bits_ref, ...), custom_call_target="tpu_custom_call" | custom-call | flops 1811939328 | bytes 14972952 | tf_op jit(solution)/shard_map/project_own/pallas_call | solution.py:80
  13.8 1.1 collective-permute-done.rest_0_
  14.9 1.8 %collective-permute-start.1 = (bf16[3,192,384]{2,1,0:T(8,128)(2,1)S(1)}, bf16[3,192,384]{2,1,0:T(8,128)(2,1)S(1)}, u32[]{:S(2)}, u32[]{:S(2)}) collective-permute-start(bf16[3,192,384]{2,1,0:T(8,128)(2,1)S(1)} %collective-permute-done.rest_0_), channel_id=1, source_target_pairs={{0,4},{2,6},{4,0},{6,2},{8,12},{10,14},{12,8},{14,10},{16,20},{18,... | collective-permute-start | bytes 1327112 | tf_op jit(solution)/shard_map/ppermute | solution.py:1279
  16.7 1.5 collective-permute-start.3
  18.7 8.4 %attention_forward_own.1 = (f32[6,1024]{1,0:T(8,128)}, bf16[1024,384]{1,0:T(8,128)(2,1)}, f32[384,1024]{1,0:T(8,128)}, bf16[1024,1152]{1,0:T(8,128)(2,1)}) custom-call(s32[1]{0:T(128)S(6)} %copy.59.length_ref, bf16[1024,1152]{1,0:T(8,128)(2,1)S(1)} %get-tuple-element.109.qkv_ref), custom_call_target="tpu_custom_call" | custom-call | flops 2415919104 | bytes 4743172 | tf_op jit(solution)/shard_map/attention_forward_own/pallas_call | solution.py:80
  28.3 1.5 collective-permute-start.7
  31.4 17.3 %attention_forward_other.1 = (f32[6,1024]{1,0:T(8,128)}, bf16[1024,768]{1,0:T(8,128)(2,1)S(1)}, bf16[768,1024]{1,0:T(8,128)(2,1)S(1)}, f32[1024,768]{1,0:T(8,128...) custom-call(s32[5]{0:T(128)S(1)} %stack.35.bits_ref, s32[1]{0:T(128)S(6)} %copy.59.length_ref, ...), custom_call_target="tpu_custom_call" | custom-call | flops 5435817984 | bytes 14155800 | tf_op jit(solution)/shard_map/attention_forward_other/pallas_call | solution.py:80
  48.7 3.9 %collective-permute-done.7.rest_4_ = bf16[384,768]{1,0:T(8,128)(2,1)S(1)} collective-permute-done((bf16[384,768]{1,0:T(8,128)(2,1)S(1)}, bf16[384,768]{1,0:T(8,128)(2,1)S(1)}, u32[]{:S(2)}, u32[]{:S(2)}) %collective-permute-start.7) | collective-permute-done | bytes 589856 | tf_op jit(solution)/shard_map/ppermute | solution.py:1274
  52.6 1.6 collective-permute-start.10
  54.9 19.0 %feed_forward_own.1 = (bf16[1024,768]{1,0:T(8,128)(2,1)}, bf16[1024,1536]{1,0:T(8,128)(2,1)}, bf16[384,1536]{1,0:T(8,128)(2,1)}, bf16[384,1536]{1,0:T(8,128)(2,1...) custom-call(s32[5]{0:T(128)S(1)} %stack.35.bits_ref, ...), custom_call_target="tpu_custom_call" | custom-call | flops 12079595520 | bytes 11851796 | tf_op jit(solution)/shard_map/feed_forward_own/pallas_call | solution.py:80
  75.4 1.1 collective-permute-done.12.rest_3_
  76.5 1.6 collective-permute-done.13.rest_7_
  78.8 1.4 copy-done.1
  80.2 19.1 %feed_forward_other.1 = (bf16[1024,384]{1,0:T(8,128)(2,1)S(1)}, bf16[384,1536]{1,0:T(8,128)(2,1)S(1)}, bf16[384,1536]{1,0:T(8,128)(2,1)S(1)}, f32[3,768]{1,0:T(4...) custom-call(s32[5]{0:T(128)S(1)} %stack.35.bits_ref, ...), custom_call_target="tpu_custom_call" | custom-call | flops 8455716864 | bytes 23381016 | tf_op jit(solution)/shard_map/feed_forward_other/pallas_call | solution.py:80
  99.3 1.2 constant_dynamic-slice_fusion.2
  100.5 1.2 add_convert_fusion.2
  101.7 1.2 add_convert_fusion.3
  102.9 1.6 collective-permute-start.16
  105.0 1.1 constant_dynamic-slice_fusion.4
  106.4 18.1 %attention_backward_own.1 = (f32[8,768]{1,0:T(8,128)S(1)}, f32[16,768]{1,0:T(8,128)S(1)}, bf16[384,1536]{1,0:T(8,128)(2,1)S(1)}, bf16[384,1536]{1,0:T(8,128)(2,1)S(1)}, bf16[1024,1152]{1,0:T(8,128)(2,1)}) custom-call(s32[5]{0:T(128)S(1)} %stack.35.bits_ref, s32[1]{0:T(128)S(6)} %copy.59.length_ref, f32[6,1024]{1,0:T(8,128)} %get-tuple-element.110.lse_ref, ...), custom_call_target="tpu_custom_call" | custom-call | flops 6039797760 | bytes 11298840 | tf_op jit(solution)/shard_map/attention_backward_own/pallas_call | solution.py:80
  124.7 1.6 collective-permute-start.19
  127.0 1.6 collective-permute-done.19
  128.9 1.6 collective-permute-start.21
  131.5 1.0 collective-permute-start.24
  132.6 14.3 %attention_backward_other.1 = (bf16[1024,2304]{1,0:T(8,128)(2,1)S(1)}, bf16[768,2304]{1,0:T(8,128)(2,1)S(1)}, bf16[3072,768]{1,0:T(8,128)(2,1)S(1)}) custom-call(s32[5]{0:T(128)S(1)} %stack.35.bits_ref, s32[1]{0:T(128)S(6)} %copy.59.length_ref, f32[6,1024]{1,0:T(8,128)} %get-tuple-element.161.lse_ref, bf16[1024,1152]{1,0:T(8,128)(2,1)} %get-tuple-element.165.qkv_hbm, ...), custom_call_target="tpu_custom_call" | custom-call | flops 3623878656 | bytes 15360024 | tf_op jit(solution)/shard_map/attention_backward_other/pallas_call | solution.py:80
  147.4 2.7 %collective-permute-start.28 = (bf16[96,1536]{1,0:T(8,128)(2,1)S(1)}, bf16[96,1536]{1,0:T(8,128)(2,1)S(1)}, u32[]{:S(2)}, u32[]{:S(2)}) collective-permute-start(bf16[96,1536]{1,0:T(8,128)(2,1)S(1)} %pad_maximum_fusion.1), channel_id=1, source_target_pairs={{0,16},{2,18},{4,20},{6,22},{8,24},{10,26},{12,28},{14,30},{16,0},... | collective-permute-start | bytes 884744 | tf_op jit(solution)/shard_map/ppermute | solution.py:1279
  150.1 1.1 collective-permute-start.25
  151.1 1.5 collective-permute-start.26
  152.7 9.7 %final.1 = (f32[1024,768]{1,0:T(8,128)}, bf16[1024,3072]{1,0:T(8,128)(2,1)S(1)}) custom-call(s32[5]{0:T(128)S(1)} %stack.35.bits_ref, f32[16,768]{1,0:T(8,128)} %get-tuple-element.105.vec_ref, bf16[1024,2304]{1,0:T(8,128)(2,1)S(1)} %get-tuple-element.179.d_ref, bf16[768,2304]{1,0:T(8,128)(2,1)S(1)} %get-tuple-element.180.w_ref, bf16[1024,768]{1,0:T(8,128)(2,1)} %x_hbm.5, ...), custom_call_target="tpu_custom_call" | custom-call | flops 3623878656 | bytes 14204948 | tf_op jit(solution)/shard_map/final/pallas_call | solution.py:80
  162.9 7.6 %output.1 = bf16[1024,768]{1,0:T(8,128)(2,1)} custom-call(f32[16,768]{1,0:T(8,128)} %get-tuple-element.105.vec_ref, bf16[1024,3072]{1,0:T(8,128)(2,1)S(1)} %get-tuple-element.191.act_ref, bf16[3072,768]{1,0:T(8,128)(2,1)S(1)} %get-tuple-element.192.ow_ref, f32[1024,768]{1,0:T(8,128)} %get-tuple-element.129.middle_hbm.middle_ref), custom_call_target="tpu_custom_call" | custom-call | flops 4831838208 | bytes 4767744 | tf_op jit(solution)/shard_map/output/pallas_call | solution.py:80
  (111 shorter events, 15.1 us)
Async XLA Ops:
  1.7 13.2 %collective-permute-start = (bf16[3,192,384]{2,1,0:T(8,128)(2,1)S(1)}, bf16[3,192,384]{2,1,0:T(8,128)(2,1)S(1)}, u32[]{:S(2)}, u32[]{:S(2)}) collective-permute-start(bf16[3,192,384]{2,1,0:T(8,128)(2,1)S(1)} %dynamic-slice_bitcast_fusion), channel_id=1, source_target_pairs={{0,1},{1,0},{2,3},{3,2},{4,5},{5,4},{6,7},{7,6},{8,9},{9,8},{10,11... | collective-permute-start | bytes 1327112 | tf_op jit(solution)/shard_map/ppermute | solution.py:1274
  14.9 12.8 %collective-permute-start.1 = (bf16[3,192,384]{2,1,0:T(8,128)(2,1)S(1)}, bf16[3,192,384]{2,1,0:T(8,128)(2,1)S(1)}, u32[]{:S(2)}, u32[]{:S(2)}) collective-permute-start(bf16[3,192,384]{2,1,0:T(8,128)(2,1)S(1)} %collective-permute-done.rest_0_), channel_id=1, source_target_pairs={{0,4},{2,6},{4,0},{6,2},{8,12},{10,14},{12,8},{14,10},{16,20},{18,... | collective-permute-start | bytes 1327112 | tf_op jit(solution)/shard_map/ppermute | solution.py:1279
  16.7 11.1 %collective-permute-start.2 = (bf16[3,192,384]{2,1,0:T(8,128)(2,1)S(1)}, bf16[3,192,384]{2,1,0:T(8,128)(2,1)S(1)}, u32[]{:S(2)}, u32[]{:S(2)}) collective-permute-start(bf16[3,192,384]{2,1,0:T(8,128)(2,1)S(1)} %collective-permute-done.rest_0_), channel_id=1, source_target_pairs={{0,2},{2,0},{4,6},{6,4},{8,10},{10,8},{12,14},{14,12},{16,18},{18,... | collective-permute-start | bytes 1327112 | tf_op jit(solution)/shard_map/ppermute | solution.py:1279
  16.7 11.1 %collective-permute-start.3 = (bf16[224,768]{1,0:T(8,128)(2,1)}, bf16[224,768]{1,0:T(8,128)(2,1)S(1)}, u32[]{:S(2)}, u32[]{:S(2)}) collective-permute-start(bf16[224,768]{1,0:T(8,128)(2,1)} %get-tuple-element.113), channel_id=1, source_target_pairs={{0,1},{1,0},{2,3},{3,2},{4,5},{5,4},{6,7},{7,6},{8,9},{9,8},{10,11... | collective-permute-start | bytes 1032200 | tf_op jit(solution)/shard_map/ppermute | solution.py:1274
  18.2 30.5 %collective-permute-start.6 = (bf16[192,1536]{1,0:T(8,128)(2,1)}, bf16[192,1536]{1,0:T(8,128)(2,1)S(1)}, u32[]{:S(2)}, u32[]{:S(2)}) collective-permute-start(bf16[192,1536]{1,0:T(8,128)(2,1)} %get-tuple-element.122), channel_id=1, source_target_pairs={{0,1},{1,0},{2,3},{3,2},{4,5},{5,4},{6,7},{7,6},{8,9},{9,8},{10,11... | collective-permute-start | bytes 1769480 | tf_op jit(solution)/shard_map/ppermute | solution.py:1274
  27.8 2.7 %collective-permute-start.4 = (bf16[3,192,384]{2,1,0:T(8,128)(2,1)S(1)}, bf16[3,192,384]{2,1,0:T(8,128)(2,1)S(1)}, u32[]{:S(2)}, u32[]{:S(2)}) collective-permute-start(bf16[3,192,384]{2,1,0:T(8,128)(2,1)S(1)} %collective-permute-done.1.rest_2_), channel_id=1, source_target_pairs={{0,2},{2,0},{4,6},{6,4},{8,10},{10,8},{12,14},{14,12},{16,18},{18,... | collective-permute-start | bytes 1327112 | tf_op jit(solution)/shard_map/ppermute | solution.py:1279
  27.8 2.6 %collective-permute-start.5 = (bf16[224,768]{1,0:T(8,128)(2,1)S(1)}, bf16[224,768]{1,0:T(8,128)(2,1)S(1)}, u32[]{:S(2)}, u32[]{:S(2)}) collective-permute-start(bf16[224,768]{1,0:T(8,128)(2,1)S(1)} %collective-permute-done.3.rest_4_.rest_8_), channel_id=1, source_target_pairs={{0,2},{2,0},{4,6},{6,4},{8,10},{10,8},{12,14},{14,12},{16,18},{18,... | collective-permute-start | bytes 1032200 | tf_op jit(solution)/shard_map/ppermute | solution.py:1279
  28.3 24.3 %collective-permute-start.7 = (bf16[384,768]{1,0:T(8,128)(2,1)S(1)}, bf16[384,768]{1,0:T(8,128)(2,1)S(1)}, u32[]{:S(2)}, u32[]{:S(2)}) collective-permute-start(bf16[384,768]{1,0:T(8,128)(2,1)S(1)} %copy-done.12), channel_id=1, source_target_pairs={{0,1},{1,0},{2,3},{3,2},{4,5},{5,4},{6,7},{7,6},{8,9},{9,8},{10,11... | collective-permute-start | bytes 1769480 | tf_op jit(solution)/shard_map/ppermute | solution.py:1274
  48.7 25.3 %copy-start = (bf16[1024,768]{1,0:T(8,128)(2,1)}, bf16[1024,768]{1,0:T(8,128)(2,1)S(1)}, u32[]{:S(2)}) copy-start(bf16[1024,768]{1,0:T(8,128)(2,1)S(1)} %get-tuple-element.124.c_ref) | copy-start | bytes 4718596
  48.7 25.3 %copy-start.10 = (bf16[192,1536]{1,0:T(8,128)(2,1)}, bf16[192,1536]{1,0:T(8,128)(2,1)S(1)}, u32[]{:S(2)}) copy-start(bf16[192,1536]{1,0:T(8,128)(2,1)S(1)} %collective-permute-done.6.rest_0_) | copy-start | bytes 1769476
  52.6 21.4 %copy-start.2 = (bf16[384,768]{1,0:T(8,128)(2,1)}, bf16[384,768]{1,0:T(8,128)(2,1)S(1)}, u32[]{:S(2)}) copy-start(bf16[384,768]{1,0:T(8,128)(2,1)S(1)} %collective-permute-done.7.rest_4_) | copy-start | bytes 1769476
  52.6 21.4 %collective-permute-start.10 = (bf16[384,768]{1,0:T(8,128)(2,1)S(1)}, bf16[384,768]{1,0:T(8,128)(2,1)}, u32[]{:S(2)}, u32[]{:S(2)}) collective-permute-start(bf16[384,768]{1,0:T(8,128)(2,1)S(1)} %collective-permute-done.7.rest_4_), channel_id=1, source_target_pairs={{0,8},{2,10},{4,12},{6,14},{8,0},{10,2},{12,4},{14,6},{16,24},{18,... | collective-permute-start | bytes 1769480 | tf_op jit(solution)/shard_map/ppermute | solution.py:1279
  54.2 19.8 %collective-permute-start.11 = (bf16[384,768]{1,0:T(8,128)(2,1)S(1)}, bf16[384,768]{1,0:T(8,128)(2,1)S(1)}, u32[]{:S(2)}, u32[]{:S(2)}) collective-permute-start(bf16[384,768]{1,0:T(8,128)(2,1)S(1)} %collective-permute-done.7.rest_4_), channel_id=1, source_target_pairs={{0,2},{2,0},{4,6},{6,4},{8,10},{10,8},{12,14},{14,12},{16,18},{18,... | collective-permute-start | bytes 1769480 | tf_op jit(solution)/shard_map/ppermute | solution.py:1279
  54.2 19.8 %collective-permute-start.8 = (bf16[192,1536]{1,0:T(8,128)(2,1)S(1)}, bf16[192,1536]{1,0:T(8,128)(2,1)}, u32[]{:S(2)}, u32[]{:S(2)}) collective-permute-start(bf16[192,1536]{1,0:T(8,128)(2,1)S(1)} %collective-permute-done.6.rest_0_), channel_id=1, source_target_pairs={{0,4},{2,6},{4,0},{6,2},{8,12},{10,14},{12,8},{14,10},{16,20},{18,... | collective-permute-start | bytes 1769480 | tf_op jit(solution)/shard_map/ppermute | solution.py:1279
  54.7 19.3 %collective-permute-start.9 = (bf16[192,1536]{1,0:T(8,128)(2,1)S(1)}, bf16[192,1536]{1,0:T(8,128)(2,1)S(1)}, u32[]{:S(2)}, u32[]{:S(2)}) collective-permute-start(bf16[192,1536]{1,0:T(8,128)(2,1)S(1)} %collective-permute-done.6.rest_0_), channel_id=1, source_target_pairs={{0,2},{2,0},{4,6},{6,4},{8,10},{10,8},{12,14},{14,12},{16,18},{18,... | collective-permute-start | bytes 1769480 | tf_op jit(solution)/shard_map/ppermute | solution.py:1279
  74.1 2.4 %collective-permute-start.12 = (bf16[192,1536]{1,0:T(8,128)(2,1)}, bf16[192,1536]{1,0:T(8,128)(2,1)}, u32[]{:S(2)}, u32[]{:S(2)}) collective-permute-start(bf16[192,1536]{1,0:T(8,128)(2,1)} %collective-permute-done.8.rest_2_), channel_id=1, source_target_pairs={{0,2},{2,0},{4,6},{6,4},{8,10},{10,8},{12,14},{14,12},{16,18},{18,... | collective-permute-start | bytes 1769480 | tf_op jit(solution)/shard_map/ppermute | solution.py:1279
  74.4 3.7 %collective-permute-start.13 = (bf16[384,768]{1,0:T(8,128)(2,1)}, bf16[384,768]{1,0:T(8,128)(2,1)S(1)}, u32[]{:S(2)}, u32[]{:S(2)}) collective-permute-start(bf16[384,768]{1,0:T(8,128)(2,1)} %collective-permute-done.10.rest_6_), channel_id=1, source_target_pairs={{0,2},{2,0},{4,6},{6,4},{8,10},{10,8},{12,14},{14,12},{16,18},{18,... | collective-permute-start | bytes 1769480 | tf_op jit(solution)/shard_map/ppermute | solution.py:1279
  74.8 24.5 %collective-permute-start.14 = (bf16[384,1536]{1,0:T(8,128)(2,1)}, bf16[384,1536]{1,0:T(8,128)(2,1)}, u32[]{:S(2)}, u32[]{:S(2)}) collective-permute-start(bf16[384,1536]{1,0:T(8,128)(2,1)} %get-tuple-element.143), channel_id=1, source_target_pairs={{0,2},{2,0},{4,6},{6,4},{8,10},{10,8},{12,14},{14,12},{16,18},{18,... | collective-permute-start | bytes 3538952 | tf_op jit(solution)/shard_map/ppermute | solution.py:1279
  75.1 24.2 %collective-permute-start.15 = (bf16[384,1536]{1,0:T(8,128)(2,1)S(1)}, bf16[384,1536]{1,0:T(8,128)(2,1)}, u32[]{:S(2)}, u32[]{:S(2)}) collective-permute-start(bf16[384,1536]{1,0:T(8,128)(2,1)S(1)} %get-tuple-element.144), channel_id=1, source_target_pairs={{0,2},{2,0},{4,6},{6,4},{8,10},{10,8},{12,14},{14,12},{16,18},{18,... | collective-permute-start | bytes 3538952 | tf_op jit(solution)/shard_map/ppermute | solution.py:1279
  102.9 21.6 %collective-permute-start.16 = (bf16[192,1536]{1,0:T(8,128)(2,1)S(1)}, bf16[192,1536]{1,0:T(8,128)(2,1)S(1)}, u32[]{:S(2)}, u32[]{:S(2)}) collective-permute-start(bf16[192,1536]{1,0:T(8,128)(2,1)S(1)} %bitcast.152), channel_id=1, source_target_pairs={{0,4},{2,6},{4,0},{6,2},{8,12},{10,14},{12,8},{14,10},{16,20},{18,... | collective-permute-start | bytes 1769480 | tf_op jit(solution)/shard_map/ppermute | solution.py:1279
  104.5 20.0 %collective-permute-start.17 = (bf16[192,1536]{1,0:T(8,128)(2,1)S(1)}, bf16[192,1536]{1,0:T(8,128)(2,1)S(1)}, u32[]{:S(2)}, u32[]{:S(2)}) collective-permute-start(bf16[192,1536]{1,0:T(8,128)(2,1)S(1)} %bitcast.151), channel_id=1, source_target_pairs={{0,8},{2,10},{4,12},{6,14},{8,0},{10,2},{12,4},{14,6},{16,24},{18,... | collective-permute-start | bytes 1769480 | tf_op jit(solution)/shard_map/ppermute | solution.py:1279
  124.5 6.0 %collective-permute-start.18 = (bf16[384,1536]{1,0:T(8,128)(2,1)S(1)}, bf16[384,1536]{1,0:T(8,128)(2,1)S(1)}, u32[]{:S(2)}, u32[]{:S(2)}) collective-permute-start(bf16[384,1536]{1,0:T(8,128)(2,1)S(1)} %get-tuple-element.160), channel_id=1, source_target_pairs={{0,2},{2,0},{4,6},{6,4},{8,10},{10,8},{12,14},{14,12},{16,18},{18,... | collective-permute-start | bytes 3538952 | tf_op jit(solution)/shard_map/ppermute | solution.py:1279
  124.7 3.9 %collective-permute-start.19 = (f32[8,768]{1,0:T(8,128)S(1)}, f32[8,768]{1,0:T(8,128)S(1)}, u32[]{:S(2)}, u32[]{:S(2)}) collective-permute-start(f32[8,768]{1,0:T(8,128)S(1)} %get-tuple-element.162), channel_id=1, source_target_pairs={{0,1},{1,0},{2,3},{3,2},{4,5},{5,4},{6,7},{7,6},{8,9},{9,8},{10,11... | collective-permute-start | bytes 73736 | tf_op jit(solution)/shard_map/ppermute | solution.py:1274
  126.4 20.5 %collective-permute-start.22 = (bf16[96,1536]{1,0:T(8,128)(2,1)S(1)}, bf16[96,1536]{1,0:T(8,128)(2,1)S(1)}, u32[]{:S(2)}, u32[]{:S(2)}) collective-permute-start(bf16[96,1536]{1,0:T(8,128)(2,1)S(1)} %bitcast.159), channel_id=1, source_target_pairs={{0,4},{2,6},{4,0},{6,2},{8,12},{10,14},{12,8},{14,10},{16,20},{18,... | collective-permute-start | bytes 884744 | tf_op jit(solution)/shard_map/ppermute | solution.py:1279
  128.6 1.9 %collective-permute-start.20 = (bf16[16,768]{1,0:T(8,128)(2,1)S(1)}, bf16[16,768]{1,0:T(8,128)(2,1)S(1)}, u32[]{:S(2)}, u32[]{:S(2)}) collective-permute-start(bf16[16,768]{1,0:T(8,128)(2,1)S(1)} %fusion.25), channel_id=1, source_target_pairs={{0,2},{2,0},{4,6},{6,4},{8,10},{10,8},{12,14},{14,12},{16,18},{18,... | collective-permute-start | bytes 73736 | tf_op jit(solution)/shard_map/ppermute | solution.py:1279
  128.9 18.1 %collective-permute-start.21 = (bf16[96,1536]{1,0:T(8,128)(2,1)S(1)}, bf16[96,1536]{1,0:T(8,128)(2,1)S(1)}, u32[]{:S(2)}, u32[]{:S(2)}) collective-permute-start(bf16[96,1536]{1,0:T(8,128)(2,1)S(1)} %bitcast.160), channel_id=1, source_target_pairs={{0,8},{2,10},{4,12},{6,14},{8,0},{10,2},{12,4},{14,6},{16,24},{18,... | collective-permute-start | bytes 884744 | tf_op jit(solution)/shard_map/ppermute | solution.py:1279
  131.0 16.1 %collective-permute-start.23 = (bf16[208,768]{1,0:T(8,128)(2,1)S(1)}, bf16[208,768]{1,0:T(8,128)(2,1)S(1)}, u32[]{:S(2)}, u32[]{:S(2)}) collective-permute-start(bf16[208,768]{1,0:T(8,128)(2,1)S(1)} %pad_maximum_fusion), channel_id=1, source_target_pairs={{0,4},{2,6},{4,0},{6,2},{8,12},{10,14},{12,8},{14,10},{16,20},{18,... | collective-permute-start | bytes 958472 | tf_op jit(solution)/shard_map/ppermute | solution.py:1279
  131.5 15.5 %collective-permute-start.24 = (bf16[192,768]{1,0:T(8,128)(2,1)S(1)}, bf16[192,768]{1,0:T(8,128)(2,1)S(1)}, u32[]{:S(2)}, u32[]{:S(2)}) collective-permute-start(bf16[192,768]{1,0:T(8,128)(2,1)S(1)} %bitcast.154), channel_id=1, source_target_pairs={{0,8},{2,10},{4,12},{6,14},{8,0},{10,2},{12,4},{14,6},{16,24},{18,... | collective-permute-start | bytes 884744 | tf_op jit(solution)/shard_map/ppermute | solution.py:1279
  147.4 23.1 %collective-permute-start.28 = (bf16[96,1536]{1,0:T(8,128)(2,1)S(1)}, bf16[96,1536]{1,0:T(8,128)(2,1)S(1)}, u32[]{:S(2)}, u32[]{:S(2)}) collective-permute-start(bf16[96,1536]{1,0:T(8,128)(2,1)S(1)} %pad_maximum_fusion.1), channel_id=1, source_target_pairs={{0,16},{2,18},{4,20},{6,22},{8,24},{10,26},{12,28},{14,30},{16,0},... | collective-permute-start | bytes 884744 | tf_op jit(solution)/shard_map/ppermute | solution.py:1279
  150.1 12.3 %collective-permute-start.25 = (bf16[112,768]{1,0:T(8,128)(2,1)S(1)}, bf16[112,768]{1,0:T(8,128)(2,1)S(1)}, u32[]{:S(2)}, u32[]{:S(2)}) collective-permute-start(bf16[112,768]{1,0:T(8,128)(2,1)S(1)} %pad_maximum_fusion.3), channel_id=1, source_target_pairs={{0,8},{2,10},{4,12},{6,14},{8,0},{10,2},{12,4},{14,6},{16,24},{18,... | collective-permute-start | bytes 516104 | tf_op jit(solution)/shard_map/ppermute | solution.py:1279
  151.1 11.2 %collective-permute-start.26 = (bf16[96,768]{1,0:T(8,128)(2,1)S(1)}, bf16[96,768]{1,0:T(8,128)(2,1)S(1)}, u32[]{:S(2)}, u32[]{:S(2)}) collective-permute-start(bf16[96,768]{1,0:T(8,128)(2,1)S(1)} %bitcast.164), channel_id=1, source_target_pairs={{0,4},{2,6},{4,0},{6,2},{8,12},{10,14},{12,8},{14,10},{16,20},{18,... | collective-permute-start | bytes 442376 | tf_op jit(solution)/shard_map/ppermute | solution.py:1279
  162.5 9.7 %collective-permute-start.27 = (bf16[112,768]{1,0:T(8,128)(2,1)S(1)}, bf16[112,768]{1,0:T(8,128)(2,1)S(1)}, u32[]{:S(2)}, u32[]{:S(2)}) collective-permute-start(bf16[112,768]{1,0:T(8,128)(2,1)S(1)} %pad_maximum_fusion.4), channel_id=1, source_target_pairs={{0,16},{2,18},{4,20},{6,22},{8,24},{10,26},{12,28},{14,30},{16,0},... | collective-permute-start | bytes 516104 | tf_op jit(solution)/shard_map/ppermute | solution.py:1279
  (11 other events, 39.7 us)

commit v2 on v1

--- a/solution.py
+++ b/solution.py
@@ -60,6 +60,7 @@
 
 SMEM = pl.BlockSpec(memory_space=pltpu.SMEM)
 HBM = pl.BlockSpec(memory_space=pl.ANY)
+LOOSE = pl.BlockSpec(memory_space=pl.ANY)
 KEPT = pl.BlockSpec(memory_space=pltpu.VMEM)
 
 
@@ -68,7 +69,7 @@
     for array, spec in ins:
         if spec is KEPT:
             array = pltpu.with_memory_space_constraint(array, pltpu.VMEM)
-        elif spec is not SMEM:
+        elif spec is not SMEM and spec is not LOOSE:
             array = pltpu.with_memory_space_constraint(array, pltpu.HBM)
         args.append(array)
     moved = sum(a.size * a.dtype.itemsize for a, spec in ins if spec is not KEPT)
@@ -159,9 +160,8 @@
 
 
 def halves(value_ref, side, block, kept_ref, sent_ref):
-    @pl.loop(0, value_ref.shape[0] // (2 * block))
-    def _(index):
-        rows = pl.ds(pl.multiple_of(index * block, 16), block)
+    for index in range(value_ref.shape[0] // (2 * block)):
+        rows = slice(index * block, (index + 1) * block)
         first = 2 * block * index
         here = pl.ds(pl.multiple_of(first + block * side, 16), block)
         there = pl.ds(pl.multiple_of(first + block * (1 - side), 16), block)
@@ -581,7 +581,8 @@
     dma = pltpu.SemaphoreType.DMA
     ins = [(bits, SMEM), (length, SMEM)]
     ins += [(value, whole(value.shape)) for value in (other_vec, vec)]
-    ins += [(value, HBM) for value in (a_low, x, ctx, proj, *pieces, *proj_pieces)]
+    ins += [(value, HBM) for value in (a_low, x, ctx, proj)]
+    ins += [(value, LOOSE) for value in (*pieces, *proj_pieces)]
     return call(
         forward_other_kernel,
         "attention_forward_other",
@@ -618,8 +619,7 @@
     )
 
 
-def mlp_step(c_ref, g_ref, fc, ow, bias):
-    hidden = dot(c_ref[...], fc) + bias
+def mlp_step(hidden, g_ref, ow):
     square = hidden * hidden
     tanh = jnp.tanh(hidden * (GELU + GELU * CUBIC * square))
     share = 0.5 + 0.5 * tanh
@@ -653,27 +653,35 @@
     fc_sent_ref,
     out_sent_ref,
     db_ref,
+    c_out,
+    g_out,
     gc_ref,
     gc_low_ref,
     bias_ref,
     gh_ref,
     dw_ref,
-    sem,
+    sems,
 ):
+    saved = [
+        pltpu.make_async_copy(c_ref, c_out, sems.at[1]),
+        pltpu.make_async_copy(g_ref, g_out, sems.at[2]),
+    ]
     step = pl.program_id(0)
 
     @pl.when(step == 0)
     def _():
+        start_all(saved)
         unit_bias(vec_ref, BIAS_FC, bias_ref)
         clear(gc_ref)
 
     lanes = pl.ds(pl.multiple_of(step * HIDDEN, HIDDEN), HIDDEN)
-    act, gh = mlp_step(c_ref, g_ref, fc_ref[...], ow_ref[...], bias_ref[:, lanes])
+    hidden = dot(c_ref[...], fc_ref[...]) + bias_ref[:, lanes]
+    act, gh = mlp_step(hidden, g_ref, ow_ref[...])
     act_ref[...] = act
     gh_ref[...] = gh
     db_ref[...] = jnp.sum(gh.astype(F32), 0, keepdims=True)
     gc_ref[...] += dot_nt(gh, fc_ref[...])
-    results = [pltpu.make_async_copy(gc_low_ref, gc_out, sem)]
+    results = [pltpu.make_async_copy(gc_low_ref, gc_out, sems.at[0])]
 
     @pl.when(step == steps - 1)
     def _():
@@ -687,7 +695,7 @@
 
     @pl.when(step == steps - 1)
     def _():
-        wait_all(results)
+        wait_all(results + saved)
 
 
 def feed_forward_own(bits, block, c_low, grad_mlp, c_turned, grad_turned, vec, fc, ow):
@@ -709,14 +717,15 @@
         [((slots, model), BF, HBM), ((slots, units), BF, column_tile(slots, HIDDEN))]
         + [((model // 2, units), BF, half)] * 2
         + [((model // 2, units), BF, KEPT)] * 2
-        + [((1, units), F32, column_tile(1, HIDDEN))],
+        + [((1, units), F32, column_tile(1, HIDDEN))]
+        + [((slots, model), BF, HBM)] * 2,
         [
             pltpu.VMEM((slots, model), F32),
             pltpu.VMEM((slots, model), BF),
             pltpu.VMEM((1, units), F32),
             pltpu.VMEM((slots, HIDDEN), BF),
             pltpu.VMEM((2, model, HIDDEN), BF),
-            pltpu.SemaphoreType.DMA,
+            pltpu.SemaphoreType.DMA((3,)),
         ],
         10 * slots * model * units,
         19,
@@ -727,8 +736,8 @@
     steps,
     bits_ref,
     length_ref,
-    c_ref,
-    g_ref,
+    c_hbm,
+    g_hbm,
     other_vec_ref,
     vec_ref,
     gc0_hbm,
@@ -741,13 +750,15 @@
 ):
     fc_pieces, out_pieces, proj_pieces, rest = rest[:4], rest[4:8], rest[8:10], rest[10:]
     do0_ref, fc_kept_ref, out_kept_ref, sums_ref, act_ref, gmid_out, ga_out, do1_out, *rest = rest
-    gc_ref, bias_ref, fc_ref, ow_ref, *rest = rest
+    gc_ref, bias_ref, fc_ref, ow_ref, c_ref, g_ref, *rest = rest
     late_refs, (gmid_ref, ga_ref, low_ref, do1_ref, proj1_ref, *rest) = rest[:4], rest[4:]
     sems, late_sems, proj_sems, out_sems = rest
     step = pl.program_id(0)
     slots, model = c_ref.shape
-    copies = fetch_rows(fc_pieces, bits_ref[1], fc_ref, sems.at[0])
-    copies += fetch_rows(out_pieces, bits_ref[4], ow_ref, sems.at[1])
+    first = fetch_rows(fc_pieces, bits_ref[1], fc_ref, sems.at[0])
+    first += [pltpu.make_async_copy(c_hbm, c_ref, sems.at[2, 0])]
+    second = fetch_rows(out_pieces, bits_ref[4], ow_ref, sems.at[1])
+    second += [pltpu.make_async_copy(g_hbm, g_ref, sems.at[2, 1])]
     late = [
         pltpu.make_async_copy(source, target, late_sems.at[index])
         for index, (source, target) in enumerate(
@@ -763,14 +774,15 @@
 
     @pl.when(step == 0)
     def _():
-        start_all(copies)
+        start_all(first + second)
         unit_bias(other_vec_ref, 1, bias_ref)
         clear(gc_ref)
-        wait_all(copies)
+        wait_all(first + second)
         start_all(late)
 
     lanes = pl.ds(pl.multiple_of(step * HIDDEN, HIDDEN), HIDDEN)
-    act, gh = mlp_step(c_ref, g_ref, fc_ref[:, lanes], ow_ref[lanes, :], bias_ref[:, lanes])
+    hidden = dot(c_ref[...], fc_ref[:, lanes]) + bias_ref[:, lanes]
+    act, gh = mlp_step(hidden, g_ref, ow_ref[lanes, :])
     act_ref[...] = act
     gc_ref[...] += dot_nt(gh, fc_ref[:, lanes])
 
@@ -831,7 +843,7 @@
         functools.partial(mlp_other_kernel, steps),
         "feed_forward_other",
         steps,
-        [(bits, SMEM), (length, SMEM), (c_low, KEPT), (grad_mlp, KEPT)]
+        [(bits, SMEM), (length, SMEM), (c_low, HBM), (grad_mlp, HBM)]
         + [(value, whole(value.shape)) for value in (other_vec, vec)]
         + [(value, HBM) for value in (grad_c, middle, cot, proj, *kept, *fc, *ow, *proj_pieces)],
         [
@@ -849,6 +861,8 @@
             pltpu.VMEM((model, units), BF),
             pltpu.VMEM((units, model), BF),
             pltpu.VMEM((slots, model), BF),
+            pltpu.VMEM((slots, model), BF),
+            pltpu.VMEM((slots, model), BF),
             pltpu.VMEM((slots, model), F32),
             pltpu.VMEM((slots, model), BF),
             pltpu.VMEM((width, model), BF),
@@ -857,13 +871,13 @@
             pltpu.VMEM((TILE, model), BF),
             pltpu.VMEM((slots, width), BF),
             pltpu.VMEM((width, model), BF),
-            dma((2, 4)),
+            dma((3, 4)),
             dma((6,)),
             dma((2,)),
             dma((3, tokens)),
         ],
         6 * slots * model * units + 4 * slots * model * width,
-        31,
+        34,
     )
 
 
@@ -1002,11 +1016,11 @@
 
 
 def backward_other_kernel(
-    bits_ref, length_ref, lse_ref, qkv_hbm, ctxt_hbm, do_hbm, d0_hbm, w_hbm, ow_hbm, *rest
+    bits_ref, length_ref, lse_ref, qkv_hbm, ctxt_hbm, do_hbm, d0_hbm, w_hbm, ow_hbm, act0_hbm, act1_hbm, *rest
 ):
     pieces, out_pieces, rest = rest[:4], rest[4:8], rest[8:]
-    both_ref, weight_ref, ow_ref, qkv_ref, ctxt_ref, do_ref, *rest = rest
-    scratch, (sems, late_sem, w_sems, ow_sems) = rest[:14], rest[14:]
+    both_ref, weight_ref, ow_ref, act_ref, qkv_ref, ctxt_ref, do_ref, *rest = rest
+    scratch, (sems, late_sem, w_sems, ow_sems, act_sems) = rest[:14], rest[14:]
     width = do_ref.shape[1]
     sources = lambda pair: pair_sources(
         pair, width, (qkv_hbm, qkv_ref), (ctxt_hbm, ctxt_ref), (do_hbm, do_ref), sems
@@ -1021,8 +1035,10 @@
     units = ow_hbm.shape[0]
     rows = pl.ds(pl.multiple_of(bits_ref[3] * units, 128), units)
     late += fetch_rows([ow_hbm], 0, ow_ref.at[rows, :], ow_sems.at[0])
+    late += [pltpu.make_async_copy(act0_hbm, act_ref.at[:, rows], act_sems.at[0])]
     rows = pl.ds(pl.multiple_of((1 - bits_ref[3]) * units, 128), units)
     late += fetch_rows(out_pieces, bits_ref[4], ow_ref.at[rows, :], ow_sems.at[1])
+    late += [pltpu.make_async_copy(act1_hbm, act_ref.at[:, rows], act_sems.at[1])]
     start_all(late)
     d_ref = both_ref.at[:, other]
     backward_pairs(length_ref[0], qkv_ref, do_ref, ctxt_ref, lse_ref, d_ref, scratch, sources)
@@ -1132,12 +1148,15 @@
     ]
 
 
-def attention_backward_other(bits, length, lse, qkv, ctxt, do, d0, weight, ow, pieces, out_pieces):
+def attention_backward_other(
+    bits, length, lse, qkv, ctxt, do, d0, weight, ow, act0, act1, pieces, out_pieces
+):
     slots, width = do.shape
     model = weight.shape[1]
     dma = pltpu.SemaphoreType.DMA
     ins = [(bits, SMEM), (length, SMEM), (lse, whole(lse.shape))]
-    ins += [(value, HBM) for value in (qkv, ctxt, do, d0, weight, ow, *pieces, *out_pieces)]
+    ins += [(value, HBM) for value in (qkv, ctxt, do, d0, weight, ow, act0, act1)]
+    ins += [(value, HBM) for value in (*pieces, *out_pieces)]
     return call(
         backward_other_kernel,
         "attention_backward_other",
@@ -1147,6 +1166,7 @@
             ((slots, 6 * width), BF, KEPT),
             ((model, 6 * width), BF, KEPT),
             ((2 * ow.shape[0], model), BF, KEPT),
+            ((slots, 2 * ow.shape[0]), BF, KEPT),
         ],
         [
             pltpu.VMEM((slots, 3 * width), BF),
@@ -1157,6 +1177,7 @@
             dma,
             dma((2, 12)),
             dma((2, 4)),
+            dma((2,)),
         ],
         9 * slots * slots * width,
         12,
@@ -1198,23 +1219,12 @@
     )
 
 
-def final_kernel(
-    bits_ref, vec_ref, d_ref, w_ref, x_hbm, gmid_hbm, act0_hbm, act1_hbm, *rest
-):
-    gin_out, act_ref, x_ref, gmid_ref, gin_ref, product_ref, *rest = rest
-    x_sems, gmid_sems, gin_sems, act_sems = rest
+def final_kernel(vec_ref, d_ref, w_ref, x_hbm, gmid_hbm, gin_out, *rest):
+    x_ref, gmid_ref, gin_ref, product_ref, x_sems, gmid_sems, gin_sems = rest
     x_in = tiles(x_hbm, x_ref, x_sems)
     gmid_in = tiles(gmid_hbm, gmid_ref, gmid_sems)
     gin_tiles = tiles(gin_ref, gin_out, gin_sems)
     start_all(x_in + gmid_in)
-    units = act0_hbm.shape[1]
-    own = pl.ds(pl.multiple_of(bits_ref[3] * units, 128), units)
-    other = pl.ds(pl.multiple_of((1 - bits_ref[3]) * units, 128), units)
-    late = [
-        pltpu.make_async_copy(act0_hbm, act_ref.at[:, own], act_sems.at[0]),
-        pltpu.make_async_copy(act1_hbm, act_ref.at[:, other], act_sems.at[1]),
-    ]
-    start_all(late)
     count = len(x_in)
 
     def product(index):
@@ -1237,24 +1247,19 @@
 
     norm(count - 1)
     gin_tiles[-1].start()
-    wait_all(late + gin_tiles)
-
-
-def gradient_of_input(bits, vec, both, weight, x, gmid, act0, act1):
+    wait_all(gin_tiles)
+
+
+def gradient_of_input(vec, both, weight, x, gmid):
     slots, model = x.shape
-    units = act0.shape[1]
     tokens = slots // TILE
     dma = pltpu.SemaphoreType.DMA
     return call(
         final_kernel,
         "final",
         1,
-        [(bits, SMEM), (vec, whole(vec.shape)), (both, KEPT), (weight, KEPT)]
-        + [(value, HBM) for value in (x, gmid, act0, act1)],
-        [
-            ((slots, model), F32, HBM),
-            ((slots, 2 * units), BF, KEPT),
-        ],
+        [(vec, whole(vec.shape)), (both, KEPT), (weight, KEPT), (x, HBM), (gmid, HBM)],
+        [((slots, model), F32, HBM)],
         [
             pltpu.VMEM((slots, model), BF),
             pltpu.VMEM((slots, model), F32),
@@ -1263,11 +1268,10 @@
             dma((tokens,)),
             dma((tokens,)),
             dma((tokens,)),
-            dma((2,)),
         ],
         2 * slots * model * both.shape[1],
         13,
-    )
+    )[0]
 
 
 def across(value):
@@ -1385,11 +1389,11 @@
         out_weight,
     )
 
-    qkv_mine, qkv0, proj_send, fc_send = tie(qkv_mine, qkv0, proj_send, fc_send)
+    fc_mine = across(fc_send)
+    proj_got = across(proj_send)
+    qkv_mine, qkv0 = tie(qkv_mine, qkv0)
     qkv_side = swap(qkv_mine, 2)
     qkv_core = swap(qkv_mine, 1)
-    proj_got = across(proj_send)
-    fc_mine = across(fc_send)
     lse0, ctx0, ctxt0, qkv0 = attention_forward_own(length, qkv0)
 
     qkv_side, qkv_core, proj_got, ctx0, out_send = tie(
@@ -1419,7 +1423,7 @@
     fc_core = swap(fc_mine, 1)
     out_side = swap(out_mine, 4)
     out_core = swap(out_mine, 1)
-    gc0, act0, fc_kept, out_kept, fc_sent, out_sent, grad_fc_bias = feed_forward_own(
+    gc0, act0, fc_kept, out_kept, fc_sent, out_sent, grad_fc_bias, c_low, grad_mlp = feed_forward_own(
         bits, block, c_low, grad_mlp, c_turned, grad_mlp_turned, vec, fc_weight, out_weight
     )
 
@@ -1496,8 +1500,20 @@
     first_sent, second_sent, qkv1 = tie(first_sent, second_sent, qkv1)
     first_got = swap(first_sent, 1 << first_sum.bit)
     second_got = swap(second_sent, 1 << second_sum.bit)
-    both, weights, ow = attention_backward_other(
-        bits, length, lse1, qkv1, ctxt1, do1, d0, qkv_weight, out_weight, qkv_other, out_other
+    both, weights, ow, act = attention_backward_other(
+        bits,
+        length,
+        lse1,
+        qkv1,
+        ctxt1,
+        do1,
+        d0,
+        qkv_weight,
+        out_weight,
+        act0,
+        act1,
+        qkv_other,
+        out_other,
     )
 
     both, fc_got, out_got, first_got, second_got = tie(both, fc_got, out_got, first_got, second_got)
@@ -1511,9 +1527,7 @@
     first_got = swap(first_sent, 1 << first_sum.bit)
     second_got = swap(second_sent, 1 << second_sum.bit)
     rest_got = swap(rest_sent, 1 << fc_sum.bit)
-    grad_input, act = gradient_of_input(
-        bits, vec, both, weights, block_input, grad_middle, act0, act1
-    )
+    grad_input = gradient_of_input(vec, both, weights, block_input, grad_middle)
 
     grad_input, first_got, second_got, act = tie(grad_input, first_got, second_got, act)
     for level in range(3, levels):

time: 176 us -> 173 us (0.983)
  local copies, waits for them, and re-layouts: 9.6 us -> 6.42 us
  Pallas kernels: 122 us -> 120 us
  waiting for transfers between devices: 10.7 us -> 12.6 us
    unnamed x28 -> x24, local copies, waits for them, and re-layouts: 3.36 us -> 0.17 us
    pallas_call x9, Pallas kernels: 122 us -> 120 us  [call(): pl.pallas_call(body, name=name, grid=(steps,), out_shape=tuple(((pltpu.VM...]
  transfers between devices with their start and end apart: 29 -> 29, of which waited for: 7 -> 8; matrix products, arithmetic and copies ran while one was open for 2% -> 2% of each run, Pallas kernels for 69% -> 70%
where the time goes in v2:
time: 173 us; the launch traced here: 172 us
  Pallas kernels  120 us (69%)
  starting transfers between devices  25.3 us (15%)
  waiting for transfers between devices  12.6 us (7%)
  local copies, waits for them, and re-layouts  6.42 us (4%)
  other arithmetic  6.14 us (4%)
  between operations  1.88 us (1%)
    pallas_call x9, Pallas kernels, call(): pl.pallas_call(body, name=name, grid=(steps,), out_shape=tuple(((pltpu.VM...  120 us
    ppermute x24, starting transfers between devices, swap(): return lax.ppermute(value, 'dp', [(i, i ^ bit) for i in range(count)])  17.2 us
    ppermute x5, waiting for transfers between devices, across(): return lax.ppermute(value, 'tensor', [(0, 1), (1, 0)])  8.16 us
    ppermute x5, starting transfers between devices, across(): return lax.ppermute(value, 'tensor', [(0, 1), (1, 0)])  8.08 us
    ppermute x24, waiting for transfers between devices, swap(): return lax.ppermute(value, 'dp', [(i, i ^ bit) for i in range(count)])  4.42 us
    convert_element_type x16, other arithmetic, part(): return total.astype(BF)  3.63 us
  transfers between devices with their start and end apart: 29, of which 8 were waited for; matrix products, arithmetic and copies ran while one was open for 2% of the time, Pallas kernels for 70%

profile of v2, /device:TPU:0, one launch (start us, length us, event | category | flops | bytes accessed | tf_op | source)
XLA Modules:
  0.0 172.1 jit_solution(12043474589490607059)
XLA Ops:
  0.6 1.1 dynamic-slice_bitcast_fusion
  1.7 3.0 %collective-permute-start = (bf16[3,192,384]{2,1,0:T(8,128)(2,1)S(1)}, bf16[3,192,384]{2,1,0:T(8,128)(2,1)S(1)}, u32[]{:S(2)}, u32[]{:S(2)}) collective-permute-start(bf16[3,192,384]{2,1,0:T(8,128)(2,1)S(1)} %dynamic-slice_bitcast_fusion), channel_id=1, source_target_pairs={{0,1},{1,0},{2,3},{3,2},{4,5},{5,4},{6,7},{7,6},{8,9},{9,8},{10,11... | collective-permute-start | bytes 1327112 | tf_op jit(solution)/shard_map/ppermute | solution.py:1278
  5.5 8.3 %project_own.1 = (f32[16,768]{1,0:T(8,128)}, bf16[1024,1152]{1,0:T(8,128)(2,1)S(1)}, bf16[1024,768]{1,0:T(8,128)(2,1)S(1)}, bf16[768,1024]{1,0:T(8,128)(2,1)S(1)...) custom-call(s32[5]{0:T(128)S(1)} %stack.35.bits_ref, ...), custom_call_target="tpu_custom_call" | custom-call | flops 1811939328 | bytes 14972952 | tf_op jit(solution)/shard_map/project_own/pallas_call | solution.py:81
  13.8 1.1 collective-permute-done.rest_0_
  14.9 1.8 %collective-permute-start.1 = (bf16[3,192,384]{2,1,0:T(8,128)(2,1)S(1)}, bf16[3,192,384]{2,1,0:T(8,128)(2,1)S(1)}, u32[]{:S(2)}, u32[]{:S(2)}) collective-permute-start(bf16[3,192,384]{2,1,0:T(8,128)(2,1)S(1)} %collective-permute-done.rest_0_), channel_id=1, source_target_pairs={{0,4},{2,6},{4,0},{6,2},{8,12},{10,14},{12,8},{14,10},{16,20},{18,... | collective-permute-start | bytes 1327112 | tf_op jit(solution)/shard_map/ppermute | solution.py:1283
  16.7 1.5 collective-permute-start.3
  18.7 8.4 %attention_forward_own.1 = (f32[6,1024]{1,0:T(8,128)}, bf16[1024,384]{1,0:T(8,128)(2,1)}, f32[384,1024]{1,0:T(8,128)}, bf16[1024,1152]{1,0:T(8,128)(2,1)}) custom-call(s32[1]{0:T(128)S(6)} %copy.59.length_ref, bf16[1024,1152]{1,0:T(8,128)(2,1)S(1)} %get-tuple-element.106.qkv_ref), custom_call_target="tpu_custom_call" | custom-call | flops 2415919104 | bytes 4743172 | tf_op jit(solution)/shard_map/attention_forward_own/pallas_call | solution.py:81
  28.4 1.5 collective-permute-start.7
  30.5 17.0 %attention_forward_other.1 = (f32[6,1024]{1,0:T(8,128)}, bf16[1024,768]{1,0:T(8,128)(2,1)S(1)}, bf16[768,1024]{1,0:T(8,128)(2,1)S(1)}, f32[1024,768]{1,0:T(8,128...) custom-call(s32[5]{0:T(128)S(1)} %stack.35.bits_ref, s32[1]{0:T(128)S(6)} %copy.59.length_ref, ...), custom_call_target="tpu_custom_call" | custom-call | flops 5435817984 | bytes 14155800 | tf_op jit(solution)/shard_map/attention_forward_other/pallas_call | solution.py:81
  47.6 4.8 %collective-permute-done.7.rest_4_ = bf16[384,768]{1,0:T(8,128)(2,1)S(1)} collective-permute-done((bf16[384,768]{1,0:T(8,128)(2,1)S(1)}, bf16[384,768]{1,0:T(8,128)(2,1)S(1)}, u32[]{:S(2)}, u32[]{:S(2)}) %collective-permute-start.7) | collective-permute-done | bytes 589856 | tf_op jit(solution)/shard_map/ppermute | solution.py:1278
  52.9 1.8 %collective-permute-start.10 = (bf16[384,768]{1,0:T(8,128)(2,1)S(1)}, bf16[384,768]{1,0:T(8,128)(2,1)S(1)}, u32[]{:S(2)}, u32[]{:S(2)}) collective-permute-start(bf16[384,768]{1,0:T(8,128)(2,1)S(1)} %collective-permute-done.7.rest_4_), channel_id=1, source_target_pairs={{0,8},{2,10},{4,12},{6,14},{8,0},{10,2},{12,4},{14,6},{16,24},{18,... | collective-permute-start | bytes 1769480 | tf_op jit(solution)/shard_map/ppermute | solution.py:1283
  54.7 17.8 %feed_forward_own.1 = (bf16[1024,768]{1,0:T(8,128)(2,1)}, bf16[1024,1536]{1,0:T(8,128)(2,1)}, bf16[384,1536]{1,0:T(8,128)(2,1)}, bf16[384,1536]{1,0:T(8,128)(2,1...) custom-call(s32[5]{0:T(128)S(1)} %stack.35.bits_ref, ...), custom_call_target="tpu_custom_call" | custom-call | flops 12079595520 | bytes 14997524 | tf_op jit(solution)/shard_map/feed_forward_own/pallas_call | solution.py:81
  73.6 1.4 collective-permute-done.12.rest_3_
  75.6 19.7 %feed_forward_other.1 = (bf16[1024,384]{1,0:T(8,128)(2,1)S(1)}, bf16[384,1536]{1,0:T(8,128)(2,1)S(1)}, bf16[384,1536]{1,0:T(8,128)(2,1)S(1)}, f32[3,768]{1,0:T(4...) custom-call(s32[5]{0:T(128)S(1)} %stack.35.bits_ref, ...), custom_call_target="tpu_custom_call" | custom-call | flops 8455716864 | bytes 26526744 | tf_op jit(solution)/shard_map/feed_forward_other/pallas_call | solution.py:81
  95.4 1.2 add_convert_fusion.3
  96.6 1.2 constant_dynamic-slice_fusion.4
  97.8 1.2 add_convert_fusion.2
  99.0 1.2 constant_dynamic-slice_fusion.2
  100.1 1.6 collective-permute-start.16
  102.5 18.1 %attention_backward_own.1 = (f32[8,768]{1,0:T(8,128)S(1)}, f32[16,768]{1,0:T(8,128)S(1)}, bf16[384,1536]{1,0:T(8,128)(2,1)S(1)}, bf16[384,1536]{1,0:T(8,128)(2,1)S(1)}, bf16[1024,1152]{1,0:T(8,128)(2,1)}) custom-call(s32[5]{0:T(128)S(1)} %stack.35.bits_ref, s32[1]{0:T(128)S(6)} %copy.59.length_ref, f32[6,1024]{1,0:T(8,128)} %get-tuple-element.107.lse_ref, ...), custom_call_target="tpu_custom_call" | custom-call | flops 6039797760 | bytes 11298840 | tf_op jit(solution)/shard_map/attention_backward_own/pallas_call | solution.py:81
  120.7 1.6 collective-permute-start.19
  123.0 1.6 collective-permute-done.19
  124.9 1.6 collective-permute-start.21
  127.0 1.0 collective-permute-start.24
  128.6 14.4 %attention_backward_other.1 = (bf16[1024,2304]{1,0:T(8,128)(2,1)S(1)}, bf16[768,2304]{1,0:T(8,128)(2,1)S(1)}, bf16[3072,768]{1,0:T(8,128)(2,1)S(1)}, bf16[1024,3072]{1,0:T(8,128)(2,1)S(1)}) custom-call(s32[5]{0:T(128)S(1)} %stack.35.bits_ref, s32[1]{0:T(128)S(6)} %copy.59.length_ref, f32[6,1024]{1,0:T(8,128)} %get-tuple-element.160.lse_ref, ...), custom_call_target="tpu_custom_call" | custom-call | flops 3623878656 | bytes 21651480 | tf_op jit(solution)/shard_map/attention_backward_other/pallas_call | solution.py:81
  143.4 1.6 collective-permute-start.26
  145.0 1.1 collective-permute-start.25
  146.1 2.6 %collective-permute-start.28 = (bf16[96,1536]{1,0:T(8,128)(2,1)S(1)}, bf16[96,1536]{1,0:T(8,128)(2,1)S(1)}, u32[]{:S(2)}, u32[]{:S(2)}) collective-permute-start(bf16[96,1536]{1,0:T(8,128)(2,1)S(1)} %pad_maximum_fusion.1), channel_id=1, source_target_pairs={{0,16},{2,18},{4,20},{6,22},{8,24},{10,26},{12,28},{14,30},{16,0},... | collective-permute-start | bytes 884744 | tf_op jit(solution)/shard_map/ppermute | solution.py:1283
  148.7 8.6 %final.1 = f32[1024,768]{1,0:T(8,128)} custom-call(f32[16,768]{1,0:T(8,128)} %get-tuple-element.104.vec_ref, bf16[1024,2304]{1,0:T(8,128)(2,1)S(1)} %get-tuple-element.180.d_ref, bf16[768,2304]{1,0:T(8,128)(2,1)S(1)} %get-tuple-element.181.w_ref, bf16[1024,768]{1,0:T(8,128)(2,1)} %x_hbm.5, f32[1024,768]{1,0:T(8,128)} %get-tuple-element.182.gmid_hbm), custom_call_target="tpu_custom_call" | custom-call | flops 3623878656 | bytes 7913472 | tf_op jit(solution)/shard_map/final/pallas_call | solution.py:81
  157.8 7.6 %output.1 = bf16[1024,768]{1,0:T(8,128)(2,1)} custom-call(f32[16,768]{1,0:T(8,128)} %get-tuple-element.104.vec_ref, bf16[1024,3072]{1,0:T(8,128)(2,1)S(1)} %get-tuple-element.189.act_ref, bf16[3072,768]{1,0:T(8,128)(2,1)S(1)} %get-tuple-element.190.ow_ref, f32[1024,768]{1,0:T(8,128)} %get-tuple-element.128.middle_hbm.middle_ref), custom_call_target="tpu_custom_call" | custom-call | flops 4831838208 | bytes 4767744 | tf_op jit(solution)/shard_map/output/pallas_call | solution.py:81
  165.4 1.1 collective-permute-done.28
  167.5 1.3 collective-permute-done.27
  (107 shorter events, 12.7 us)
Async XLA Ops:
  1.7 13.2 %collective-permute-start = (bf16[3,192,384]{2,1,0:T(8,128)(2,1)S(1)}, bf16[3,192,384]{2,1,0:T(8,128)(2,1)S(1)}, u32[]{:S(2)}, u32[]{:S(2)}) collective-permute-start(bf16[3,192,384]{2,1,0:T(8,128)(2,1)S(1)} %dynamic-slice_bitcast_fusion), channel_id=1, source_target_pairs={{0,1},{1,0},{2,3},{3,2},{4,5},{5,4},{6,7},{7,6},{8,9},{9,8},{10,11... | collective-permute-start | bytes 1327112 | tf_op jit(solution)/shard_map/ppermute | solution.py:1278
  14.9 12.9 %collective-permute-start.2 = (bf16[3,192,384]{2,1,0:T(8,128)(2,1)S(1)}, bf16[3,192,384]{2,1,0:T(8,128)(2,1)S(1)}, u32[]{:S(2)}, u32[]{:S(2)}) collective-permute-start(bf16[3,192,384]{2,1,0:T(8,128)(2,1)S(1)} %collective-permute-done.rest_0_), channel_id=1, source_target_pairs={{0,2},{2,0},{4,6},{6,4},{8,10},{10,8},{12,14},{14,12},{16,18},{18,... | collective-permute-start | bytes 1327112 | tf_op jit(solution)/shard_map/ppermute | solution.py:1283
  14.9 12.9 %collective-permute-start.1 = (bf16[3,192,384]{2,1,0:T(8,128)(2,1)S(1)}, bf16[3,192,384]{2,1,0:T(8,128)(2,1)S(1)}, u32[]{:S(2)}, u32[]{:S(2)}) collective-permute-start(bf16[3,192,384]{2,1,0:T(8,128)(2,1)S(1)} %collective-permute-done.rest_0_), channel_id=1, source_target_pairs={{0,4},{2,6},{4,0},{6,2},{8,12},{10,14},{12,8},{14,10},{16,20},{18,... | collective-permute-start | bytes 1327112 | tf_op jit(solution)/shard_map/ppermute | solution.py:1283
  16.7 11.1 %collective-permute-start.3 = (bf16[224,768]{1,0:T(8,128)(2,1)}, bf16[224,768]{1,0:T(8,128)(2,1)S(1)}, u32[]{:S(2)}, u32[]{:S(2)}) collective-permute-start(bf16[224,768]{1,0:T(8,128)(2,1)} %get-tuple-element.110), channel_id=1, source_target_pairs={{0,1},{1,0},{2,3},{3,2},{4,5},{5,4},{6,7},{7,6},{8,9},{9,8},{10,11... | collective-permute-start | bytes 1032200 | tf_op jit(solution)/shard_map/ppermute | solution.py:1278
  18.2 29.4 %collective-permute-start.6 = (bf16[192,1536]{1,0:T(8,128)(2,1)}, bf16[192,1536]{1,0:T(8,128)(2,1)S(1)}, u32[]{:S(2)}, u32[]{:S(2)}) collective-permute-start(bf16[192,1536]{1,0:T(8,128)(2,1)} %get-tuple-element.119), channel_id=1, source_target_pairs={{0,1},{1,0},{2,3},{3,2},{4,5},{5,4},{6,7},{7,6},{8,9},{9,8},{10,11... | collective-permute-start | bytes 1769480 | tf_op jit(solution)/shard_map/ppermute | solution.py:1278
  27.8 19.7 %copy-start.2 = (bf16[3,192,384]{2,1,0:T(8,128)(2,1)}, bf16[3,192,384]{2,1,0:T(8,128)(2,1)S(1)}, u32[]{:S(2)}) copy-start(bf16[3,192,384]{2,1,0:T(8,128)(2,1)S(1)} %collective-permute-done.1.rest_2_) | copy-start | bytes 1327108
  27.8 2.7 %collective-permute-start.5 = (bf16[224,768]{1,0:T(8,128)(2,1)S(1)}, bf16[224,768]{1,0:T(8,128)(2,1)S(1)}, u32[]{:S(2)}, u32[]{:S(2)}) collective-permute-start(bf16[224,768]{1,0:T(8,128)(2,1)S(1)} %collective-permute-done.3.rest_4_.rest_8_), channel_id=1, source_target_pairs={{0,2},{2,0},{4,6},{6,4},{8,10},{10,8},{12,14},{14,12},{16,18},{18,... | collective-permute-start | bytes 1032200 | tf_op jit(solution)/shard_map/ppermute | solution.py:1283
  27.9 2.6 %collective-permute-start.4 = (bf16[3,192,384]{2,1,0:T(8,128)(2,1)S(1)}, bf16[3,192,384]{2,1,0:T(8,128)(2,1)S(1)}, u32[]{:S(2)}, u32[]{:S(2)}) collective-permute-start(bf16[3,192,384]{2,1,0:T(8,128)(2,1)S(1)} %collective-permute-done.1.rest_2_), channel_id=1, source_target_pairs={{0,2},{2,0},{4,6},{6,4},{8,10},{10,8},{12,14},{14,12},{16,18},{18,... | collective-permute-start | bytes 1327112 | tf_op jit(solution)/shard_map/ppermute | solution.py:1283
  28.4 24.0 %collective-permute-start.7 = (bf16[384,768]{1,0:T(8,128)(2,1)S(1)}, bf16[384,768]{1,0:T(8,128)(2,1)S(1)}, u32[]{:S(2)}, u32[]{:S(2)}) collective-permute-start(bf16[384,768]{1,0:T(8,128)(2,1)S(1)} %copy-done.11), channel_id=1, source_target_pairs={{0,1},{1,0},{2,3},{3,2},{4,5},{5,4},{6,7},{7,6},{8,9},{9,8},{10,11... | collective-permute-start | bytes 1769480 | tf_op jit(solution)/shard_map/ppermute | solution.py:1278
  47.5 24.9 %copy-start.9 = (bf16[192,1536]{1,0:T(8,128)(2,1)}, bf16[192,1536]{1,0:T(8,128)(2,1)S(1)}, u32[]{:S(2)}) copy-start(bf16[192,1536]{1,0:T(8,128)(2,1)S(1)} %collective-permute-done.6.rest_0_) | copy-start | bytes 1769476
  52.3 20.1 %copy-start.6 = (bf16[384,768]{1,0:T(8,128)(2,1)}, bf16[384,768]{1,0:T(8,128)(2,1)S(1)}, u32[]{:S(2)}) copy-start(bf16[384,768]{1,0:T(8,128)(2,1)S(1)} %collective-permute-done.7.rest_4_) | copy-start | bytes 1769476
  52.4 20.1 %collective-permute-start.9 = (bf16[192,1536]{1,0:T(8,128)(2,1)S(1)}, bf16[192,1536]{1,0:T(8,128)(2,1)S(1)}, u32[]{:S(2)}, u32[]{:S(2)}) collective-permute-start(bf16[192,1536]{1,0:T(8,128)(2,1)S(1)} %collective-permute-done.6.rest_0_), channel_id=1, source_target_pairs={{0,2},{2,0},{4,6},{6,4},{8,10},{10,8},{12,14},{14,12},{16,18},{18,... | collective-permute-start | bytes 1769480 | tf_op jit(solution)/shard_map/ppermute | solution.py:1283
  52.4 20.2 %collective-permute-start.8 = (bf16[192,1536]{1,0:T(8,128)(2,1)S(1)}, bf16[192,1536]{1,0:T(8,128)(2,1)}, u32[]{:S(2)}, u32[]{:S(2)}) collective-permute-start(bf16[192,1536]{1,0:T(8,128)(2,1)S(1)} %collective-permute-done.6.rest_0_), channel_id=1, source_target_pairs={{0,4},{2,6},{4,0},{6,2},{8,12},{10,14},{12,8},{14,10},{16,20},{18,... | collective-permute-start | bytes 1769480 | tf_op jit(solution)/shard_map/ppermute | solution.py:1283
  52.6 19.9 %collective-permute-start.11 = (bf16[384,768]{1,0:T(8,128)(2,1)S(1)}, bf16[384,768]{1,0:T(8,128)(2,1)S(1)}, u32[]{:S(2)}, u32[]{:S(2)}) collective-permute-start(bf16[384,768]{1,0:T(8,128)(2,1)S(1)} %collective-permute-done.7.rest_4_), channel_id=1, source_target_pairs={{0,2},{2,0},{4,6},{6,4},{8,10},{10,8},{12,14},{14,12},{16,18},{18,... | collective-permute-start | bytes 1769480 | tf_op jit(solution)/shard_map/ppermute | solution.py:1283
  52.9 19.7 %collective-permute-start.10 = (bf16[384,768]{1,0:T(8,128)(2,1)S(1)}, bf16[384,768]{1,0:T(8,128)(2,1)S(1)}, u32[]{:S(2)}, u32[]{:S(2)}) collective-permute-start(bf16[384,768]{1,0:T(8,128)(2,1)S(1)} %collective-permute-done.7.rest_4_), channel_id=1, source_target_pairs={{0,8},{2,10},{4,12},{6,14},{8,0},{10,2},{12,4},{14,6},{16,24},{18,... | collective-permute-start | bytes 1769480 | tf_op jit(solution)/shard_map/ppermute | solution.py:1283
  72.6 2.5 %collective-permute-start.12 = (bf16[192,1536]{1,0:T(8,128)(2,1)}, bf16[192,1536]{1,0:T(8,128)(2,1)}, u32[]{:S(2)}, u32[]{:S(2)}) collective-permute-start(bf16[192,1536]{1,0:T(8,128)(2,1)} %collective-permute-done.8.rest_2_), channel_id=1, source_target_pairs={{0,2},{2,0},{4,6},{6,4},{8,10},{10,8},{12,14},{14,12},{16,18},{18,... | collective-permute-start | bytes 1769480 | tf_op jit(solution)/shard_map/ppermute | solution.py:1283
  72.6 3.0 %collective-permute-start.13 = (bf16[384,768]{1,0:T(8,128)(2,1)S(1)}, bf16[384,768]{1,0:T(8,128)(2,1)}, u32[]{:S(2)}, u32[]{:S(2)}) collective-permute-start(bf16[384,768]{1,0:T(8,128)(2,1)S(1)} %collective-permute-done.10.rest_6_), channel_id=1, source_target_pairs={{0,2},{2,0},{4,6},{6,4},{8,10},{10,8},{12,14},{14,12},{16,18},{18,... | collective-permute-start | bytes 1769480 | tf_op jit(solution)/shard_map/ppermute | solution.py:1283
  73.1 22.2 %collective-permute-start.14 = (bf16[384,1536]{1,0:T(8,128)(2,1)S(1)}, bf16[384,1536]{1,0:T(8,128)(2,1)}, u32[]{:S(2)}, u32[]{:S(2)}) collective-permute-start(bf16[384,1536]{1,0:T(8,128)(2,1)S(1)} %get-tuple-element.142), channel_id=1, source_target_pairs={{0,2},{2,0},{4,6},{6,4},{8,10},{10,8},{12,14},{14,12},{16,18},{18,... | collective-permute-start | bytes 3538952 | tf_op jit(solution)/shard_map/ppermute | solution.py:1283
  73.3 22.0 %collective-permute-start.15 = (bf16[384,1536]{1,0:T(8,128)(2,1)S(1)}, bf16[384,1536]{1,0:T(8,128)(2,1)}, u32[]{:S(2)}, u32[]{:S(2)}) collective-permute-start(bf16[384,1536]{1,0:T(8,128)(2,1)S(1)} %get-tuple-element.143), channel_id=1, source_target_pairs={{0,2},{2,0},{4,6},{6,4},{8,10},{10,8},{12,14},{14,12},{16,18},{18,... | collective-permute-start | bytes 3538952 | tf_op jit(solution)/shard_map/ppermute | solution.py:1283
  100.1 20.4 %collective-permute-start.16 = (bf16[192,1536]{1,0:T(8,128)(2,1)S(1)}, bf16[192,1536]{1,0:T(8,128)(2,1)S(1)}, u32[]{:S(2)}, u32[]{:S(2)}) collective-permute-start(bf16[192,1536]{1,0:T(8,128)(2,1)S(1)} %bitcast.151), channel_id=1, source_target_pairs={{0,4},{2,6},{4,0},{6,2},{8,12},{10,14},{12,8},{14,10},{16,20},{18,... | collective-permute-start | bytes 1769480 | tf_op jit(solution)/shard_map/ppermute | solution.py:1283
  101.7 18.8 %collective-permute-start.17 = (bf16[192,1536]{1,0:T(8,128)(2,1)S(1)}, bf16[192,1536]{1,0:T(8,128)(2,1)S(1)}, u32[]{:S(2)}, u32[]{:S(2)}) collective-permute-start(bf16[192,1536]{1,0:T(8,128)(2,1)S(1)} %bitcast.152), channel_id=1, source_target_pairs={{0,8},{2,10},{4,12},{6,14},{8,0},{10,2},{12,4},{14,6},{16,24},{18,... | collective-permute-start | bytes 1769480 | tf_op jit(solution)/shard_map/ppermute | solution.py:1283
  120.5 6.0 %collective-permute-start.18 = (bf16[384,1536]{1,0:T(8,128)(2,1)S(1)}, bf16[384,1536]{1,0:T(8,128)(2,1)S(1)}, u32[]{:S(2)}, u32[]{:S(2)}) collective-permute-start(bf16[384,1536]{1,0:T(8,128)(2,1)S(1)} %get-tuple-element.159), channel_id=1, source_target_pairs={{0,2},{2,0},{4,6},{6,4},{8,10},{10,8},{12,14},{14,12},{16,18},{18,... | collective-permute-start | bytes 3538952 | tf_op jit(solution)/shard_map/ppermute | solution.py:1283
  120.7 3.9 %collective-permute-start.19 = (f32[8,768]{1,0:T(8,128)S(1)}, f32[8,768]{1,0:T(8,128)S(1)}, u32[]{:S(2)}, u32[]{:S(2)}) collective-permute-start(f32[8,768]{1,0:T(8,128)S(1)} %get-tuple-element.161), channel_id=1, source_target_pairs={{0,1},{1,0},{2,3},{3,2},{4,5},{5,4},{6,7},{7,6},{8,9},{9,8},{10,11... | collective-permute-start | bytes 73736 | tf_op jit(solution)/shard_map/ppermute | solution.py:1278
  122.4 20.6 %collective-permute-start.22 = (bf16[96,1536]{1,0:T(8,128)(2,1)S(1)}, bf16[96,1536]{1,0:T(8,128)(2,1)S(1)}, u32[]{:S(2)}, u32[]{:S(2)}) collective-permute-start(bf16[96,1536]{1,0:T(8,128)(2,1)S(1)} %bitcast.159), channel_id=1, source_target_pairs={{0,4},{2,6},{4,0},{6,2},{8,12},{10,14},{12,8},{14,10},{16,20},{18,... | collective-permute-start | bytes 884744 | tf_op jit(solution)/shard_map/ppermute | solution.py:1283
  124.6 1.9 %collective-permute-start.20 = (bf16[16,768]{1,0:T(8,128)(2,1)S(1)}, bf16[16,768]{1,0:T(8,128)(2,1)S(1)}, u32[]{:S(2)}, u32[]{:S(2)}) collective-permute-start(bf16[16,768]{1,0:T(8,128)(2,1)S(1)} %fusion.25), channel_id=1, source_target_pairs={{0,2},{2,0},{4,6},{6,4},{8,10},{10,8},{12,14},{14,12},{16,18},{18,... | collective-permute-start | bytes 73736 | tf_op jit(solution)/shard_map/ppermute | solution.py:1283
  124.9 18.1 %collective-permute-start.21 = (bf16[96,1536]{1,0:T(8,128)(2,1)S(1)}, bf16[96,1536]{1,0:T(8,128)(2,1)S(1)}, u32[]{:S(2)}, u32[]{:S(2)}) collective-permute-start(bf16[96,1536]{1,0:T(8,128)(2,1)S(1)} %bitcast.160), channel_id=1, source_target_pairs={{0,8},{2,10},{4,12},{6,14},{8,0},{10,2},{12,4},{14,6},{16,24},{18,... | collective-permute-start | bytes 884744 | tf_op jit(solution)/shard_map/ppermute | solution.py:1283
  127.0 16.1 %collective-permute-start.24 = (bf16[192,768]{1,0:T(8,128)(2,1)S(1)}, bf16[192,768]{1,0:T(8,128)(2,1)S(1)}, u32[]{:S(2)}, u32[]{:S(2)}) collective-permute-start(bf16[192,768]{1,0:T(8,128)(2,1)S(1)} %bitcast.154), channel_id=1, source_target_pairs={{0,8},{2,10},{4,12},{6,14},{8,0},{10,2},{12,4},{14,6},{16,24},{18,... | collective-permute-start | bytes 884744 | tf_op jit(solution)/shard_map/ppermute | solution.py:1283
  128.0 15.1 %collective-permute-start.23 = (bf16[208,768]{1,0:T(8,128)(2,1)S(1)}, bf16[208,768]{1,0:T(8,128)(2,1)S(1)}, u32[]{:S(2)}, u32[]{:S(2)}) collective-permute-start(bf16[208,768]{1,0:T(8,128)(2,1)S(1)} %pad_maximum_fusion), channel_id=1, source_target_pairs={{0,4},{2,6},{4,0},{6,2},{8,12},{10,14},{12,8},{14,10},{16,20},{18,... | collective-permute-start | bytes 958472 | tf_op jit(solution)/shard_map/ppermute | solution.py:1283
  143.4 13.8 %collective-permute-start.26 = (bf16[96,768]{1,0:T(8,128)(2,1)S(1)}, bf16[96,768]{1,0:T(8,128)(2,1)S(1)}, u32[]{:S(2)}, u32[]{:S(2)}) collective-permute-start(bf16[96,768]{1,0:T(8,128)(2,1)S(1)} %bitcast.164), channel_id=1, source_target_pairs={{0,4},{2,6},{4,0},{6,2},{8,12},{10,14},{12,8},{14,10},{16,20},{18,... | collective-permute-start | bytes 442376 | tf_op jit(solution)/shard_map/ppermute | solution.py:1283
  145.0 12.3 %collective-permute-start.25 = (bf16[112,768]{1,0:T(8,128)(2,1)S(1)}, bf16[112,768]{1,0:T(8,128)(2,1)S(1)}, u32[]{:S(2)}, u32[]{:S(2)}) collective-permute-start(bf16[112,768]{1,0:T(8,128)(2,1)S(1)} %pad_maximum_fusion.3), channel_id=1, source_target_pairs={{0,8},{2,10},{4,12},{6,14},{8,0},{10,2},{12,4},{14,6},{16,24},{18,... | collective-permute-start | bytes 516104 | tf_op jit(solution)/shard_map/ppermute | solution.py:1283
  146.1 20.4 %collective-permute-start.28 = (bf16[96,1536]{1,0:T(8,128)(2,1)S(1)}, bf16[96,1536]{1,0:T(8,128)(2,1)S(1)}, u32[]{:S(2)}, u32[]{:S(2)}) collective-permute-start(bf16[96,1536]{1,0:T(8,128)(2,1)S(1)} %pad_maximum_fusion.1), channel_id=1, source_target_pairs={{0,16},{2,18},{4,20},{6,22},{8,24},{10,26},{12,28},{14,30},{16,0},... | collective-permute-start | bytes 884744 | tf_op jit(solution)/shard_map/ppermute | solution.py:1283
  157.4 11.3 %collective-permute-start.27 = (bf16[112,768]{1,0:T(8,128)(2,1)S(1)}, bf16[112,768]{1,0:T(8,128)(2,1)S(1)}, u32[]{:S(2)}, u32[]{:S(2)}) collective-permute-start(bf16[112,768]{1,0:T(8,128)(2,1)S(1)} %pad_maximum_fusion.4), channel_id=1, source_target_pairs={{0,16},{2,18},{4,20},{6,22},{8,24},{10,26},{12,28},{14,30},{16,0},... | collective-permute-start | bytes 516104 | tf_op jit(solution)/shard_map/ppermute | solution.py:1283
  (9 other events, 106.3 us)

commit v3 on v2

--- a/solution.py
+++ b/solution.py
@@ -225,13 +225,13 @@
     start_all(w_in)
     start_all(x_in[1:])
     model = x_ref.shape[1]
-    half, quarter, fourth = proj_hbm.shape[0] // 2, fc_hbm.shape[0] // 4, out_hbm.shape[0] // 4
+    half, quarter, out_half = proj_hbm.shape[0] // 2, fc_hbm.shape[0] // 4, out_hbm.shape[0] // 2
     sends_in = []
     for index, (source, target, place, rows) in enumerate(
         (
             (proj_hbm, proj_ref.at[:half, :], bits_ref[0], half),
             (fc_hbm, fc_ref, bits_ref[1], quarter),
-            (out_hbm, out_ref, bits_ref[4], fourth),
+            (out_hbm, out_ref, bits_ref[0], out_half),
         )
     ):
         where = pl.ds(pl.multiple_of(place * rows, 32), rows)
@@ -319,7 +319,7 @@
     sends = [
         (width // 2 + 32, model),
         (model // 4, units),
-        (units // 4, model),
+        (units // 2, model),
     ]
     shapes = [(slots, model), (model, slots)]
     dma = pltpu.SemaphoreType.DMA
@@ -344,7 +344,7 @@
         + [pltpu.VMEM((slots, model), BF), pltpu.VMEM((TILE, model), BF)]
         + [dma((tokens,)), dma((3,)), dma((tokens,)), dma((6,)), dma((tokens,)), dma((tokens,))],
         6 * slots * model * width,
-        12,
+        13,
     )
 
 
@@ -748,7 +748,7 @@
     out_kept_hbm,
     *rest,
 ):
-    fc_pieces, out_pieces, proj_pieces, rest = rest[:4], rest[4:8], rest[8:10], rest[10:]
+    fc_pieces, out_pieces, proj_pieces, rest = rest[:4], rest[4:6], rest[6:8], rest[8:]
     do0_ref, fc_kept_ref, out_kept_ref, sums_ref, act_ref, gmid_out, ga_out, do1_out, *rest = rest
     gc_ref, bias_ref, fc_ref, ow_ref, c_ref, g_ref, *rest = rest
     late_refs, (gmid_ref, ga_ref, low_ref, do1_ref, proj1_ref, *rest) = rest[:4], rest[4:]
@@ -757,7 +757,7 @@
     slots, model = c_ref.shape
     first = fetch_rows(fc_pieces, bits_ref[1], fc_ref, sems.at[0])
     first += [pltpu.make_async_copy(c_hbm, c_ref, sems.at[2, 0])]
-    second = fetch_rows(out_pieces, bits_ref[4], ow_ref, sems.at[1])
+    second = fetch_rows(out_pieces, bits_ref[0], ow_ref, sems.at[1])
     second += [pltpu.make_async_copy(g_hbm, g_ref, sems.at[2, 1])]
     late = [
         pltpu.make_async_copy(source, target, late_sems.at[index])
@@ -1018,7 +1018,7 @@
 def backward_other_kernel(
     bits_ref, length_ref, lse_ref, qkv_hbm, ctxt_hbm, do_hbm, d0_hbm, w_hbm, ow_hbm, act0_hbm, act1_hbm, *rest
 ):
-    pieces, out_pieces, rest = rest[:4], rest[4:8], rest[8:]
+    pieces, out_pieces, rest = rest[:4], rest[4:6], rest[6:]
     both_ref, weight_ref, ow_ref, act_ref, qkv_ref, ctxt_ref, do_ref, *rest = rest
     scratch, (sems, late_sem, w_sems, ow_sems, act_sems) = rest[:14], rest[14:]
     width = do_ref.shape[1]
@@ -1037,7 +1037,7 @@
     late += fetch_rows([ow_hbm], 0, ow_ref.at[rows, :], ow_sems.at[0])
     late += [pltpu.make_async_copy(act0_hbm, act_ref.at[:, rows], act_sems.at[0])]
     rows = pl.ds(pl.multiple_of((1 - bits_ref[3]) * units, 128), units)
-    late += fetch_rows(out_pieces, bits_ref[4], ow_ref.at[rows, :], ow_sems.at[1])
+    late += fetch_rows(out_pieces, bits_ref[0], ow_ref.at[rows, :], ow_sems.at[1])
     late += [pltpu.make_async_copy(act1_hbm, act_ref.at[:, rows], act_sems.at[1])]
     start_all(late)
     d_ref = both_ref.at[:, other]
@@ -1359,7 +1359,6 @@
             quarter,
             (place >> first_bit) & 1,
             lax.axis_index("tensor"),
-            ((place >> 2) & 1) * 2 + one_bit,
         ]
     ).astype(jnp.int32)
     length = lengths.astype(jnp.int32)
@@ -1418,20 +1417,21 @@
         proj_other,
     )
 
-    c_low, fc_mine, out_mine = tie(c_low, fc_mine, out_mine)
+    c_low, fc_mine = tie(c_low, fc_mine)
     fc_side = swap(fc_mine, 2)
     fc_core = swap(fc_mine, 1)
-    out_side = swap(out_mine, 4)
-    out_core = swap(out_mine, 1)
     gc0, act0, fc_kept, out_kept, fc_sent, out_sent, grad_fc_bias, c_low, grad_mlp = feed_forward_own(
         bits, block, c_low, grad_mlp, c_turned, grad_mlp_turned, vec, fc_weight, out_weight
     )
 
-    fc_sent, out_sent, fc_side, fc_core, out_side, out_core = tie(
-        fc_sent, out_sent, fc_side, fc_core, out_side, out_core
+    fc_sent, out_sent, fc_side, fc_core, out_mine = tie(
+        fc_sent, out_sent, fc_side, fc_core, out_mine
     )
     fc_other = [fc_mine, fc_core, fc_side, swap(fc_side, 1)]
-    out_other = [out_mine, out_core, out_side, swap(out_side, 1)]
+    out_other = [out_mine, swap(out_mine, 1)]
+    fc_sent, out_sent, fc_other[3], out_other[1] = tie(
+        fc_sent, out_sent, fc_other[3], out_other[1]
+    )
     fc_got = swap(fc_sent, 1 << first_bit)
     out_got = swap(out_sent, 1 << first_bit)
     do0, fc_kept, out_kept, sums2, act1, grad_middle, grad_attn, do1 = feed_forward_other(

time: 173 us -> 169 us (0.977)
  waiting for transfers between devices: 12.6 us -> 8.81 us
    ppermute x5, waiting for transfers between devices: 8.16 us -> 2.68 us  [across(): return lax.ppermute(value, 'tensor', [(0, 1), (1, 0)])]
    ppermute x24 -> x22, waiting for transfers between devices: 4.42 us -> 6.12 us  [swap(): return lax.ppermute(value, 'dp', [(i, i ^ bit) for i in range(count)])]
    ppermute x24 -> x22, starting transfers between devices: 17.2 us -> 16.4 us  [swap(): return lax.ppermute(value, 'dp', [(i, i ^ bit) for i in range(count)])]
  transfers between devices with their start and end apart: 29 -> 27, of which waited for: 8 -> 7; matrix products, arithmetic and copies ran while one was open for 2% -> 2% of each run, Pallas kernels for 70% -> 71%
where the time goes in v3:
time: 169 us; the launch traced here: 168 us
  Pallas kernels  120 us (71%)
  starting transfers between devices  24.1 us (14%)
  waiting for transfers between devices  8.81 us (5%)
  local copies, waits for them, and re-layouts  7.17 us (4%)
  other arithmetic  6.22 us (4%)
  between operations  1.87 us (1%)
    pallas_call x9, Pallas kernels, call(): pl.pallas_call(body, name=name, grid=(steps,), out_shape=tuple(((pltpu.VM...  120 us
    ppermute x22, starting transfers between devices, swap(): return lax.ppermute(value, 'dp', [(i, i ^ bit) for i in range(count)])  16.4 us
    ppermute x5, starting transfers between devices, across(): return lax.ppermute(value, 'tensor', [(0, 1), (1, 0)])  7.7 us
    ppermute x22, waiting for transfers between devices, swap(): return lax.ppermute(value, 'dp', [(i, i ^ bit) for i in range(count)])  6.12 us
    convert_element_type x16, other arithmetic, part(): return total.astype(BF)  3.63 us
  transfers between devices with their start and end apart: 27, of which 7 were waited for; matrix products, arithmetic and copies ran while one was open for 2% of the time, Pallas kernels for 71%

profile of v3, /device:TPU:0, one launch (start us, length us, event | category | flops | bytes accessed | tf_op | source)
XLA Modules:
  0.0 168.2 jit_solution(7777637946757124785)
XLA Ops:
  0.6 1.1 dynamic-slice_bitcast_fusion
  1.7 3.0 %collective-permute-start = (bf16[3,192,384]{2,1,0:T(8,128)(2,1)S(1)}, bf16[3,192,384]{2,1,0:T(8,128)(2,1)S(1)}, u32[]{:S(2)}, u32[]{:S(2)}) collective-permute-start(bf16[3,192,384]{2,1,0:T(8,128)(2,1)S(1)} %dynamic-slice_bitcast_fusion), channel_id=1, source_target_pairs={{0,1},{1,0},{2,3},{3,2},{4,5},{5,4},{6,7},{7,6},{8,9},{9,8},{10,11... | collective-permute-start | bytes 1327112 | tf_op jit(solution)/shard_map/ppermute | solution.py:1278
  5.5 8.5 %project_own.1 = (f32[16,768]{1,0:T(8,128)}, bf16[1024,1152]{1,0:T(8,128)(2,1)S(1)}, bf16[1024,768]{1,0:T(8,128)(2,1)S(1)}, bf16[768,1024]{1,0:T(8,128)(2,1)S(1)...) custom-call(s32[4]{0:T(128)S(1)} %pad_add_fusion.bits_ref, ...), custom_call_target="tpu_custom_call" | custom-call | flops 1811939328 | bytes 15562772 | tf_op jit(solution)/shard_map/project_own/pallas_call | solution.py:81
  14.0 0.9 collective-permute-done.rest_0_
  14.9 1.8 %collective-permute-start.1 = (bf16[3,192,384]{2,1,0:T(8,128)(2,1)S(1)}, bf16[3,192,384]{2,1,0:T(8,128)(2,1)S(1)}, u32[]{:S(2)}, u32[]{:S(2)}) collective-permute-start(bf16[3,192,384]{2,1,0:T(8,128)(2,1)S(1)} %collective-permute-done.rest_0_), channel_id=1, source_target_pairs={{0,4},{2,6},{4,0},{6,2},{8,12},{10,14},{12,8},{14,10},{16,20},{18,... | collective-permute-start | bytes 1327112 | tf_op jit(solution)/shard_map/ppermute | solution.py:1283
  16.7 1.5 collective-permute-start.3
  18.7 8.4 %attention_forward_own.1 = (f32[6,1024]{1,0:T(8,128)}, bf16[1024,384]{1,0:T(8,128)(2,1)}, f32[384,1024]{1,0:T(8,128)}, bf16[1024,1152]{1,0:T(8,128)(2,1)}) custom-call(s32[1]{0:T(128)S(6)} %copy.59.length_ref, bf16[1024,1152]{1,0:T(8,128)(2,1)S(1)} %get-tuple-element.108.qkv_ref), custom_call_target="tpu_custom_call" | custom-call | flops 2415919104 | bytes 4743172 | tf_op jit(solution)/shard_map/attention_forward_own/pallas_call | solution.py:81
  29.0 1.5 collective-permute-start.9
  30.5 16.9 %attention_forward_other.1 = (f32[6,1024]{1,0:T(8,128)}, bf16[1024,768]{1,0:T(8,128)(2,1)S(1)}, bf16[768,1024]{1,0:T(8,128)(2,1)S(1)}, f32[1024,768]{1,0:T(8,128...) custom-call(s32[4]{0:T(128)S(1)} %pad_add_fusion.bits_ref, s32[1]{0:T(128)S(6)} %copy.59.length_ref, ...), custom_call_target="tpu_custom_call" | custom-call | flops 5435817984 | bytes 14155796 | tf_op jit(solution)/shard_map/attention_forward_other/pallas_call | solution.py:81
  47.6 1.4 collective-permute-start.7
  49.1 17.8 %feed_forward_own.1 = (bf16[1024,768]{1,0:T(8,128)(2,1)}, bf16[1024,1536]{1,0:T(8,128)(2,1)}, bf16[384,1536]{1,0:T(8,128)(2,1)}, bf16[384,1536]{1,0:T(8,128)(2,1...) custom-call(s32[4]{0:T(128)S(1)} %pad_add_fusion.bits_ref, ...), custom_call_target="tpu_custom_call" | custom-call | flops 12079595520 | bytes 14997520 | tf_op jit(solution)/shard_map/feed_forward_own/pallas_call | solution.py:81
  67.5 3.2 %collective-permute-done.10.rest_3_ = bf16[192,1536]{1,0:T(8,128)(2,1)S(1)} collective-permute-done((bf16[192,1536]{1,0:T(8,128)(2,1)S(1)}, bf16[192,1536]{1,0:T(8,128)(2,1)S(1)}, u32[]{:S(2)}, u32[]{:S(2)}) %collective-permute-start.10) | collective-permute-done | bytes 589856 | tf_op jit(solution)/shard_map/ppermute | solution.py:1283
  72.1 19.8 %feed_forward_other.1 = (bf16[1024,384]{1,0:T(8,128)(2,1)S(1)}, bf16[384,1536]{1,0:T(8,128)(2,1)S(1)}, bf16[384,1536]{1,0:T(8,128)(2,1)S(1)}, f32[3,768]{1,0:T(4...) custom-call(s32[4]{0:T(128)S(1)} %pad_add_fusion.bits_ref, ...), custom_call_target="tpu_custom_call" | custom-call | flops 8455716864 | bytes 26526740 | tf_op jit(solution)/shard_map/feed_forward_other/pallas_call | solution.py:81
  91.9 1.2 add_convert_fusion.3
  93.1 1.2 constant_dynamic-slice_fusion.4
  94.3 1.2 add_convert_fusion.2
  95.5 1.2 constant_dynamic-slice_fusion.2
  97.4 1.6 collective-permute-start.15
  99.2 18.1 %attention_backward_own.1 = (f32[8,768]{1,0:T(8,128)S(1)}, f32[16,768]{1,0:T(8,128)S(1)}, bf16[384,1536]{1,0:T(8,128)(2,1)S(1)}, bf16[384,1536]{1,0:T(8,128)(2,1)S(1)}, bf16[1024,1152]{1,0:T(8,128)(2,1)}) custom-call(s32[4]{0:T(128)S(1)} %pad_add_fusion.bits_ref, s32[1]{0:T(128)S(6)} %copy.59.length_ref, f32[6,1024]{1,0:T(8,128)} %get-tuple-element.109.lse_ref, ...), custom_call_target="tpu_custom_call" | custom-call | flops 6039797760 | bytes 11298836 | tf_op jit(solution)/shard_map/attention_backward_own/pallas_call | solution.py:81
  117.5 1.2 collective-permute-start.17
  118.8 1.5 collective-permute-start.20
  120.3 1.1 collective-permute-done.17
  123.1 1.1 collective-permute-start.22
  124.2 1.4 collective-permute-start.21
  125.8 14.4 %attention_backward_other.1 = (bf16[1024,2304]{1,0:T(8,128)(2,1)S(1)}, bf16[768,2304]{1,0:T(8,128)(2,1)S(1)}, bf16[3072,768]{1,0:T(8,128)(2,1)S(1)}, bf16[1024,3072]{1,0:T(8,128)(2,1)S(1)}) custom-call(s32[4]{0:T(128)S(1)} %pad_add_fusion.bits_ref, s32[1]{0:T(128)S(6)} %copy.59.length_ref, f32[6,1024]{1,0:T(8,128)} %get-tuple-element.164.lse_ref, ...), custom_call_target="tpu_custom_call" | custom-call | flops 3623878656 | bytes 21651476 | tf_op jit(solution)/shard_map/attention_backward_other/pallas_call | solution.py:81
  141.3 1.0 collective-permute-start.23
  142.2 2.6 %collective-permute-start.26 = (bf16[96,1536]{1,0:T(8,128)(2,1)S(1)}, bf16[96,1536]{1,0:T(8,128)(2,1)S(1)}, u32[]{:S(2)}, u32[]{:S(2)}) collective-permute-start(bf16[96,1536]{1,0:T(8,128)(2,1)S(1)} %pad_maximum_fusion.1), channel_id=1, source_target_pairs={{0,16},{2,18},{4,20},{6,22},{8,24},{10,26},{12,28},{14,30},{16,0},... | collective-permute-start | bytes 884744 | tf_op jit(solution)/shard_map/ppermute | solution.py:1283
  144.8 8.6 %final.1 = f32[1024,768]{1,0:T(8,128)} custom-call(f32[16,768]{1,0:T(8,128)} %get-tuple-element.106.vec_ref, bf16[1024,2304]{1,0:T(8,128)(2,1)S(1)} %get-tuple-element.184.d_ref, bf16[768,2304]{1,0:T(8,128)(2,1)S(1)} %get-tuple-element.185.w_ref, bf16[1024,768]{1,0:T(8,128)(2,1)} %x_hbm.5, f32[1024,768]{1,0:T(8,128)} %get-tuple-element.186.gmid_hbm), custom_call_target="tpu_custom_call" | custom-call | flops 3623878656 | bytes 7913472 | tf_op jit(solution)/shard_map/final/pallas_call | solution.py:81
  154.0 7.6 %output.1 = bf16[1024,768]{1,0:T(8,128)(2,1)} custom-call(f32[16,768]{1,0:T(8,128)} %get-tuple-element.106.vec_ref, bf16[1024,3072]{1,0:T(8,128)(2,1)S(1)} %get-tuple-element.193.act_ref, bf16[3072,768]{1,0:T(8,128)(2,1)S(1)} %get-tuple-element.194.ow_ref, f32[1024,768]{1,0:T(8,128)} %get-tuple-element.129.middle_hbm.middle_ref), custom_call_target="tpu_custom_call" | custom-call | flops 4831838208 | bytes 4767744 | tf_op jit(solution)/shard_map/output/pallas_call | solution.py:81
  161.5 1.1 collective-permute-done.26
  162.7 0.9 fusion.4
  163.6 1.3 collective-permute-done.25
  (105 shorter events, 12.5 us)
Async XLA Ops:
  1.7 13.2 %collective-permute-start = (bf16[3,192,384]{2,1,0:T(8,128)(2,1)S(1)}, bf16[3,192,384]{2,1,0:T(8,128)(2,1)S(1)}, u32[]{:S(2)}, u32[]{:S(2)}) collective-permute-start(bf16[3,192,384]{2,1,0:T(8,128)(2,1)S(1)} %dynamic-slice_bitcast_fusion), channel_id=1, source_target_pairs={{0,1},{1,0},{2,3},{3,2},{4,5},{5,4},{6,7},{7,6},{8,9},{9,8},{10,11... | collective-permute-start | bytes 1327112 | tf_op jit(solution)/shard_map/ppermute | solution.py:1278
  14.9 12.9 %collective-permute-start.2 = (bf16[3,192,384]{2,1,0:T(8,128)(2,1)S(1)}, bf16[3,192,384]{2,1,0:T(8,128)(2,1)S(1)}, u32[]{:S(2)}, u32[]{:S(2)}) collective-permute-start(bf16[3,192,384]{2,1,0:T(8,128)(2,1)S(1)} %collective-permute-done.rest_0_), channel_id=1, source_target_pairs={{0,2},{2,0},{4,6},{6,4},{8,10},{10,8},{12,14},{14,12},{16,18},{18,... | collective-permute-start | bytes 1327112 | tf_op jit(solution)/shard_map/ppermute | solution.py:1283
  14.9 12.9 %collective-permute-start.1 = (bf16[3,192,384]{2,1,0:T(8,128)(2,1)S(1)}, bf16[3,192,384]{2,1,0:T(8,128)(2,1)S(1)}, u32[]{:S(2)}, u32[]{:S(2)}) collective-permute-start(bf16[3,192,384]{2,1,0:T(8,128)(2,1)S(1)} %collective-permute-done.rest_0_), channel_id=1, source_target_pairs={{0,4},{2,6},{4,0},{6,2},{8,12},{10,14},{12,8},{14,10},{16,20},{18,... | collective-permute-start | bytes 1327112 | tf_op jit(solution)/shard_map/ppermute | solution.py:1283
  16.7 11.1 %collective-permute-start.3 = (bf16[224,768]{1,0:T(8,128)(2,1)}, bf16[224,768]{1,0:T(8,128)(2,1)S(1)}, u32[]{:S(2)}, u32[]{:S(2)}) collective-permute-start(bf16[224,768]{1,0:T(8,128)(2,1)} %get-tuple-element.112), channel_id=1, source_target_pairs={{0,1},{1,0},{2,3},{3,2},{4,5},{5,4},{6,7},{7,6},{8,9},{9,8},{10,11... | collective-permute-start | bytes 1032200 | tf_op jit(solution)/shard_map/ppermute | solution.py:1278
  18.2 29.4 %collective-permute-start.6 = (bf16[192,1536]{1,0:T(8,128)(2,1)}, bf16[192,1536]{1,0:T(8,128)(2,1)S(1)}, u32[]{:S(2)}, u32[]{:S(2)}) collective-permute-start(bf16[192,1536]{1,0:T(8,128)(2,1)} %get-tuple-element.121), channel_id=1, source_target_pairs={{0,1},{1,0},{2,3},{3,2},{4,5},{5,4},{6,7},{7,6},{8,9},{9,8},{10,11... | collective-permute-start | bytes 1769480 | tf_op jit(solution)/shard_map/ppermute | solution.py:1278
  27.8 19.7 %copy-start.4 = (bf16[224,768]{1,0:T(8,128)(2,1)}, bf16[224,768]{1,0:T(8,128)(2,1)S(1)}, u32[]{:S(2)}) copy-start(bf16[224,768]{1,0:T(8,128)(2,1)S(1)} %collective-permute-done.3.rest_4_.rest_6_) | copy-start | bytes 1032196
  27.8 19.7 %copy-start.1 = (bf16[3,192,384]{2,1,0:T(8,128)(2,1)}, bf16[3,192,384]{2,1,0:T(8,128)(2,1)S(1)}, u32[]{:S(2)}) copy-start(bf16[3,192,384]{2,1,0:T(8,128)(2,1)S(1)} %collective-permute-done.2.rest_1_) | copy-start | bytes 1327108
  27.8 19.7 %copy-start.2 = (bf16[3,192,384]{2,1,0:T(8,128)(2,1)}, bf16[3,192,384]{2,1,0:T(8,128)(2,1)S(1)}, u32[]{:S(2)}) copy-start(bf16[3,192,384]{2,1,0:T(8,128)(2,1)S(1)} %collective-permute-done.1.rest_2_) | copy-start | bytes 1327108
  27.8 2.7 %collective-permute-start.5 = (bf16[224,768]{1,0:T(8,128)(2,1)S(1)}, bf16[224,768]{1,0:T(8,128)(2,1)S(1)}, u32[]{:S(2)}, u32[]{:S(2)}) collective-permute-start(bf16[224,768]{1,0:T(8,128)(2,1)S(1)} %collective-permute-done.3.rest_4_.rest_6_), channel_id=1, source_target_pairs={{0,2},{2,0},{4,6},{6,4},{8,10},{10,8},{12,14},{14,12},{16,18},{18,... | collective-permute-start | bytes 1032200 | tf_op jit(solution)/shard_map/ppermute | solution.py:1283
  27.9 2.6 %collective-permute-start.4 = (bf16[3,192,384]{2,1,0:T(8,128)(2,1)S(1)}, bf16[3,192,384]{2,1,0:T(8,128)(2,1)S(1)}, u32[]{:S(2)}, u32[]{:S(2)}) collective-permute-start(bf16[3,192,384]{2,1,0:T(8,128)(2,1)S(1)} %collective-permute-done.1.rest_2_), channel_id=1, source_target_pairs={{0,2},{2,0},{4,6},{6,4},{8,10},{10,8},{12,14},{14,12},{16,18},{18,... | collective-permute-start | bytes 1327112 | tf_op jit(solution)/shard_map/ppermute | solution.py:1283
  29.0 37.9 %collective-permute-start.9 = (bf16[768,768]{1,0:T(8,128)(2,1)S(1)}, bf16[768,768]{1,0:T(8,128)(2,1)S(1)}, u32[]{:S(2)}, u32[]{:S(2)}) collective-permute-start(bf16[768,768]{1,0:T(8,128)(2,1)S(1)} %copy-done.8), channel_id=1, source_target_pairs={{0,1},{1,0},{2,3},{3,2},{4,5},{5,4},{6,7},{7,6},{8,9},{9,8},{10,11... | collective-permute-start | bytes 3538952 | tf_op jit(solution)/shard_map/ppermute | solution.py:1278
  30.5 17.0 %copy-start.3 = (bf16[3,192,384]{2,1,0:T(8,128)(2,1)}, bf16[3,192,384]{2,1,0:T(8,128)(2,1)S(1)}, u32[]{:S(2)}) copy-start(bf16[3,192,384]{2,1,0:T(8,128)(2,1)S(1)} %collective-permute-done.4.rest_3_) | copy-start | bytes 1327108
  47.5 19.3 %copy-start.9 = (bf16[192,1536]{1,0:T(8,128)(2,1)}, bf16[192,1536]{1,0:T(8,128)(2,1)S(1)}, u32[]{:S(2)}) copy-start(bf16[192,1536]{1,0:T(8,128)(2,1)S(1)} %collective-permute-done.6.rest_0_) | copy-start | bytes 1769476
  47.5 19.3 %collective-permute-start.8 = (bf16[192,1536]{1,0:T(8,128)(2,1)S(1)}, bf16[192,1536]{1,0:T(8,128)(2,1)S(1)}, u32[]{:S(2)}, u32[]{:S(2)}) collective-permute-start(bf16[192,1536]{1,0:T(8,128)(2,1)S(1)} %collective-permute-done.6.rest_0_), channel_id=1, source_target_pairs={{0,2},{2,0},{4,6},{6,4},{8,10},{10,8},{12,14},{14,12},{16,18},{18,... | collective-permute-start | bytes 1769480 | tf_op jit(solution)/shard_map/ppermute | solution.py:1283
  47.6 19.3 %collective-permute-start.7 = (bf16[192,1536]{1,0:T(8,128)(2,1)S(1)}, bf16[192,1536]{1,0:T(8,128)(2,1)S(1)}, u32[]{:S(2)}, u32[]{:S(2)}) collective-permute-start(bf16[192,1536]{1,0:T(8,128)(2,1)S(1)} %collective-permute-done.6.rest_0_), channel_id=1, source_target_pairs={{0,4},{2,6},{4,0},{6,2},{8,12},{10,14},{12,8},{14,10},{16,20},{18,... | collective-permute-start | bytes 1769480 | tf_op jit(solution)/shard_map/ppermute | solution.py:1283
  66.9 3.8 %collective-permute-start.11 = (bf16[768,768]{1,0:T(8,128)(2,1)S(1)}, bf16[768,768]{1,0:T(8,128)(2,1)S(1)}, u32[]{:S(2)}, u32[]{:S(2)}) collective-permute-start(bf16[768,768]{1,0:T(8,128)(2,1)S(1)} %collective-permute-done.9.rest_4_), channel_id=1, source_target_pairs={{0,2},{2,0},{4,6},{6,4},{8,10},{10,8},{12,14},{14,12},{16,18},{18,... | collective-permute-start | bytes 3538952 | tf_op jit(solution)/shard_map/ppermute | solution.py:1283
  67.2 3.5 %collective-permute-start.10 = (bf16[192,1536]{1,0:T(8,128)(2,1)S(1)}, bf16[192,1536]{1,0:T(8,128)(2,1)S(1)}, u32[]{:S(2)}, u32[]{:S(2)}) collective-permute-start(bf16[192,1536]{1,0:T(8,128)(2,1)S(1)} %collective-permute-done.7.rest_2_), channel_id=1, source_target_pairs={{0,2},{2,0},{4,6},{6,4},{8,10},{10,8},{12,14},{14,12},{16,18},{18,... | collective-permute-start | bytes 1769480 | tf_op jit(solution)/shard_map/ppermute | solution.py:1283
  70.7 21.2 %collective-permute-start.12 = (bf16[384,1536]{1,0:T(8,128)(2,1)S(1)}, bf16[384,1536]{1,0:T(8,128)(2,1)}, u32[]{:S(2)}, u32[]{:S(2)}) collective-permute-start(bf16[384,1536]{1,0:T(8,128)(2,1)S(1)} %get-tuple-element.146), channel_id=1, source_target_pairs={{0,2},{2,0},{4,6},{6,4},{8,10},{10,8},{12,14},{14,12},{16,18},{18,... | collective-permute-start | bytes 3538952 | tf_op jit(solution)/shard_map/ppermute | solution.py:1283
  71.9 20.0 %collective-permute-start.13 = (bf16[384,1536]{1,0:T(8,128)(2,1)S(1)}, bf16[384,1536]{1,0:T(8,128)(2,1)}, u32[]{:S(2)}, u32[]{:S(2)}) collective-permute-start(bf16[384,1536]{1,0:T(8,128)(2,1)S(1)} %get-tuple-element.147), channel_id=1, source_target_pairs={{0,2},{2,0},{4,6},{6,4},{8,10},{10,8},{12,14},{14,12},{16,18},{18,... | collective-permute-start | bytes 3538952 | tf_op jit(solution)/shard_map/ppermute | solution.py:1283
  96.6 20.7 %collective-permute-start.14 = (bf16[192,1536]{1,0:T(8,128)(2,1)S(1)}, bf16[192,1536]{1,0:T(8,128)(2,1)S(1)}, u32[]{:S(2)}, u32[]{:S(2)}) collective-permute-start(bf16[192,1536]{1,0:T(8,128)(2,1)S(1)} %bitcast.150), channel_id=1, source_target_pairs={{0,4},{2,6},{4,0},{6,2},{8,12},{10,14},{12,8},{14,10},{16,20},{18,... | collective-permute-start | bytes 1769480 | tf_op jit(solution)/shard_map/ppermute | solution.py:1283
  97.4 19.9 %collective-permute-start.15 = (bf16[192,1536]{1,0:T(8,128)(2,1)S(1)}, bf16[192,1536]{1,0:T(8,128)(2,1)S(1)}, u32[]{:S(2)}, u32[]{:S(2)}) collective-permute-start(bf16[192,1536]{1,0:T(8,128)(2,1)S(1)} %bitcast.151), channel_id=1, source_target_pairs={{0,8},{2,10},{4,12},{6,14},{8,0},{10,2},{12,4},{14,6},{16,24},{18,... | collective-permute-start | bytes 1769480 | tf_op jit(solution)/shard_map/ppermute | solution.py:1283
  117.3 5.4 %collective-permute-start.16 = (bf16[384,1536]{1,0:T(8,128)(2,1)S(1)}, bf16[384,1536]{1,0:T(8,128)(2,1)S(1)}, u32[]{:S(2)}, u32[]{:S(2)}) collective-permute-start(bf16[384,1536]{1,0:T(8,128)(2,1)S(1)} %get-tuple-element.163), channel_id=1, source_target_pairs={{0,2},{2,0},{4,6},{6,4},{8,10},{10,8},{12,14},{14,12},{16,18},{18,... | collective-permute-start | bytes 3538952 | tf_op jit(solution)/shard_map/ppermute | solution.py:1283
  117.5 3.9 %collective-permute-start.17 = (f32[8,768]{1,0:T(8,128)S(1)}, f32[8,768]{1,0:T(8,128)S(1)}, u32[]{:S(2)}, u32[]{:S(2)}) collective-permute-start(f32[8,768]{1,0:T(8,128)S(1)} %get-tuple-element.165), channel_id=1, source_target_pairs={{0,1},{1,0},{2,3},{3,2},{4,5},{5,4},{6,7},{7,6},{8,9},{9,8},{10,11... | collective-permute-start | bytes 73736 | tf_op jit(solution)/shard_map/ppermute | solution.py:1278
  118.8 21.3 %collective-permute-start.20 = (bf16[96,1536]{1,0:T(8,128)(2,1)S(1)}, bf16[96,1536]{1,0:T(8,128)(2,1)S(1)}, u32[]{:S(2)}, u32[]{:S(2)}) collective-permute-start(bf16[96,1536]{1,0:T(8,128)(2,1)S(1)} %bitcast.158), channel_id=1, source_target_pairs={{0,4},{2,6},{4,0},{6,2},{8,12},{10,14},{12,8},{14,10},{16,20},{18,... | collective-permute-start | bytes 884744 | tf_op jit(solution)/shard_map/ppermute | solution.py:1283
  121.4 1.3 collective-permute-start.18
  121.6 18.5 %collective-permute-start.19 = (bf16[96,1536]{1,0:T(8,128)(2,1)S(1)}, bf16[96,1536]{1,0:T(8,128)(2,1)S(1)}, u32[]{:S(2)}, u32[]{:S(2)}) collective-permute-start(bf16[96,1536]{1,0:T(8,128)(2,1)S(1)} %bitcast.159), channel_id=1, source_target_pairs={{0,8},{2,10},{4,12},{6,14},{8,0},{10,2},{12,4},{14,6},{16,24},{18,... | collective-permute-start | bytes 884744 | tf_op jit(solution)/shard_map/ppermute | solution.py:1283
  123.1 17.1 %collective-permute-start.22 = (bf16[192,768]{1,0:T(8,128)(2,1)S(1)}, bf16[192,768]{1,0:T(8,128)(2,1)S(1)}, u32[]{:S(2)}, u32[]{:S(2)}) collective-permute-start(bf16[192,768]{1,0:T(8,128)(2,1)S(1)} %bitcast.153), channel_id=1, source_target_pairs={{0,8},{2,10},{4,12},{6,14},{8,0},{10,2},{12,4},{14,6},{16,24},{18,... | collective-permute-start | bytes 884744 | tf_op jit(solution)/shard_map/ppermute | solution.py:1283
  124.2 15.9 %collective-permute-start.21 = (bf16[208,768]{1,0:T(8,128)(2,1)S(1)}, bf16[208,768]{1,0:T(8,128)(2,1)S(1)}, u32[]{:S(2)}, u32[]{:S(2)}) collective-permute-start(bf16[208,768]{1,0:T(8,128)(2,1)S(1)} %pad_maximum_fusion), channel_id=1, source_target_pairs={{0,4},{2,6},{4,0},{6,2},{8,12},{10,14},{12,8},{14,10},{16,20},{18,... | collective-permute-start | bytes 958472 | tf_op jit(solution)/shard_map/ppermute | solution.py:1283
  140.6 12.8 %collective-permute-start.24 = (bf16[96,768]{1,0:T(8,128)(2,1)S(1)}, bf16[96,768]{1,0:T(8,128)(2,1)S(1)}, u32[]{:S(2)}, u32[]{:S(2)}) collective-permute-start(bf16[96,768]{1,0:T(8,128)(2,1)S(1)} %bitcast.163), channel_id=1, source_target_pairs={{0,4},{2,6},{4,0},{6,2},{8,12},{10,14},{12,8},{14,10},{16,20},{18,... | collective-permute-start | bytes 442376 | tf_op jit(solution)/shard_map/ppermute | solution.py:1283
  141.3 12.1 %collective-permute-start.23 = (bf16[112,768]{1,0:T(8,128)(2,1)S(1)}, bf16[112,768]{1,0:T(8,128)(2,1)S(1)}, u32[]{:S(2)}, u32[]{:S(2)}) collective-permute-start(bf16[112,768]{1,0:T(8,128)(2,1)S(1)} %pad_maximum_fusion.3), channel_id=1, source_target_pairs={{0,8},{2,10},{4,12},{6,14},{8,0},{10,2},{12,4},{14,6},{16,24},{18,... | collective-permute-start | bytes 516104 | tf_op jit(solution)/shard_map/ppermute | solution.py:1283
  142.2 20.4 %collective-permute-start.26 = (bf16[96,1536]{1,0:T(8,128)(2,1)S(1)}, bf16[96,1536]{1,0:T(8,128)(2,1)S(1)}, u32[]{:S(2)}, u32[]{:S(2)}) collective-permute-start(bf16[96,1536]{1,0:T(8,128)(2,1)S(1)} %pad_maximum_fusion.1), channel_id=1, source_target_pairs={{0,16},{2,18},{4,20},{6,22},{8,24},{10,26},{12,28},{14,30},{16,0},... | collective-permute-start | bytes 884744 | tf_op jit(solution)/shard_map/ppermute | solution.py:1283
  153.6 11.3 %collective-permute-start.25 = (bf16[112,768]{1,0:T(8,128)(2,1)S(1)}, bf16[112,768]{1,0:T(8,128)(2,1)S(1)}, u32[]{:S(2)}, u32[]{:S(2)}) collective-permute-start(bf16[112,768]{1,0:T(8,128)(2,1)S(1)} %pad_maximum_fusion.4), channel_id=1, source_target_pairs={{0,16},{2,18},{4,20},{6,22},{8,24},{10,26},{12,28},{14,30},{16,0},... | collective-permute-start | bytes 516104 | tf_op jit(solution)/shard_map/ppermute | solution.py:1283
  (8 other events, 59.8 us)

commit v4 on v3

--- a/solution.py
+++ b/solution.py
@@ -1274,6 +1274,47 @@
     )[0]
 
 
+def stage_kernel(blocks, bits_ref, fc_kept, out_kept, fc_got, out_got, *rest):
+    kept_refs, sent_refs, (got_ref, total_ref, sems) = rest[:2], rest[2:4], rest[4:]
+    copies = [
+        pltpu.make_async_copy(got, got_ref.at[index], sems.at[index])
+        for index, got in enumerate((fc_got, out_got))
+    ]
+    start_all(copies)
+    for index, kept in enumerate((fc_kept, out_kept)):
+        copies[index].wait()
+
+        @pl.loop(0, kept.shape[0] // 48)
+        def _(part):
+            rows = pl.ds(pl.multiple_of(part * 48, 16), 48)
+            total = kept[rows, :].astype(F32) + got_ref[index, rows, :].astype(F32)
+            total_ref[index, rows, :] = total.astype(BF)
+
+        halves(
+            total_ref.at[index], bits_ref[4 + index], blocks[index], kept_refs[index], sent_refs[index]
+        )
+
+
+def second_stage(bits, blocks, kept, got):
+    rows, columns = kept[0].shape
+    shape = (rows // 2, columns)
+    saved, sent = (shape, BF, whole(shape)), (shape, BF, KEPT)
+    return call(
+        functools.partial(stage_kernel, blocks),
+        "second_stage",
+        1,
+        [(bits, SMEM)] + [(value, KEPT) for value in kept] + [(value, HBM) for value in got],
+        [saved] * 2 + [sent] * 2,
+        [
+            pltpu.VMEM((2, rows, columns), BF),
+            pltpu.VMEM((2, rows, columns), BF),
+            pltpu.SemaphoreType.DMA((2,)),
+        ],
+        4 * rows * columns,
+        12,
+    )
+
+
 def across(value):
     return lax.ppermute(value, "tensor", [(0, 1), (1, 0)])
 
@@ -1317,6 +1358,15 @@
         sent = part(1 - side)
         self.kept = part(side)
         return sent.reshape(-1, sent.shape[-1])
+
+    def block(self):
+        lower = [bit for bit in self.bits if bit < self.order[0]]
+        return self.kept.shape[-2] << len(lower)
+
+    def advanced(self, kept):
+        self.bit = self.order.pop(0)
+        self.bits.remove(self.bit)
+        self.kept = kept.reshape(*[2] * len(self.bits), *self.kept.shape[-2:])
 
     def finish(self, got):
         return self.kept.astype(F32) + got.reshape(self.kept.shape).astype(F32)
@@ -1347,7 +1397,7 @@
     share = model // shards
     first_bit = next(bit for bit in range(levels) if (share << bit) % 16 == 0)
     block = share << first_bit
-    later = [bit for bit in range(levels) if bit != first_bit]
+    later = list(range(first_bit + 1, levels)) + list(range(first_bit))
     order_a = list(later)
     order_b = [later[1], later[0]] + later[2:]
     place = lax.axis_index("dp")
@@ -1359,6 +1409,8 @@
             quarter,
             (place >> first_bit) & 1,
             lax.axis_index("tensor"),
+            (place >> order_a[0]) & 1,
+            (place >> order_b[0]) & 1,
         ]
     ).astype(jnp.int32)
     length = lengths.astype(jnp.int32)
@@ -1454,8 +1506,11 @@
     fc_sum = Reduction(fc_kept, first_bit, list(order_a))
     out_sum = Reduction(out_kept, first_bit, list(order_b))
     do0, fc_got, out_got = tie(do0, fc_got, out_got)
-    fc_sent = fc_sum.advance(fc_got)
-    out_sent = out_sum.advance(out_got)
+    fc_kept, out_kept, fc_sent, out_sent = second_stage(
+        bits, (fc_sum.block(), out_sum.block()), (fc_kept, out_kept), (fc_got, out_got)
+    )
+    fc_sum.advanced(fc_kept)
+    out_sum.advanced(out_kept)
     do0, fc_sent, out_sent = tie(do0, fc_sent, out_sent)
     fc_got = swap(fc_sent, 1 << fc_sum.bit)
     out_got = swap(out_sent, 1 << out_sum.bit)

time: 169 us -> 169 us (level)
  Pallas kernels: 120 us -> 124 us
  other arithmetic: 6.22 us -> 3.39 us
    pallas_call x9 -> x10, Pallas kernels: 120 us -> 124 us  [call(): pl.pallas_call(body, name=name, grid=(steps,), out_shape=tuple(((pltpu.VM...]
    convert_element_type x16 -> x11, other arithmetic: 3.63 us -> 0.9 us  [part(): return total.astype(BF)]
    dynamic_slice x4 -> x2, local copies, waits for them, and re-layouts: 2.4 us -> 0.1 us  [pick(): return lax.dynamic_index_in_dim(value, index, axis, keepdims=False)]
where the time goes in v4:
time: 169 us; the launch traced here: 168 us
  Pallas kernels  124 us (73%)
  starting transfers between devices  24.3 us (14%)
  waiting for transfers between devices  8.76 us (5%)
  local copies, waits for them, and re-layouts  6.01 us (4%)
  other arithmetic  3.39 us (2%)
  between operations  1.89 us (1%)
    pallas_call x10, Pallas kernels, call(): pl.pallas_call(body, name=name, grid=(steps,), out_shape=tuple(((pltpu.VM...  124 us
    ppermute x22, starting transfers between devices, swap(): return lax.ppermute(value, 'dp', [(i, i ^ bit) for i in range(count)])  16.6 us
    ppermute x5, starting transfers between devices, across(): return lax.ppermute(value, 'tensor', [(0, 1), (1, 0)])  7.72 us
    ppermute x22, waiting for transfers between devices, swap(): return lax.ppermute(value, 'dp', [(i, i ^ bit) for i in range(count)])  6.11 us
  transfers between devices with their start and end apart: 27, of which 7 were waited for; matrix products, arithmetic and copies ran while one was open for 2% of the time, Pallas kernels for 71%

profile of v4, /device:TPU:0, one launch (start us, length us, event | category | flops | bytes accessed | tf_op | source)
XLA Modules:
  0.0 168.0 jit_solution(8992556809274545055)
XLA Ops:
  0.6 1.1 dynamic-slice_bitcast_fusion
  1.7 3.0 %collective-permute-start = (bf16[3,192,384]{2,1,0:T(8,128)(2,1)S(1)}, bf16[3,192,384]{2,1,0:T(8,128)(2,1)S(1)}, u32[]{:S(2)}, u32[]{:S(2)}) collective-permute-start(bf16[3,192,384]{2,1,0:T(8,128)(2,1)S(1)} %dynamic-slice_bitcast_fusion), channel_id=1, source_target_pairs={{0,1},{1,0},{2,3},{3,2},{4,5},{5,4},{6,7},{7,6},{8,9},{9,8},{10,11... | collective-permute-start | bytes 1327112 | tf_op jit(solution)/shard_map/ppermute | solution.py:1319
  5.5 8.5 %project_own.1 = (f32[16,768]{1,0:T(8,128)}, bf16[1024,1152]{1,0:T(8,128)(2,1)S(1)}, bf16[1024,768]{1,0:T(8,128)(2,1)S(1)}, bf16[768,1024]{1,0:T(8,128)(2,1)S(1)...) custom-call(s32[6]{0:T(128)S(1)} %stack.39.bits_ref, ...), custom_call_target="tpu_custom_call" | custom-call | flops 1811939328 | bytes 15562780 | tf_op jit(solution)/shard_map/project_own/pallas_call | solution.py:81
  14.0 0.9 collective-permute-done.rest_0_
  14.9 1.8 %collective-permute-start.1 = (bf16[3,192,384]{2,1,0:T(8,128)(2,1)S(1)}, bf16[3,192,384]{2,1,0:T(8,128)(2,1)S(1)}, u32[]{:S(2)}, u32[]{:S(2)}) collective-permute-start(bf16[3,192,384]{2,1,0:T(8,128)(2,1)S(1)} %collective-permute-done.rest_0_), channel_id=1, source_target_pairs={{0,4},{2,6},{4,0},{6,2},{8,12},{10,14},{12,8},{14,10},{16,20},{18,... | collective-permute-start | bytes 1327112 | tf_op jit(solution)/shard_map/ppermute | solution.py:1324
  16.7 1.5 collective-permute-start.3
  18.7 8.4 %attention_forward_own.1 = (f32[6,1024]{1,0:T(8,128)}, bf16[1024,384]{1,0:T(8,128)(2,1)}, f32[384,1024]{1,0:T(8,128)}, bf16[1024,1152]{1,0:T(8,128)(2,1)}) custom-call(s32[1]{0:T(128)S(6)} %copy.45.length_ref, bf16[1024,1152]{1,0:T(8,128)(2,1)S(1)} %get-tuple-element.112.qkv_ref), custom_call_target="tpu_custom_call" | custom-call | flops 2415919104 | bytes 4743172 | tf_op jit(solution)/shard_map/attention_forward_own/pallas_call | solution.py:81
  29.0 1.5 collective-permute-start.9
  30.5 16.9 %attention_forward_other.1 = (f32[6,1024]{1,0:T(8,128)}, bf16[1024,768]{1,0:T(8,128)(2,1)S(1)}, bf16[768,1024]{1,0:T(8,128)(2,1)S(1)}, f32[1024,768]{1,0:T(8,128...) custom-call(s32[6]{0:T(128)S(1)} %stack.39.bits_ref, s32[1]{0:T(128)S(6)} %copy.45.length_ref, ...), custom_call_target="tpu_custom_call" | custom-call | flops 5435817984 | bytes 14155804 | tf_op jit(solution)/shard_map/attention_forward_other/pallas_call | solution.py:81
  47.6 1.4 collective-permute-start.7
  49.1 17.8 %feed_forward_own.1 = (bf16[1024,768]{1,0:T(8,128)(2,1)}, bf16[1024,1536]{1,0:T(8,128)(2,1)}, bf16[384,1536]{1,0:T(8,128)(2,1)}, bf16[384,1536]{1,0:T(8,128)(2,1...) custom-call(s32[6]{0:T(128)S(1)} %stack.39.bits_ref, ...), custom_call_target="tpu_custom_call" | custom-call | flops 12079595520 | bytes 14997528 | tf_op jit(solution)/shard_map/feed_forward_own/pallas_call | solution.py:81
  67.5 3.2 %collective-permute-done.10.rest_3_ = bf16[192,1536]{1,0:T(8,128)(2,1)S(1)} collective-permute-done((bf16[192,1536]{1,0:T(8,128)(2,1)S(1)}, bf16[192,1536]{1,0:T(8,128)(2,1)S(1)}, u32[]{:S(2)}, u32[]{:S(2)}) %collective-permute-start.10) | collective-permute-done | bytes 589856 | tf_op jit(solution)/shard_map/ppermute | solution.py:1324
  71.9 19.8 %feed_forward_other.1 = (bf16[1024,384]{1,0:T(8,128)(2,1)S(1)}, bf16[384,1536]{1,0:T(8,128)(2,1)S(1)}, bf16[384,1536]{1,0:T(8,128)(2,1)S(1)}, f32[3,768]{1,0:T(4...) custom-call(s32[6]{0:T(128)S(1)} %stack.39.bits_ref, ...), custom_call_target="tpu_custom_call" | custom-call | flops 8455716864 | bytes 26526748 | tf_op jit(solution)/shard_map/feed_forward_other/pallas_call | solution.py:81
  91.8 1.0 copy-done.6
  93.1 3.6 %second_stage.1 = (bf16[192,1536]{1,0:T(8,128)(2,1)}, bf16[192,1536]{1,0:T(8,128)(2,1)}, bf16[192,1536]{1,0:T(8,128)(2,1)S(1)}, bf16[192,1536]{1,0:T(8,128)(2,1)S(1)}) custom-call(s32[6]{0:T(128)S(1)} %stack.39.bits_ref, bf16[384,1536]{1,0:T(8,128)(2,1)S(1)} %get-tuple-element.153.fc_kept, bf16[384,1536]{1,0:T(8,128)(2,1)S(1)} %get-tuple-element.154.out_kept, ...), custom_call_target="tpu_custom_call" | custom-call | flops 2359296 | bytes 3538968 | tf_op jit(solution)/shard_map/second_stage/pallas_call | solution.py:81
  96.8 0.7 collective-permute-start.14
  97.5 1.6 collective-permute-start.15
  99.1 18.1 %attention_backward_own.1 = (f32[8,768]{1,0:T(8,128)S(1)}, f32[16,768]{1,0:T(8,128)S(1)}, bf16[384,1536]{1,0:T(8,128)(2,1)S(1)}, bf16[384,1536]{1,0:T(8,128)(2,1)S(1)}, bf16[1024,1152]{1,0:T(8,128)(2,1)}) custom-call(s32[6]{0:T(128)S(1)} %stack.39.bits_ref, s32[1]{0:T(128)S(6)} %copy.45.length_ref, f32[6,1024]{1,0:T(8,128)} %get-tuple-element.113.lse_ref, ...), custom_call_target="tpu_custom_call" | custom-call | flops 6039797760 | bytes 11298844 | tf_op jit(solution)/shard_map/attention_backward_own/pallas_call | solution.py:81
  117.3 1.2 collective-permute-start.17
  118.7 1.5 collective-permute-start.20
  120.1 1.1 collective-permute-done.17
  123.0 1.1 collective-permute-start.22
  124.1 1.4 collective-permute-start.21
  125.6 14.4 %attention_backward_other.1 = (bf16[1024,2304]{1,0:T(8,128)(2,1)S(1)}, bf16[768,2304]{1,0:T(8,128)(2,1)S(1)}, bf16[3072,768]{1,0:T(8,128)(2,1)S(1)}, bf16[1024,3072]{1,0:T(8,128)(2,1)S(1)}) custom-call(s32[6]{0:T(128)S(1)} %stack.39.bits_ref, s32[1]{0:T(128)S(6)} %copy.45.length_ref, f32[6,1024]{1,0:T(8,128)} %get-tuple-element.170.lse_ref, ...), custom_call_target="tpu_custom_call" | custom-call | flops 3623878656 | bytes 21651484 | tf_op jit(solution)/shard_map/attention_backward_other/pallas_call | solution.py:81
  141.1 1.0 collective-permute-start.23
  142.1 2.6 %collective-permute-start.26 = (bf16[96,1536]{1,0:T(8,128)(2,1)S(1)}, bf16[96,1536]{1,0:T(8,128)(2,1)S(1)}, u32[]{:S(2)}, u32[]{:S(2)}) collective-permute-start(bf16[96,1536]{1,0:T(8,128)(2,1)S(1)} %pad_maximum_fusion.1), channel_id=1, source_target_pairs={{0,16},{2,18},{4,20},{6,22},{8,24},{10,26},{12,28},{14,30},{16,0},... | collective-permute-start | bytes 884744 | tf_op jit(solution)/shard_map/ppermute | solution.py:1324
  144.7 8.6 %final.1 = f32[1024,768]{1,0:T(8,128)} custom-call(f32[16,768]{1,0:T(8,128)} %get-tuple-element.110.vec_ref, bf16[1024,2304]{1,0:T(8,128)(2,1)S(1)} %get-tuple-element.192.d_ref, bf16[768,2304]{1,0:T(8,128)(2,1)S(1)} %get-tuple-element.193.w_ref, bf16[1024,768]{1,0:T(8,128)(2,1)} %x_hbm.5, f32[1024,768]{1,0:T(8,128)} %get-tuple-element.194.gmid_hbm), custom_call_target="tpu_custom_call" | custom-call | flops 3623878656 | bytes 7913472 | tf_op jit(solution)/shard_map/final/pallas_call | solution.py:81
  153.8 7.6 %output.1 = bf16[1024,768]{1,0:T(8,128)(2,1)} custom-call(f32[16,768]{1,0:T(8,128)} %get-tuple-element.110.vec_ref, bf16[1024,3072]{1,0:T(8,128)(2,1)S(1)} %get-tuple-element.201.act_ref, bf16[3072,768]{1,0:T(8,128)(2,1)S(1)} %get-tuple-element.202.ow_ref, f32[1024,768]{1,0:T(8,128)} %get-tuple-element.133.middle_hbm.middle_ref), custom_call_target="tpu_custom_call" | custom-call | flops 4831838208 | bytes 4767744 | tf_op jit(solution)/shard_map/output/pallas_call | solution.py:81
  161.4 1.1 collective-permute-done.26
  162.5 0.9 fusion
  163.4 1.3 collective-permute-done.25
  167.3 0.7 pad_maximum_fusion.2
  (107 shorter events, 11.0 us)
Async XLA Ops:
  1.7 13.2 %collective-permute-start = (bf16[3,192,384]{2,1,0:T(8,128)(2,1)S(1)}, bf16[3,192,384]{2,1,0:T(8,128)(2,1)S(1)}, u32[]{:S(2)}, u32[]{:S(2)}) collective-permute-start(bf16[3,192,384]{2,1,0:T(8,128)(2,1)S(1)} %dynamic-slice_bitcast_fusion), channel_id=1, source_target_pairs={{0,1},{1,0},{2,3},{3,2},{4,5},{5,4},{6,7},{7,6},{8,9},{9,8},{10,11... | collective-permute-start | bytes 1327112 | tf_op jit(solution)/shard_map/ppermute | solution.py:1319
  14.9 12.9 %collective-permute-start.2 = (bf16[3,192,384]{2,1,0:T(8,128)(2,1)S(1)}, bf16[3,192,384]{2,1,0:T(8,128)(2,1)S(1)}, u32[]{:S(2)}, u32[]{:S(2)}) collective-permute-start(bf16[3,192,384]{2,1,0:T(8,128)(2,1)S(1)} %collective-permute-done.rest_0_), channel_id=1, source_target_pairs={{0,2},{2,0},{4,6},{6,4},{8,10},{10,8},{12,14},{14,12},{16,18},{18,... | collective-permute-start | bytes 1327112 | tf_op jit(solution)/shard_map/ppermute | solution.py:1324
  14.9 12.9 %collective-permute-start.1 = (bf16[3,192,384]{2,1,0:T(8,128)(2,1)S(1)}, bf16[3,192,384]{2,1,0:T(8,128)(2,1)S(1)}, u32[]{:S(2)}, u32[]{:S(2)}) collective-permute-start(bf16[3,192,384]{2,1,0:T(8,128)(2,1)S(1)} %collective-permute-done.rest_0_), channel_id=1, source_target_pairs={{0,4},{2,6},{4,0},{6,2},{8,12},{10,14},{12,8},{14,10},{16,20},{18,... | collective-permute-start | bytes 1327112 | tf_op jit(solution)/shard_map/ppermute | solution.py:1324
  16.7 11.1 %collective-permute-start.3 = (bf16[224,768]{1,0:T(8,128)(2,1)}, bf16[224,768]{1,0:T(8,128)(2,1)S(1)}, u32[]{:S(2)}, u32[]{:S(2)}) collective-permute-start(bf16[224,768]{1,0:T(8,128)(2,1)} %get-tuple-element.116), channel_id=1, source_target_pairs={{0,1},{1,0},{2,3},{3,2},{4,5},{5,4},{6,7},{7,6},{8,9},{9,8},{10,11... | collective-permute-start | bytes 1032200 | tf_op jit(solution)/shard_map/ppermute | solution.py:1319
  18.2 29.4 %collective-permute-start.6 = (bf16[192,1536]{1,0:T(8,128)(2,1)}, bf16[192,1536]{1,0:T(8,128)(2,1)S(1)}, u32[]{:S(2)}, u32[]{:S(2)}) collective-permute-start(bf16[192,1536]{1,0:T(8,128)(2,1)} %get-tuple-element.125), channel_id=1, source_target_pairs={{0,1},{1,0},{2,3},{3,2},{4,5},{5,4},{6,7},{7,6},{8,9},{9,8},{10,11... | collective-permute-start | bytes 1769480 | tf_op jit(solution)/shard_map/ppermute | solution.py:1319
  27.8 19.7 %copy-start.4 = (bf16[224,768]{1,0:T(8,128)(2,1)}, bf16[224,768]{1,0:T(8,128)(2,1)S(1)}, u32[]{:S(2)}) copy-start(bf16[224,768]{1,0:T(8,128)(2,1)S(1)} %collective-permute-done.3.rest_4_.rest_6_) | copy-start | bytes 1032196
  27.8 19.7 %copy-start.1 = (bf16[3,192,384]{2,1,0:T(8,128)(2,1)}, bf16[3,192,384]{2,1,0:T(8,128)(2,1)S(1)}, u32[]{:S(2)}) copy-start(bf16[3,192,384]{2,1,0:T(8,128)(2,1)S(1)} %collective-permute-done.2.rest_1_) | copy-start | bytes 1327108
  27.8 19.7 %copy-start.2 = (bf16[3,192,384]{2,1,0:T(8,128)(2,1)}, bf16[3,192,384]{2,1,0:T(8,128)(2,1)S(1)}, u32[]{:S(2)}) copy-start(bf16[3,192,384]{2,1,0:T(8,128)(2,1)S(1)} %collective-permute-done.1.rest_2_) | copy-start | bytes 1327108
  27.8 2.7 %collective-permute-start.5 = (bf16[224,768]{1,0:T(8,128)(2,1)S(1)}, bf16[224,768]{1,0:T(8,128)(2,1)S(1)}, u32[]{:S(2)}, u32[]{:S(2)}) collective-permute-start(bf16[224,768]{1,0:T(8,128)(2,1)S(1)} %collective-permute-done.3.rest_4_.rest_6_), channel_id=1, source_target_pairs={{0,2},{2,0},{4,6},{6,4},{8,10},{10,8},{12,14},{14,12},{16,18},{18,... | collective-permute-start | bytes 1032200 | tf_op jit(solution)/shard_map/ppermute | solution.py:1324
  27.9 2.6 %collective-permute-start.4 = (bf16[3,192,384]{2,1,0:T(8,128)(2,1)S(1)}, bf16[3,192,384]{2,1,0:T(8,128)(2,1)S(1)}, u32[]{:S(2)}, u32[]{:S(2)}) collective-permute-start(bf16[3,192,384]{2,1,0:T(8,128)(2,1)S(1)} %collective-permute-done.1.rest_2_), channel_id=1, source_target_pairs={{0,2},{2,0},{4,6},{6,4},{8,10},{10,8},{12,14},{14,12},{16,18},{18,... | collective-permute-start | bytes 1327112 | tf_op jit(solution)/shard_map/ppermute | solution.py:1324
  29.0 37.9 %collective-permute-start.9 = (bf16[768,768]{1,0:T(8,128)(2,1)S(1)}, bf16[768,768]{1,0:T(8,128)(2,1)S(1)}, u32[]{:S(2)}, u32[]{:S(2)}) collective-permute-start(bf16[768,768]{1,0:T(8,128)(2,1)S(1)} %copy-done.12), channel_id=1, source_target_pairs={{0,1},{1,0},{2,3},{3,2},{4,5},{5,4},{6,7},{7,6},{8,9},{9,8},{10,11... | collective-permute-start | bytes 3538952 | tf_op jit(solution)/shard_map/ppermute | solution.py:1319
  30.5 17.0 %copy-start.3 = (bf16[3,192,384]{2,1,0:T(8,128)(2,1)}, bf16[3,192,384]{2,1,0:T(8,128)(2,1)S(1)}, u32[]{:S(2)}) copy-start(bf16[3,192,384]{2,1,0:T(8,128)(2,1)S(1)} %collective-permute-done.4.rest_3_) | copy-start | bytes 1327108
  47.5 19.3 %copy-start.13 = (bf16[192,1536]{1,0:T(8,128)(2,1)}, bf16[192,1536]{1,0:T(8,128)(2,1)S(1)}, u32[]{:S(2)}) copy-start(bf16[192,1536]{1,0:T(8,128)(2,1)S(1)} %collective-permute-done.6.rest_0_) | copy-start | bytes 1769476
  47.5 19.3 %collective-permute-start.8 = (bf16[192,1536]{1,0:T(8,128)(2,1)S(1)}, bf16[192,1536]{1,0:T(8,128)(2,1)S(1)}, u32[]{:S(2)}, u32[]{:S(2)}) collective-permute-start(bf16[192,1536]{1,0:T(8,128)(2,1)S(1)} %collective-permute-done.6.rest_0_), channel_id=1, source_target_pairs={{0,2},{2,0},{4,6},{6,4},{8,10},{10,8},{12,14},{14,12},{16,18},{18,... | collective-permute-start | bytes 1769480 | tf_op jit(solution)/shard_map/ppermute | solution.py:1324
  47.6 19.3 %collective-permute-start.7 = (bf16[192,1536]{1,0:T(8,128)(2,1)S(1)}, bf16[192,1536]{1,0:T(8,128)(2,1)S(1)}, u32[]{:S(2)}, u32[]{:S(2)}) collective-permute-start(bf16[192,1536]{1,0:T(8,128)(2,1)S(1)} %collective-permute-done.6.rest_0_), channel_id=1, source_target_pairs={{0,4},{2,6},{4,0},{6,2},{8,12},{10,14},{12,8},{14,10},{16,20},{18,... | collective-permute-start | bytes 1769480 | tf_op jit(solution)/shard_map/ppermute | solution.py:1324
  66.9 3.8 %collective-permute-start.11 = (bf16[768,768]{1,0:T(8,128)(2,1)S(1)}, bf16[768,768]{1,0:T(8,128)(2,1)S(1)}, u32[]{:S(2)}, u32[]{:S(2)}) collective-permute-start(bf16[768,768]{1,0:T(8,128)(2,1)S(1)} %collective-permute-done.9.rest_4_), channel_id=1, source_target_pairs={{0,2},{2,0},{4,6},{6,4},{8,10},{10,8},{12,14},{14,12},{16,18},{18,... | collective-permute-start | bytes 3538952 | tf_op jit(solution)/shard_map/ppermute | solution.py:1324
  67.2 3.5 %collective-permute-start.10 = (bf16[192,1536]{1,0:T(8,128)(2,1)S(1)}, bf16[192,1536]{1,0:T(8,128)(2,1)S(1)}, u32[]{:S(2)}, u32[]{:S(2)}) collective-permute-start(bf16[192,1536]{1,0:T(8,128)(2,1)S(1)} %collective-permute-done.7.rest_2_), channel_id=1, source_target_pairs={{0,2},{2,0},{4,6},{6,4},{8,10},{10,8},{12,14},{14,12},{16,18},{18,... | collective-permute-start | bytes 1769480 | tf_op jit(solution)/shard_map/ppermute | solution.py:1324
  70.7 21.0 %collective-permute-start.12 = (bf16[384,1536]{1,0:T(8,128)(2,1)S(1)}, bf16[384,1536]{1,0:T(8,128)(2,1)S(1)}, u32[]{:S(2)}, u32[]{:S(2)}) collective-permute-start(bf16[384,1536]{1,0:T(8,128)(2,1)S(1)} %get-tuple-element.150), channel_id=1, source_target_pairs={{0,2},{2,0},{4,6},{6,4},{8,10},{10,8},{12,14},{14,12},{16,18},{18,... | collective-permute-start | bytes 3538952 | tf_op jit(solution)/shard_map/ppermute | solution.py:1324
  70.9 20.8 %collective-permute-start.13 = (bf16[384,1536]{1,0:T(8,128)(2,1)S(1)}, bf16[384,1536]{1,0:T(8,128)(2,1)S(1)}, u32[]{:S(2)}, u32[]{:S(2)}) collective-permute-start(bf16[384,1536]{1,0:T(8,128)(2,1)S(1)} %get-tuple-element.151), channel_id=1, source_target_pairs={{0,2},{2,0},{4,6},{6,4},{8,10},{10,8},{12,14},{14,12},{16,18},{18,... | collective-permute-start | bytes 3538952 | tf_op jit(solution)/shard_map/ppermute | solution.py:1324
  96.8 20.4 %collective-permute-start.14 = (bf16[192,1536]{1,0:T(8,128)(2,1)S(1)}, bf16[192,1536]{1,0:T(8,128)(2,1)S(1)}, u32[]{:S(2)}, u32[]{:S(2)}) collective-permute-start(bf16[192,1536]{1,0:T(8,128)(2,1)S(1)} %get-tuple-element.167), channel_id=1, source_target_pairs={{0,4},{2,6},{4,0},{6,2},{8,12},{10,14},{12,8},{14,10},{16,20},{18,... | collective-permute-start | bytes 1769480 | tf_op jit(solution)/shard_map/ppermute | solution.py:1324
  97.5 19.7 %collective-permute-start.15 = (bf16[192,1536]{1,0:T(8,128)(2,1)S(1)}, bf16[192,1536]{1,0:T(8,128)(2,1)S(1)}, u32[]{:S(2)}, u32[]{:S(2)}) collective-permute-start(bf16[192,1536]{1,0:T(8,128)(2,1)S(1)} %get-tuple-element.168), channel_id=1, source_target_pairs={{0,8},{2,10},{4,12},{6,14},{8,0},{10,2},{12,4},{14,6},{16,24},{18,... | collective-permute-start | bytes 1769480 | tf_op jit(solution)/shard_map/ppermute | solution.py:1324
  117.2 5.4 %collective-permute-start.16 = (bf16[384,1536]{1,0:T(8,128)(2,1)S(1)}, bf16[384,1536]{1,0:T(8,128)(2,1)S(1)}, u32[]{:S(2)}, u32[]{:S(2)}) collective-permute-start(bf16[384,1536]{1,0:T(8,128)(2,1)S(1)} %get-tuple-element.169), channel_id=1, source_target_pairs={{0,2},{2,0},{4,6},{6,4},{8,10},{10,8},{12,14},{14,12},{16,18},{18,... | collective-permute-start | bytes 3538952 | tf_op jit(solution)/shard_map/ppermute | solution.py:1324
  117.3 3.9 %collective-permute-start.17 = (f32[8,768]{1,0:T(8,128)S(1)}, f32[8,768]{1,0:T(8,128)S(1)}, u32[]{:S(2)}, u32[]{:S(2)}) collective-permute-start(f32[8,768]{1,0:T(8,128)S(1)} %get-tuple-element.171), channel_id=1, source_target_pairs={{0,1},{1,0},{2,3},{3,2},{4,5},{5,4},{6,7},{7,6},{8,9},{9,8},{10,11... | collective-permute-start | bytes 73736 | tf_op jit(solution)/shard_map/ppermute | solution.py:1319
  118.7 21.3 %collective-permute-start.20 = (bf16[96,1536]{1,0:T(8,128)(2,1)S(1)}, bf16[96,1536]{1,0:T(8,128)(2,1)S(1)}, u32[]{:S(2)}, u32[]{:S(2)}) collective-permute-start(bf16[96,1536]{1,0:T(8,128)(2,1)S(1)} %bitcast.134), channel_id=1, source_target_pairs={{0,4},{2,6},{4,0},{6,2},{8,12},{10,14},{12,8},{14,10},{16,20},{18,... | collective-permute-start | bytes 884744 | tf_op jit(solution)/shard_map/ppermute | solution.py:1324
  121.3 1.3 collective-permute-start.18
  121.5 18.5 %collective-permute-start.19 = (bf16[96,1536]{1,0:T(8,128)(2,1)S(1)}, bf16[96,1536]{1,0:T(8,128)(2,1)S(1)}, u32[]{:S(2)}, u32[]{:S(2)}) collective-permute-start(bf16[96,1536]{1,0:T(8,128)(2,1)S(1)} %bitcast.135), channel_id=1, source_target_pairs={{0,8},{2,10},{4,12},{6,14},{8,0},{10,2},{12,4},{14,6},{16,24},{18,... | collective-permute-start | bytes 884744 | tf_op jit(solution)/shard_map/ppermute | solution.py:1324
  123.0 17.1 %collective-permute-start.22 = (bf16[192,768]{1,0:T(8,128)(2,1)S(1)}, bf16[192,768]{1,0:T(8,128)(2,1)S(1)}, u32[]{:S(2)}, u32[]{:S(2)}) collective-permute-start(bf16[192,768]{1,0:T(8,128)(2,1)S(1)} %bitcast.129), channel_id=1, source_target_pairs={{0,8},{2,10},{4,12},{6,14},{8,0},{10,2},{12,4},{14,6},{16,24},{18,... | collective-permute-start | bytes 884744 | tf_op jit(solution)/shard_map/ppermute | solution.py:1324
  124.1 15.9 %collective-permute-start.21 = (bf16[208,768]{1,0:T(8,128)(2,1)S(1)}, bf16[208,768]{1,0:T(8,128)(2,1)S(1)}, u32[]{:S(2)}, u32[]{:S(2)}) collective-permute-start(bf16[208,768]{1,0:T(8,128)(2,1)S(1)} %pad_maximum_fusion), channel_id=1, source_target_pairs={{0,4},{2,6},{4,0},{6,2},{8,12},{10,14},{12,8},{14,10},{16,20},{18,... | collective-permute-start | bytes 958472 | tf_op jit(solution)/shard_map/ppermute | solution.py:1324
  140.4 12.9 %collective-permute-start.24 = (bf16[96,768]{1,0:T(8,128)(2,1)S(1)}, bf16[96,768]{1,0:T(8,128)(2,1)S(1)}, u32[]{:S(2)}, u32[]{:S(2)}) collective-permute-start(bf16[96,768]{1,0:T(8,128)(2,1)S(1)} %bitcast.139), channel_id=1, source_target_pairs={{0,4},{2,6},{4,0},{6,2},{8,12},{10,14},{12,8},{14,10},{16,20},{18,... | collective-permute-start | bytes 442376 | tf_op jit(solution)/shard_map/ppermute | solution.py:1324
  141.1 12.2 %collective-permute-start.23 = (bf16[112,768]{1,0:T(8,128)(2,1)S(1)}, bf16[112,768]{1,0:T(8,128)(2,1)S(1)}, u32[]{:S(2)}, u32[]{:S(2)}) collective-permute-start(bf16[112,768]{1,0:T(8,128)(2,1)S(1)} %pad_maximum_fusion.3), channel_id=1, source_target_pairs={{0,8},{2,10},{4,12},{6,14},{8,0},{10,2},{12,4},{14,6},{16,24},{18,... | collective-permute-start | bytes 516104 | tf_op jit(solution)/shard_map/ppermute | solution.py:1324
  142.1 20.4 %collective-permute-start.26 = (bf16[96,1536]{1,0:T(8,128)(2,1)S(1)}, bf16[96,1536]{1,0:T(8,128)(2,1)S(1)}, u32[]{:S(2)}, u32[]{:S(2)}) collective-permute-start(bf16[96,1536]{1,0:T(8,128)(2,1)S(1)} %pad_maximum_fusion.1), channel_id=1, source_target_pairs={{0,16},{2,18},{4,20},{6,22},{8,24},{10,26},{12,28},{14,30},{16,0},... | collective-permute-start | bytes 884744 | tf_op jit(solution)/shard_map/ppermute | solution.py:1324
  153.4 11.2 %collective-permute-start.25 = (bf16[112,768]{1,0:T(8,128)(2,1)S(1)}, bf16[112,768]{1,0:T(8,128)(2,1)S(1)}, u32[]{:S(2)}, u32[]{:S(2)}) collective-permute-start(bf16[112,768]{1,0:T(8,128)(2,1)S(1)} %pad_maximum_fusion.4), channel_id=1, source_target_pairs={{0,16},{2,18},{4,20},{6,22},{8,24},{10,26},{12,28},{14,30},{16,0},... | collective-permute-start | bytes 516104 | tf_op jit(solution)/shard_map/ppermute | solution.py:1324
  (12 other events, 66.5 us)
